TPU v7x, 128 devices: a whole 4x4x4 slice. The times are simulated.
128 devices in a mesh: rows: 16 (over z, x_hi, core), cols: 8 (over y, x_lo).
Axes of the slice: x: 4 (x_hi: 2, x_lo: 2; x = x_hi * 2 + x_lo), y: 4, z: 4, core: 2. Of those that a mesh axis runs over, the one named last changes fastest.
Arguments:
- wave_coarse: float32 [192, 192, 192], P('rows', 'cols'), may hold values from -6 to 6
- potential_coarse: float32 [192, 192, 192], P('rows', 'cols'), may hold values from 0 to 5
- potential_fine: float32 [384, 384, 384], P('cols', 'rows'), may hold values from 0 to 5
Outputs:
- fine_wave: float32 [384, 384, 384], P('cols', 'rows')
All inputs are finite; a program needn't handle non-finite values.
Results may differ from a plain program's by a relative error of at most 0.0003.
Values sent between devices are 32-bit elements; how exact they have to be, the bound alone decides.
No kernel may reach another device: no remote copies, remote signals or barrier semaphores. Data moves between devices by JAX's collectives and lax.ppermute only.
A program may use at most 128 MiB of HBM per device.

v0:
```python
from functools import partial
import math

import jax
import jax.numpy as jnp
from jax import lax
from jax.sharding import Mesh
from jax.sharding import PartitionSpec as P

NC = 192
NF = 384
COLS = ("cols_0", "cols_1")
ROWS = ("rows_0", "rows_1", "rows_2")
ROWS_COLS = ("rows_0", "rows_1", "rows_2", "cols_0", "cols_1")


TIME_STEP = 0.5
CONTACT = 0.4
DIPOLE_STRENGTH = 0.3
EPSILON = 1e-06
HIGHEST = lax.Precision.HIGHEST


def over_axes(value, axes):
    for axis in axes:
        value = lax.psum(value, axis)
    return value


def cas_values(product, length):
    phases = 2.0 * math.pi / length * (product % length).astype(jnp.float32)
    return jnp.cos(phases) + jnp.sin(phases)


def cas_matrix(length):
    positions = jnp.arange(length, dtype=jnp.int32)
    return cas_values(positions[:, None] * positions[None, :], length)


def lifted_positions(length):
    positions = jnp.arange(length, dtype=jnp.int32)
    return jnp.where(positions < length // 2, positions, positions + length)


def lift_matrix(length):
    lifted = lifted_positions(length)
    fine_points = jnp.arange(2 * length, dtype=jnp.int32)
    return cas_values(lifted[:, None] * fine_points[None, :], 2 * length)


def wavenumbers(length, block_count, offset, spacing):
    positions = offset + jnp.arange(block_count, dtype=jnp.int32)
    signed = jnp.where(positions < length // 2, positions, positions - length)
    return 2.0 * math.pi / (length * spacing) * signed.astype(jnp.float32)


def multipliers(along_x, along_y, along_z, length):
    squares = along_x + along_y + along_z
    volume = float(length) ** 3
    kinetic = jnp.exp(-0.5 * TIME_STEP * squares) / volume
    nonzero = jnp.where(squares > 0, squares, 1.0)
    dipolar = (
        jnp.where(squares > 0, DIPOLE_STRENGTH * (3.0 * along_z - squares) / nonzero, 0.0) / volume
    )
    return (kinetic, dipolar)


def sweep_out(values, matrix):
    turned = jnp.dot(values, matrix, precision=HIGHEST)
    turned = lax.all_to_all(turned, COLS, split_axis=2, concat_axis=1, tiled=True)
    turned = jnp.einsum("ayc,yk->ack", turned, matrix, precision=HIGHEST)
    turned = lax.all_to_all(turned, ROWS, split_axis=2, concat_axis=0, tiled=True)
    return jnp.einsum("xbc,xk->bck", turned, matrix, precision=HIGHEST)


def sweep_back(values, matrix):
    turned = jnp.dot(values, matrix, precision=HIGHEST)
    turned = lax.all_to_all(turned, ROWS, split_axis=2, concat_axis=1, tiled=True)
    turned = jnp.einsum("cyb,yk->cbk", turned, matrix, precision=HIGHEST)
    turned = lax.all_to_all(turned, COLS, split_axis=2, concat_axis=0, tiled=True)
    return jnp.einsum("zab,zk->abk", turned, matrix, precision=HIGHEST)


def sweep_lift(values, matrix):
    turned = jnp.einsum("zba,zk->bak", values, matrix, precision=HIGHEST)
    turned = lax.all_to_all(turned, COLS, split_axis=2, concat_axis=0, tiled=True)
    turned = jnp.einsum("yac,yk->ack", turned, matrix, precision=HIGHEST)
    turned = lax.all_to_all(turned, ROWS, split_axis=2, concat_axis=0, tiled=True)
    return jnp.einsum("xbc,xk->bck", turned, matrix, precision=HIGHEST)


def advance(evolved, potential, dipolar, volume, forward, inverse):
    density = evolved * evolved
    field_dd = inverse(dipolar * forward(density))
    damped = jnp.exp(-TIME_STEP * (potential + CONTACT * density + field_dd)) * evolved
    squares = over_axes(jnp.sum(damped * damped), ROWS_COLS)
    return damped * lax.rsqrt(squares / volume + EPSILON)


def per_device(wave_coarse, potential_coarse, potential_fine):
    row_index = lax.axis_index(ROWS)
    col_index = lax.axis_index(COLS)
    row_count = lax.axis_size(ROWS)
    col_count = lax.axis_size(COLS)
    coarse_matrix = cas_matrix(NC)
    fine_matrix = cas_matrix(NF)
    z_block = NC // col_count
    y_block = NC // row_count
    along_z = wavenumbers(NC, z_block, col_index * z_block, 2.0)[:, None, None] ** 2
    along_y = wavenumbers(NC, y_block, row_index * y_block, 2.0)[None, :, None] ** 2
    along_x = wavenumbers(NC, NC, 0, 2.0)[None, None, :] ** 2
    kinetic, dipolar = multipliers(along_x, along_y, along_z, NC)
    coarse_forward = partial(sweep_out, matrix=coarse_matrix)
    coarse_inverse = partial(sweep_back, matrix=coarse_matrix)
    amplitude = wave_coarse
    evolved = coarse_inverse(kinetic * coarse_forward(amplitude))
    amplitude = advance(
        evolved, potential_coarse, dipolar, float(NC) ** 3, coarse_forward, coarse_inverse
    )
    first_evolved = None
    spectrum = sweep_out(amplitude, coarse_matrix)
    placed = lax.all_to_all(
        lax.all_to_all(spectrum, ROWS, split_axis=2, concat_axis=1, tiled=True),
        COLS,
        split_axis=1,
        concat_axis=0,
        tiled=True,
    )
    y_part = NC // col_count
    x_part = NC // row_count
    lift_z = wavenumbers(NC, NC, 0, 2.0)[:, None, None] ** 2
    lift_y = wavenumbers(NC, y_part, col_index * y_part, 2.0)[None, :, None] ** 2
    lift_x = wavenumbers(NC, x_part, row_index * x_part, 2.0)[None, None, :] ** 2
    compact = jnp.exp(-0.5 * TIME_STEP * (lift_x + lift_y + lift_z)) / float(NC) ** 3
    first_evolved = sweep_lift(compact * placed, lift_matrix(NC))
    x_block = NF // row_count
    y_block = NF // col_count
    along_x = wavenumbers(NF, x_block, row_index * x_block, 1.0)[:, None, None] ** 2
    along_y = wavenumbers(NF, y_block, col_index * y_block, 1.0)[None, :, None] ** 2
    along_z = wavenumbers(NF, NF, 0, 1.0)[None, None, :] ** 2
    forward = partial(sweep_back, matrix=fine_matrix)
    inverse = partial(sweep_out, matrix=fine_matrix)
    kinetic, dipolar = multipliers(along_x, along_y, along_z, NF)
    amplitude = advance(first_evolved, potential_fine, dipolar, float(NF) ** 3, forward, inverse)
    return amplitude


def solution(mesh):
    torus = Mesh(
        mesh.devices.reshape(4, 2, 2, 4, 2), ("rows_0", "rows_1", "rows_2", "cols_0", "cols_1")
    )
    return jax.shard_map(
        per_device,
        mesh=torus,
        in_specs=(P(ROWS, COLS, None), P(ROWS, COLS, None), P(COLS, ROWS, None)),
        out_specs=P(COLS, ROWS, None),
        check_vma=False,
    )
```

profile of v0, /device:TPU:1, one launch (start us, length us, event | category | flops | bytes accessed | tf_op | source)
XLA Modules:
  0.0 691.9 jit_solution(2612188793912324381)
XLA Ops:
  23.8 9.8 %all-to-all-start.1 = ((f32[16,1,3456]{2,1,0:T(1,128)}), f32[16,1,3456]{2,1,0:T(1,128)S(1)}, u32[]{:S(2)}, u32[]{:S(2)}) async-start(f32[16,1,3456]{2,1,0:T(1,128)} %reshape.221), calls=%async_computation.1 | async-start | bytes 442368 | tf_op jit(solution)/shard_map/all_to_all | solution.py:72
  33.7 8.2 %all-to-all-done.1 = f32[16,1,3456]{2,1,0:T(1,128)S(1)} async-done(((f32[16,1,3456]{2,1,0:T(1,128)}), f32[16,1,3456]{2,1,0:T(1,128)S(1)}, u32[]{:S(2)}, u32[]{:S(2)}) %all-to-all-start.1) | async-done | bytes 221216 | tf_op jit(solution)/shard_map/all_to_all | solution.py:72
  52.9 11.7 %all_to_all.324 = f32[16,1,3456]{2,1,0:T(1,128)S(1)} all-to-all(f32[16,1,3456]{2,1,0:T(1,128)S(1)} %reshape.223), channel_id=1, replica_groups=mesh['rows_0'=4,'rows_1'=2,'rows_2'=2,'cols_0'=4,'cols_1'=2] {'rows_0','..., dimensions={0} | all-to-all | bytes 442368 | tf_op jit(solution)/shard_map/all_to_all | solution.py:78
  74.3 8.8 %all_to_all.325 = f32[8,1,6912]{2,1,0:T(1,128)S(1)} all-to-all(f32[8,1,6912]{2,1,0:T(1,128)S(1)} %reshape.225), channel_id=1, replica_groups=mesh['rows_0'=4,'rows_1'=2,'rows_2'=2,'cols_0'=4,'cols_1'=2] {'cols_0','..., dimensions={0} | all-to-all | bytes 442368 | tf_op jit(solution)/shard_map/all_to_all | solution.py:80
  90.4 8.3 %all_to_all.326 = f32[8,1,6912]{2,1,0:T(1,128)S(1)} all-to-all(f32[8,1,6912]{2,1,0:T(1,128)S(1)} %reshape.227), channel_id=1, replica_groups=mesh['rows_0'=4,'rows_1'=2,'rows_2'=2,'cols_0'=4,'cols_1'=2] {'cols_0','..., dimensions={0} | all-to-all | bytes 442368 | tf_op jit(solution)/shard_map/all_to_all | solution.py:70
  104.6 14.3 %all_to_all.327 = f32[16,1,3456]{2,1,0:T(1,128)S(1)} all-to-all(f32[16,1,3456]{2,1,0:T(1,128)S(1)} %reshape.229), channel_id=1, replica_groups=mesh['rows_0'=4,'rows_1'=2,'rows_2'=2,'cols_0'=4,'cols_1'=2] {'rows_0','..., dimensions={0} | all-to-all | bytes 442368 | tf_op jit(solution)/shard_map/all_to_all | solution.py:72
  129.9 11.9 %all_to_all.328 = f32[16,1,3456]{2,1,0:T(1,128)S(1)} all-to-all(f32[16,1,3456]{2,1,0:T(1,128)S(1)} %reshape.231), channel_id=1, replica_groups=mesh['rows_0'=4,'rows_1'=2,'rows_2'=2,'cols_0'=4,'cols_1'=2] {'rows_0','..., dimensions={0} | all-to-all | bytes 442368 | tf_op jit(solution)/shard_map/all_to_all | solution.py:78
  151.6 8.4 %all_to_all.329 = f32[8,1,6912]{2,1,0:T(1,128)S(1)} all-to-all(f32[8,1,6912]{2,1,0:T(1,128)S(1)} %reshape.233), channel_id=1, replica_groups=mesh['rows_0'=4,'rows_1'=2,'rows_2'=2,'cols_0'=4,'cols_1'=2] {'cols_0','..., dimensions={0} | all-to-all | bytes 442368 | tf_op jit(solution)/shard_map/all_to_all | solution.py:80
  165.8 8.3 %psum.70 = f32[]{:T(128)} all-reduce(f32[]{:T(128)} %get-tuple-element.5), channel_id=1, replica_groups=mesh['rows_0'=4,'rows_1'=2,'rows_2'=2,'cols_0'=4,'cols_1'=2] {'rows_0'}, use_global_device_ids=true, to_apply=%region_1.2 | all-reduce | flops 1 | bytes 8 | tf_op jit(solution)/shard_map/psum | solution.py:26
  202.4 8.3 %all_to_all.330 = f32[8,1,6912]{2,1,0:T(1,128)S(1)} all-to-all(f32[8,1,6912]{2,1,0:T(1,128)S(1)} %reshape.235), channel_id=1, replica_groups=mesh['rows_0'=4,'rows_1'=2,'rows_2'=2,'cols_0'=4,'cols_1'=2] {'cols_0','..., dimensions={0} | all-to-all | bytes 442368 | tf_op jit(solution)/shard_map/all_to_all | solution.py:70
  216.7 16.4 %all_to_all.331 = f32[16,1,3456]{2,1,0:T(1,128)S(1)} all-to-all(f32[16,1,3456]{2,1,0:T(1,128)S(1)} %reshape.237), channel_id=1, replica_groups=mesh['rows_0'=4,'rows_1'=2,'rows_2'=2,'cols_0'=4,'cols_1'=2] {'rows_0','..., dimensions={0} | all-to-all | bytes 442368 | tf_op jit(solution)/shard_map/all_to_all | solution.py:72
  247.7 8.4 %all-to-all-done.10 = f32[16,1,3456]{2,1,0:T(1,128)S(1)} async-done(((f32[16,1,3456]{2,1,0:T(1,128)}), f32[16,1,3456]{2,1,0:T(1,128)S(1)}, u32[]{:S(2)}, u32[]{:S(2)}) %all-to-all-start.10) | async-done | bytes 221216 | tf_op jit(solution)/shard_map/all_to_all | solution.py:123
  280.0 10.8 %all_to_all.332 = f32[8,1,13824]{2,1,0:T(1,128)S(1)} all-to-all(f32[8,1,13824]{2,1,0:T(1,128)} %reshape.243), channel_id=1, replica_groups=mesh['rows_0'=4,'rows_1'=2,'rows_2'=2,'cols_0'=4,'cols_1'=2] {'cols_0','..., dimensions={0} | all-to-all | bytes 884736 | tf_op jit(solution)/shard_map/all_to_all | solution.py:86
  309.4 22.2 %all_to_all.333 = f32[16,1,13824]{2,1,0:T(1,128)S(1)} all-to-all(f32[16,1,13824]{2,1,0:T(1,128)} %reshape.245), channel_id=1, replica_groups=mesh['rows_0'=4,'rows_1'=2,'rows_2'=2,'cols_0'=4,'cols_1'=2] {'rows_0','..., dimensions={0} | all-to-all | bytes 1769472 | tf_op jit(solution)/shard_map/all_to_all | solution.py:88
  364.8 30.7 %all_to_all.334 = f32[16,1,27648]{2,1,0:T(1,128)} all-to-all(f32[16,1,27648]{2,1,0:T(1,128)} %reshape.247), channel_id=1, replica_groups=mesh['rows_0'=4,'rows_1'=2,'rows_2'=2,'cols_0'=4,'cols_1'=2] {'rows_0','..., dimensions={0} | all-to-all | bytes 3538944 | tf_op jit(solution)/shard_map/all_to_all | solution.py:78
  417.9 8.5 %fusion.28 = f32[48,24,384]{2,1,0:T(8,128)} fusion(f32[48,384,24]{1,2,0:T(8,128)} %copy.157), kind=kOutput, calls=%fused_computation.48 | convolution fusion | flops 2039906304 | bytes 3538944 | tf_op jit(solution)/shard_map/cyb,yk->cbk/dot_general | solution.py:79
  431.0 8.2 %reshape.249 = f32[8,1,55296]{2,1,0:T(1,128)} reshape(f32[384,24,48]{2,1,0:T(8,128)} %bitcast.240) | data formatting | bytes 3538944
  443.8 22.6 %all-to-all-done.15 = f32[8,1,55296]{2,1,0:T(1,128)} async-done(((f32[8,1,55296]{2,1,0:T(1,128)}), f32[8,1,55296]{2,1,0:T(1,128)}, u32[]{:S(2)}, u32[]{:S(2)}) %all-to-all-start.15) | async-done | bytes 1769504 | tf_op jit(solution)/shard_map/all_to_all | solution.py:80
  499.5 7.7 %fusion.3 = f32[24,48,384]{2,1,0:T(8,128)} fusion(f32[24,48,384]{2,1,0:T(8,128)S(1)} %fusion.26, f32[384]{0:T(512)S(1)} %get-tuple-element.12, f32[384]{0:T(512)S(1)} %get-tuple-element.11, f32[24,48]{1,0:T(8,128)S(1)} %broadcast_add_fusion.1), kind=kOutput, calls=%fused_computation.8 | convolution fusion | flops 2043887616 | bytes 3546624 | tf_op jit(solution)/shard_map/dot_general | solution.py:69
  511.8 8.2 %reshape.251 = f32[8,1,55296]{2,1,0:T(1,128)} reshape(f32[384,24,48]{2,1,0:T(8,128)} %bitcast.243) | data formatting | bytes 3538944
  520.0 26.1 %all_to_all.335 = f32[8,1,55296]{2,1,0:T(1,128)} all-to-all(f32[8,1,55296]{2,1,0:T(1,128)} %reshape.251), channel_id=1, replica_groups=mesh['rows_0'=4,'rows_1'=2,'rows_2'=2,'cols_0'=4,'cols_1'=2] {'cols_0','..., dimensions={0} | all-to-all | bytes 3538944 | tf_op jit(solution)/shard_map/all_to_all | solution.py:70
  571.5 8.5 %fusion.23 = f32[24,48,384]{2,1,0:T(8,128)} fusion(f32[24,384,48]{1,2,0:T(8,128)} %all_to_all.301), kind=kOutput, calls=%fused_computation.43 | convolution fusion | flops 2039906304 | bytes 3538944 | tf_op jit(solution)/shard_map/ayc,yk->ack/dot_general | solution.py:71
  591.4 32.1 %all_to_all.336 = f32[16,1,27648]{2,1,0:T(1,128)} all-to-all(f32[16,1,27648]{2,1,0:T(1,128)} %reshape.253), channel_id=1, replica_groups=mesh['rows_0'=4,'rows_1'=2,'rows_2'=2,'cols_0'=4,'cols_1'=2] {'rows_0','..., dimensions={0} | all-to-all | bytes 3538944 | tf_op jit(solution)/shard_map/all_to_all | solution.py:72
  645.9 10.6 %multiply_reduce_fusion = (f32[]{:T(128)}, f32[48,24,384]{2,1,0:T(8,128)}) fusion(f32[48,24,384]{2,1,0:T(8,128)S(1)} %fusion.42, f32[384,48,24]{0,2,1:T(8,128)} %copy.165, f32[48,24,384]{2,1,0:T(8,128)} %param.5), kind=kOutput, calls=%fused_computation.11 | convolution fusion | flops 2043445248 | bytes 7077892 | tf_op jit(solution)/shard_map/xbc,xk->bck/dot_general | solution.py:73
  (158 shorter events, 370.4 us)
Async XLA Ops:
  0.0 1.0 copy-start
  4.7 11.9 %all-to-all-start = ((f32[8,1,6912]{2,1,0:T(1,128)}), f32[8,1,6912]{2,1,0:T(1,128)S(1)}, u32[]{:S(2)}, u32[]{:S(2)}) async-start(f32[8,1,6912]{2,1,0:T(1,128)} %reshape.219), calls=%async_computation | async-start | bytes 442368 | tf_op jit(solution)/shard_map/all_to_all | solution.py:70
  23.8 18.0 %all-to-all-start.1 = ((f32[16,1,3456]{2,1,0:T(1,128)}), f32[16,1,3456]{2,1,0:T(1,128)S(1)}, u32[]{:S(2)}, u32[]{:S(2)}) async-start(f32[16,1,3456]{2,1,0:T(1,128)} %reshape.221), calls=%async_computation.1 | async-start | bytes 442368 | tf_op jit(solution)/shard_map/all_to_all | solution.py:72
  87.3 3.0 copy-start.3
  161.9 1.1 copy-start.2
  243.5 12.6 %all-to-all-start.10 = ((f32[16,1,3456]{2,1,0:T(1,128)}), f32[16,1,3456]{2,1,0:T(1,128)S(1)}, u32[]{:S(2)}, u32[]{:S(2)}) async-start(f32[16,1,3456]{2,1,0:T(1,128)} %reshape.239), calls=%async_computation.10 | async-start | bytes 442368 | tf_op jit(solution)/shard_map/all_to_all | solution.py:123
  260.0 9.5 %all-to-all-start.11 = ((f32[8,1,6912]{2,1,0:T(1,128)}), f32[8,1,6912]{2,1,0:T(1,128)S(1)}, u32[]{:S(2)}, u32[]{:S(2)}) async-start(f32[8,1,6912]{2,1,0:T(1,128)} %reshape.241), calls=%async_computation.11 | async-start | bytes 442368 | tf_op jit(solution)/shard_map/all_to_all | solution.py:122
  439.2 27.3 %all-to-all-start.15 = ((f32[8,1,55296]{2,1,0:T(1,128)}), f32[8,1,55296]{2,1,0:T(1,128)}, u32[]{:S(2)}, u32[]{:S(2)}) async-start(f32[8,1,55296]{2,1,0:T(1,128)} %reshape.249), calls=%async_computation.15 | async-start | bytes 3538944 | tf_op jit(solution)/shard_map/all_to_all | solution.py:80
  688.6 2.9 copy-start.1
where the time goes:
time: 704 us; the launch traced here: 692 us
  blocking collectives  274 us (39%)
  local copies, waits for them, and re-layouts  202 us (29%)
  matrix products  81.1 us (12%)
  other arithmetic  53.2 us (8%)
  waiting for transfers between devices  51 us (7%)
  starting transfers between devices  28 us (4%)
    unnamed x44, local copies, waits for them, and re-layouts  91.4 us
    psum x10, blocking collectives, over_axes(): value = lax.psum(value, axis)  64.2 us
    all_to_all x3, blocking collectives, sweep_out(): lax.all_to_all(turned, ROWS, split_axis=2, concat_axis=0, tiled=True)  62.8 us
    all_to_all x3, blocking collectives, sweep_back(): lax.all_to_all(turned, ROWS, split_axis=2, concat_axis=1, tiled=True)  54.2 us
    all_to_all x3, blocking collectives, sweep_out(): lax.all_to_all(turned, COLS, split_axis=2, concat_axis=1, tiled=True)  42.8 us
    all_to_all x1, waiting for transfers between devices, sweep_back(): lax.all_to_all(turned, COLS, split_axis=2, concat_axis=0, tiled=True)  22.6 us
    all_to_all x1, blocking collectives, sweep_lift(): lax.all_to_all(turned, ROWS, split_axis=2, concat_axis=0, tiled=True)  22.2 us
    all_to_all x8, local copies, waits for them, and re-layouts, sweep_out(): lax.all_to_all(turned, ROWS, split_axis=2, concat_axis=0, tiled=True)  21.4 us
  transfers between devices with their start and end apart: 5, of which 5 were waited for; matrix products, arithmetic and copies ran while one was open for 0% of the time, Pallas kernels for 0%

commit v1 on v0

v1 whole, which is shorter than its diff:
```python
import math

import jax
import jax.numpy as jnp
import numpy as np
from jax import lax
from jax.sharding import Mesh
from jax.sharding import PartitionSpec as P

NC = 192
NF = 384
ROWS = ("rows_0", "rows_1", "rows_2")
COLS = ("cols_0", "cols_1")
ALL = ROWS + COLS
CHIPS = ("rows_0", "rows_1", "cols_0", "cols_1")
CORE = "rows_2"

TIME_STEP = 0.5
CONTACT = 0.4
DIPOLE_STRENGTH = 0.3
EPSILON = 1e-06
PREC = lax.Precision.HIGH


def cas_table(rows, columns, length):
    phases = 2.0 * math.pi / length * ((np.outer(rows, columns)) % length)
    return np.cos(phases) + np.sin(phases)


def signed(length):
    k = np.arange(length)
    return np.where(k < length // 2, k, k - length)


def tables():
    k = np.arange(NC)
    wave = 2.0 * math.pi / NF * signed(NC)
    decay = np.exp(-0.5 * TIME_STEP * wave**2)
    hc = cas_table(k, k, NC)
    hf = cas_table(np.arange(NF), np.arange(NF), NF)
    evolve = hc @ (decay[:, None] * hc) / NC
    lifted = np.where(k < NC // 2, k, k + NC)
    lift = hf[:, lifted] @ (decay[:, None] * hc) / NC
    return [t.astype(np.float32) for t in (hc, hf, evolve, lift)]


HC, HF, EVOLVE, LIFT = tables()


def squares(index, length, spacing):
    s = jnp.where(index < length // 2, index, index - length).astype(jnp.float32)
    w = 2.0 * math.pi / (length * spacing) * s
    return w * w


def dipolar(wx, wy, wz, length):
    q = wx + wy + wz
    safe = jnp.where(q > 0, q, 1.0)
    return jnp.where(q > 0, DIPOLE_STRENGTH * (3.0 * wz - q) / safe, 0.0) / float(length) ** 3


def es(spec, *args):
    return jnp.einsum(spec, *args, precision=PREC)


def exchange(buffer, axes, count):
    flat = buffer.reshape(count, 1, -1)
    return lax.all_to_all(flat, axes, split_axis=0, concat_axis=0, tiled=False)


def move_potential(potential, core):
    other = lax.ppermute(potential, CORE, [(0, 1), (1, 0)])
    low = jnp.where(core == 0, potential, other)
    high = jnp.where(core == 0, other, potential)
    both = jnp.concatenate([low, high], axis=0)
    moved = exchange(both, COLS, 8).reshape(8, 3, 24, NC)
    return moved.transpose(1, 0, 2, 3).reshape(3, NC, NC)


def per_device(wave_coarse, potential_coarse, potential_fine):
    core = lax.axis_index(CORE)
    chip = lax.axis_index(CHIPS)
    device = lax.axis_index(ALL)
    v_slab = move_potential(potential_coarse, core)

    turned = es("Zz,xyz->Zxy", EVOLVE, wave_coarse).reshape(3, 8, 8, 288)
    turned = turned.transpose(1, 2, 0, 3)[:, None]
    turned = jnp.broadcast_to(turned, (8, 2, 8, 3, 288))
    got = exchange(turned, ALL, 128).reshape(16, 8, 3, 12, 24)

    plane = got.transpose(2, 1, 4, 0, 3).reshape(3, NC, NC)
    evolved = es("Yy,kyx,xX->kYX", EVOLVE, plane, EVOLVE)
    spectrum = es("Yy,kyx->kYx", HC, evolved * evolved)
    pair = jnp.stack([spectrum, evolved], axis=2)
    pair = pair.reshape(3, 3, 64, 2, NC).transpose(2, 0, 1, 3, 4)
    got = exchange(pair, CHIPS, 64).reshape(64, 3, 3, 2, NC)

    both = got.transpose(3, 2, 4, 1, 0).reshape(2, 3, NC, NC)
    wz = squares(jnp.arange(NC), NC, 2.0)[None, None, :]
    wx = squares(jnp.arange(NC), NC, 2.0)[None, :, None]
    wy = squares(64 * jnp.arange(3) + chip, NC, 2.0)[:, None, None]
    mid = es("Xx,kxz,zZ->kXZ", HC, both[0], HC) * dipolar(wx, wy, wz, NC)
    mid = es("Xx,kxz,zZ->kXZ", HC, mid, HC)
    pair = jnp.stack([mid, both[1]], axis=2).reshape(3, 64, 3, 2, NC)
    got = exchange(pair.transpose(1, 2, 0, 3, 4), CHIPS, 64).reshape(64, 3, 3, 2, NC)

    both = got.transpose(3, 1, 2, 0, 4).reshape(2, 3, NC, NC)
    field = es("Yy,kyz->kYz", HC, both[0])
    evolved = both[1]
    damped = jnp.exp(-TIME_STEP * (v_slab + CONTACT * evolved * evolved + field)) * evolved
    part = jnp.sum(damped * damped)
    lift_y = jnp.asarray(LIFT).reshape(8, 2, 24, NC)
    lift_y = lax.dynamic_index_in_dim(lift_y, core, 1, keepdims=False).reshape(NC, NC)
    lifted = es("Zz,kyz,Yy->kZY", LIFT, damped, lift_y)
    lifted = lifted.reshape(3, 8, 48, 8, 24).transpose(3, 1, 0, 2, 4).reshape(64, 3456)
    lifted = jnp.concatenate([lifted, jnp.broadcast_to(part, (64, 128))], axis=1)
    got = exchange(lifted, CHIPS, 64).reshape(64, 3584)

    total = jnp.sum(got[:, 3456])
    scale = lax.rsqrt(total / float(NC) ** 3 + EPSILON)
    got = got[:, :3456].reshape(NC, 1152)
    evolved = es("Xx,xm->Xm", LIFT, got) * scale
    density = evolved * evolved
    spectrum = es("Xx,xm->Xm", HF, density)
    spectrum = spectrum.reshape(3, 128, 1152).transpose(1, 0, 2)
    got = exchange(spectrum, ALL, 128).reshape(16, 8, 3, 48, 24)

    plane = got.transpose(2, 1, 3, 0, 4).reshape(3, NF, NF)
    wz = squares(jnp.arange(NF), NF, 1.0)[None, :, None]
    wy = squares(jnp.arange(NF), NF, 1.0)[None, None, :]
    wx = squares(128 * jnp.arange(3) + device, NF, 1.0)[:, None, None]
    mid = es("Zz,kzy,yY->kZY", HF, plane, HF) * dipolar(wx, wy, wz, NF)
    mid = es("Zz,kzy,yY->kZY", HF, mid, HF)
    mid = mid.reshape(3, 8, 48, 16, 24).transpose(3, 1, 0, 2, 4)
    got = exchange(mid, ALL, 128).reshape(128, 3, 1152)

    spectrum = got.transpose(1, 0, 2).reshape(NF, 1152)
    field = es("Xx,xm->Xm", HF, spectrum)
    v_turned = potential_fine.reshape(1152, NF).T
    damped = jnp.exp(-TIME_STEP * (v_turned + CONTACT * density + field)) * evolved
    part = jnp.sum(damped * damped)
    parts = exchange(jnp.broadcast_to(part, (128, 128)), ALL, 128).reshape(128, 128)
    total = jnp.sum(parts[:, 0])
    return (damped.T * lax.rsqrt(total / float(NF) ** 3 + EPSILON)).reshape(48, 24, NF)


def solution(mesh):
    torus = Mesh(
        mesh.devices.reshape(4, 2, 2, 4, 2), ("rows_0", "rows_1", "rows_2", "cols_0", "cols_1")
    )
    return jax.shard_map(
        per_device,
        mesh=torus,
        in_specs=(P(ROWS, COLS, None), P(ROWS, COLS, None), P(COLS, ROWS, None)),
        out_specs=P(COLS, ROWS, None),
        check_vma=False,
    )
```

time: 704 us -> 322 us (0.46); the launches traced: 692 us -> 318 us
  blocking collectives: 274 us -> 90.4 us
  local copies, waits for them, and re-layouts: 202 us -> 93 us
  matrix products: 81.1 us -> 27.6 us
  other arithmetic: 53.2 us -> 27.9 us
    all_to_all x13 -> x4, blocking collectives: 210 us -> 90.4 us  [exchange(): return lax.all_to_all(flat, axes, split_axis=0, concat_axis=0, tiled=False)]
    unnamed x44 -> x25, local copies, waits for them, and re-layouts: 91.4 us -> 1.17 us
    all_to_all x35 -> x0, local copies, waits for them, and re-layouts: 77.8 us -> none  [the longest x8 21.4 us: sweep_out(): lax.all_to_all(turned, ROWS, split_axis=2, concat_axis=0, tiled=True)]
    psum x10 -> x0, blocking collectives: 64.2 us -> none  [over_axes(): value = lax.psum(value, axis)]
    reshape x0 -> x24, local copies, waits for them, and re-layouts: none -> 62 us  [the longest x9 24.7 us: exchange(): flat = buffer.reshape(count, 1, -1)]
    dot_general x24 -> x18, matrix products: 81.1 us -> 27.6 us  [es(): return jnp.einsum(spec, *args, precision=PREC)]
    all_to_all x18 -> x6, other arithmetic: 50.1 us -> 21 us  [exchange(): return lax.all_to_all(flat, axes, split_axis=0, concat_axis=0, tiled=False)]
    dot_general x17 -> x2, local copies, waits for them, and re-layouts: 32.6 us -> 3.63 us  [es(): return jnp.einsum(spec, *args, precision=PREC)]
  transfers between devices with their start and end apart: 5 -> 5, of which waited for: 5 -> 4; matrix products, arithmetic and copies ran while one was open for 0% -> 5% of each run, Pallas kernels for 0% -> 0%
where the time goes in v1:
time: 322 us; the launch traced here: 318 us
  local copies, waits for them, and re-layouts  93 us (29%)
  blocking collectives  90.4 us (28%)
  waiting for transfers between devices  51.5 us (16%)
  other arithmetic  27.9 us (9%)
  matrix products  27.6 us (9%)
  starting transfers between devices  25.2 us (8%)
    all_to_all x4, blocking collectives, exchange(): return lax.all_to_all(flat, axes, split_axis=0, concat_axis=0, tiled=False)  90.4 us
    all_to_all x4, waiting for transfers between devices, exchange(): return lax.all_to_all(flat, axes, split_axis=0, concat_axis=0, tiled=False)  50.4 us
    dot_general x18, matrix products, es(): return jnp.einsum(spec, *args, precision=PREC)  27.6 us
    reshape x9, local copies, waits for them, and re-layouts, exchange(): flat = buffer.reshape(count, 1, -1)  24.7 us
    all_to_all x4, starting transfers between devices, exchange(): return lax.all_to_all(flat, axes, split_axis=0, concat_axis=0, tiled=False)  24.5 us
    all_to_all x6, other arithmetic, exchange(): return lax.all_to_all(flat, axes, split_axis=0, concat_axis=0, tiled=False)  21 us
    reshape x3, local copies, waits for them, and re-layouts, per_device(): lifted.reshape(3, 8, 48, 8, 24).transpose(3, 1, 0, 2, 4).reshape(64, 3456)  8.59 us
    reshape x1, local copies, waits for them, and re-layouts, per_device(): got = exchange(spectrum, ALL, 128).reshape(16, 8, 3, 48, 24)  8.24 us
  transfers between devices with their start and end apart: 5, of which 4 were waited for; matrix products, arithmetic and copies ran while one was open for 5% of the time, Pallas kernels for 0%

profile of v1, /device:TPU:1, one launch (start us, length us, event | category | flops | bytes accessed | tf_op | source)
XLA Modules:
  0.0 317.9 jit_solution(988790697342531720)
XLA Ops:
  4.9 24.8 %all_to_all.40 = f32[128,1,864]{2,1,0:T(1,128)S(1)} all-to-all(f32[128,1,864]{2,1,0:T(1,128)S(1)} %reshape.287), channel_id=1, replica_groups=mesh['rows_0'=4,'rows_1'=2,'rows_2'=2,'cols_0'=4,'cols_1'=2] {'rows_0','..., dimensions={0} | all-to-all | bytes 884736 | tf_op jit(solution)/shard_map/all_to_all | solution.py:68
  45.2 5.1 %all-to-all-start.2 = ((f32[64,1,3456]{2,1,0:T(1,128)}), f32[64,1,3456]{2,1,0:T(1,128)S(1)}, u32[]{:S(2)}, u32[]{:S(2)}) async-start(f32[64,1,3456]{2,1,0:T(1,128)} %reshape.288), calls=%async_computation.2 | async-start | bytes 1769472 | tf_op jit(solution)/shard_map/all_to_all | solution.py:68
  53.7 12.5 %all-to-all-done.2 = f32[64,1,3456]{2,1,0:T(1,128)S(1)} async-done(((f32[64,1,3456]{2,1,0:T(1,128)}), f32[64,1,3456]{2,1,0:T(1,128)S(1)}, u32[]{:S(2)}, u32[]{:S(2)}) %all-to-all-start.2) | async-done | bytes 884768 | tf_op jit(solution)/shard_map/all_to_all | solution.py:68
  66.2 3.5 %all-to-all-start = ((f32[8,1,13824]{2,1,0:T(1,128)}), f32[8,1,13824]{2,1,0:T(1,128)S(1)}, u32[]{:S(2)}, u32[]{:S(2)}) async-start(f32[8,1,13824]{2,1,0:T(1,128)} %reshape.251), calls=%async_computation | async-start | bytes 884736 | tf_op jit(solution)/shard_map/all_to_all | solution.py:68
  81.2 7.1 %all-to-all-start.3 = ((f32[64,1,3456]{2,1,0:T(1,128)}), f32[64,1,3456]{2,1,0:T(1,128)S(1)}, u32[]{:S(2)}, u32[]{:S(2)}) async-start(f32[64,1,3456]{2,1,0:T(1,128)} %reshape.289), calls=%async_computation.3 | async-start | bytes 1769472 | tf_op jit(solution)/shard_map/all_to_all | solution.py:68
  90.6 11.8 %all-to-all-done.3 = f32[64,1,3456]{2,1,0:T(1,128)S(1)} async-done(((f32[64,1,3456]{2,1,0:T(1,128)}), f32[64,1,3456]{2,1,0:T(1,128)S(1)}, u32[]{:S(2)}, u32[]{:S(2)}) %all-to-all-start.3) | async-done | bytes 884768 | tf_op jit(solution)/shard_map/all_to_all | solution.py:68
  110.0 3.5 %copy.143 = f32[3,8,48,8,24]{4,2,0,1,3:T(8,128)} copy(f32[3,8,48,8,24]{2,1,4,3,0:T(8,128)S(1)} %reshape.262) | data formatting | bytes 1769472 | tf_op jit(solution)/shard_map/reshape | solution.py:115
  113.5 4.2 %reshape.263 = f32[64,3456]{1,0:T(8,128)S(1)} reshape(f32[8,8,3,48,24]{4,3,2,1,0:T(8,128)} %bitcast.138) | data formatting | bytes 1769472 | tf_op jit(solution)/shard_map/reshape | solution.py:115
  119.4 18.9 %all_to_all.41 = f32[64,1,3584]{2,1,0:T(1,128)S(1)} all-to-all(f32[64,1,3584]{2,1,0:T(1,128)S(1)} %copy.144), channel_id=1, replica_groups=mesh['rows_0'=4,'rows_1'=2,'rows_2'=2,'cols_0'=4,'cols_1'=2] {'rows_0','..., dimensions={0} | all-to-all | bytes 1835008 | tf_op jit(solution)/shard_map/all_to_all | solution.py:68
  146.8 4.9 %copy.146 = f32[128,1,3456]{2,1,0:T(1,128)} copy(f32[128,1,3456]{0,2,1:T(8,128)} %bitcast.140) | data formatting | bytes 3538944 | tf_op jit(solution)/shard_map/reshape | solution.py:67
  151.7 8.8 %all-to-all-start.5 = ((f32[128,1,3456]{2,1,0:T(1,128)}), f32[128,1,3456]{2,1,0:T(1,128)}, u32[]{:S(2)}, u32[]{:S(2)}) async-start(f32[128,1,3456]{2,1,0:T(1,128)} %copy.146), calls=%async_computation.5 | async-start | bytes 3538944 | tf_op jit(solution)/shard_map/all_to_all | solution.py:68
  160.7 26.1 %all-to-all-done.5 = f32[128,1,3456]{2,1,0:T(1,128)} async-done(((f32[128,1,3456]{2,1,0:T(1,128)}), f32[128,1,3456]{2,1,0:T(1,128)}, u32[]{:S(2)}, u32[]{:S(2)}) %all-to-all-start.5) | async-done | bytes 1769504 | tf_op jit(solution)/shard_map/all_to_all | solution.py:68
  186.8 6.9 %reduce.6 = f32[128,3456]{1,0:T(8,128)} reduce(f32[128,1,3456]{2,1,0:T(1,128)} %all-to-all-done.5, f32[]{:T(128)} %constant.111), dimensions={1}, to_apply=%all_to_all.29.reduce_sub_computation | reduce | bytes 3538948 | tf_op jit(solution)/shard_map/all_to_all | solution.py:68
  193.7 8.2 %reshape.269 = f32[16,8,3,48,24]{4,3,2,1,0:T(8,128)} reshape(f32[128,3456]{1,0:T(8,128)} %reduce.6) | data formatting | bytes 3538944 | tf_op jit(solution)/shard_map/reshape | solution.py:126
  201.9 8.2 %copy.147 = f32[3,8,48,16,24]{2,1,4,3,0:T(8,128)} copy(f32[3,8,48,16,24]{4,2,0,1,3:T(8,128)} %bitcast.136) | data formatting | bytes 3538944 | tf_op jit(solution)/shard_map/transpose | solution.py:128
  210.1 5.2 %reshape.270 = f32[3,384,384]{1,2,0:T(8,128)} reshape(f32[3,8,48,16,24]{2,1,4,3,0:T(8,128)} %copy.147) | data formatting | bytes 3538944 | tf_op jit(solution)/shard_map/reshape | solution.py:128
  225.4 5.0 %reshape.271 = f32[3,8,48,16,24]{2,1,4,3,0:T(8,128)} reshape(f32[3,384,384]{1,2,0:T(8,128)} %fusion.65) | data formatting | bytes 3538944 | tf_op jit(solution)/shard_map/reshape | solution.py:134
  230.3 8.1 %copy.152 = f32[16,8,3,48,24]{4,3,2,1,0:T(8,128)} copy(f32[16,8,3,48,24]{3,1,4,0,2:T(8,128)} %bitcast.137) | data formatting | bytes 3538944 | tf_op jit(solution)/shard_map/transpose | solution.py:134
  238.5 9.9 %reshape.290 = f32[128,1,3456]{2,1,0:T(1,128)} reshape(f32[16,8,3,48,24]{4,3,2,1,0:T(8,128)} %copy.152) | data formatting | bytes 3538944 | tf_op jit(solution)/shard_map/reshape | solution.py:67
  248.4 32.6 %all_to_all.42 = f32[128,1,3456]{2,1,0:T(1,128)} all-to-all(f32[128,1,3456]{2,1,0:T(1,128)} %reshape.290), channel_id=1, replica_groups=mesh['rows_0'=4,'rows_1'=2,'rows_2'=2,'cols_0'=4,'cols_1'=2] {'rows_0','..., dimensions={0} | all-to-all | bytes 3538944 | tf_op jit(solution)/shard_map/all_to_all | solution.py:68
  281.0 6.9 %reduce.7 = f32[128,3456]{1,0:T(8,128)} reduce(f32[128,1,3456]{2,1,0:T(1,128)} %all_to_all.42, f32[]{:T(128)} %constant.111), dimensions={1}, to_apply=%all_to_all.30.reduce_sub_computation | reduce | bytes 3538948 | tf_op jit(solution)/shard_map/all_to_all | solution.py:68
  290.7 7.0 %fusion.13 = (f32[]{:T(128)}, f32[1152,384]{1,0:T(8,128)}) fusion(f32[48,24,384]{2,1,0:T(8,128)} %param.23, f32[1152,384]{1,0:T(8,128)S(1)} %convolution_multiply_fusion, f32[384,1152]{1,0:T(8,128)} %reshape.278, f32[384,384]{1,0:T(8,128)S(1)} %copy-done.7), kind=kOutput, calls=%fused_computation.16 | convolution fusion | flops 1022754816 | bytes 7667716 | tf_op jit(solution)/shard_map/Xx,xm->Xm/dot_general | solution.py:63
  298.3 14.2 %all_to_all.43 = f32[128,1,128]{2,1,0:T(1,128)S(1)} all-to-all(f32[128,1,128]{2,1,0:T(1,128)S(1)} %reshape.275), channel_id=1, replica_groups=mesh['rows_0'=4,'rows_1'=2,'rows_2'=2,'cols_0'=4,'cols_1'=2] {'rows_0','..., dimensions={0} | all-to-all | bytes 131072 | tf_op jit(solution)/shard_map/all_to_all | solution.py:68
  313.9 3.8 %fusion.18 = f32[1152,384]{1,0:T(8,128)} fusion(f32[1152,384]{1,0:T(8,128)S(1)} %convolution_multiply_fusion, f32[1152,384]{1,0:T(8,128)} %get-tuple-element.14, f32[48,24,384]{2,1,0:T(8,128)} %param.23, f32[]{:T(128)S(6)} %rsqrt.7), kind=kLoop, calls=%fused_computation.23 | loop fusion | flops 3096576 | bytes 7077892 | tf_op jit(solution)/shard_map/mul | solution.py:144
  (98 shorter events, 68.6 us)
Async XLA Ops:
  0.0 1.0 copy-start
  36.5 2.2 copy-start.4
  38.7 0.9 copy-start.3
  42.5 7.8 %copy-start.10 = (f32[12,24,192]{2,1,0:T(8,128)S(1)}, f32[12,24,192]{2,1,0:T(8,128)}, u32[]{:S(2)}) copy-start(f32[12,24,192]{2,1,0:T(8,128)} %param.22) | copy-start | bytes 663556
  45.2 21.0 %all-to-all-start.2 = ((f32[64,1,3456]{2,1,0:T(1,128)}), f32[64,1,3456]{2,1,0:T(1,128)S(1)}, u32[]{:S(2)}, u32[]{:S(2)}) async-start(f32[64,1,3456]{2,1,0:T(1,128)} %reshape.288), calls=%async_computation.2 | async-start | bytes 1769472 | tf_op jit(solution)/shard_map/all_to_all | solution.py:68
  50.3 1.9 collective-permute-start
  66.2 15.1 %all-to-all-start = ((f32[8,1,13824]{2,1,0:T(1,128)}), f32[8,1,13824]{2,1,0:T(1,128)S(1)}, u32[]{:S(2)}, u32[]{:S(2)}) async-start(f32[8,1,13824]{2,1,0:T(1,128)} %reshape.251), calls=%async_computation | async-start | bytes 884736 | tf_op jit(solution)/shard_map/all_to_all | solution.py:68
  78.6 9.8 %copy-start.11 = (f32[8,2,24,192]{3,2,0,1:T(8,128)S(1)}, f32[8,2,24,192]{3,2,0,1:T(8,128)}, u32[]{:S(2)}) copy-start(f32[8,2,24,192]{3,2,0,1:T(8,128)} %constant.103) | copy-start | bytes 884740
  81.2 21.1 %all-to-all-start.3 = ((f32[64,1,3456]{2,1,0:T(1,128)}), f32[64,1,3456]{2,1,0:T(1,128)S(1)}, u32[]{:S(2)}, u32[]{:S(2)}) async-start(f32[64,1,3456]{2,1,0:T(1,128)} %reshape.289), calls=%async_computation.3 | async-start | bytes 1769472 | tf_op jit(solution)/shard_map/all_to_all | solution.py:68
  106.6 1.4 copy-start.5
  106.7 1.8 copy-start.9
  138.3 1.6 copy-start.8
  139.2 2.0 copy-start.6
  151.7 35.0 %all-to-all-start.5 = ((f32[128,1,3456]{2,1,0:T(1,128)}), f32[128,1,3456]{2,1,0:T(1,128)}, u32[]{:S(2)}, u32[]{:S(2)}) async-start(f32[128,1,3456]{2,1,0:T(1,128)} %copy.146), calls=%async_computation.5 | async-start | bytes 3538944 | tf_op jit(solution)/shard_map/all_to_all | solution.py:68
  210.1 5.2 %copy-start.2 = (f32[384,384,1]{1,0,2:T(8,128)S(1)}, f32[384,384,1]{1,0,2:T(8,128)}, u32[]{:S(2)}) copy-start(f32[384,384,1]{1,0,2:T(8,128)} %constant.110) | copy-start | bytes 1769476
  287.9 2.8 copy-start.7
  313.9 3.8 %copy-start.1 = (f32[12,24,192]{2,1,0:T(8,128)S(1)}, f32[12,24,192]{2,1,0:T(8,128)}, u32[]{:S(2)}) copy-start(f32[12,24,192]{2,1,0:T(8,128)} %param.21) | copy-start | bytes 663556

commit v2 on v1

v2 whole, which is shorter than its diff:
```python
import math

import jax
import jax.numpy as jnp
import numpy as np
from jax import lax
from jax.experimental import pallas as pl
from jax.experimental.pallas import tpu as pltpu
from jax.sharding import Mesh
from jax.sharding import PartitionSpec as P

NC = 192
NF = 384
ROWS = ("rows_0", "rows_1", "rows_2")
COLS = ("cols_0", "cols_1")
ALL = ROWS + COLS
CHIPS = ("rows_0", "rows_1", "cols_0", "cols_1")
CORE = "rows_2"

TIME_STEP = 0.5
CONTACT = 0.4
DIPOLE_STRENGTH = 0.3
EPSILON = 1e-06


def cas_table(rows, columns, length):
    phases = 2.0 * math.pi / length * ((np.outer(rows, columns)) % length)
    return np.cos(phases) + np.sin(phases)


def signed(length):
    k = np.arange(length)
    return np.where(k < length // 2, k, k - length)


def tables():
    k = np.arange(NC)
    wave = 2.0 * math.pi / NF * signed(NC)
    decay = np.exp(-0.5 * TIME_STEP * wave**2)
    hc = cas_table(k, k, NC)
    hf = cas_table(np.arange(NF), np.arange(NF), NF)
    evolve = hc @ (decay[:, None] * hc) / NC
    lifted = np.where(k < NC // 2, k, k + NC)
    lift = hf[:, lifted] @ (decay[:, None] * hc) / NC
    return [t.astype(np.float32) for t in (hc, hf, evolve, lift)]


HC, HF, EVOLVE, LIFT = tables()


def squares(index, length, spacing):
    s = jnp.where(index < length // 2, index, index - length).astype(jnp.float32)
    w = 2.0 * math.pi / (length * spacing) * s
    return w * w


def dipolar(wx, wy, wz, length):
    q = wx + wy + wz
    safe = jnp.where(q > 0, q, 1.0)
    return jnp.where(q > 0, DIPOLE_STRENGTH * (3.0 * wz - q) / safe, 0.0) / float(length) ** 3


F32 = jnp.float32
BF16 = jnp.bfloat16
VMEM = pl.BlockSpec(memory_space=pltpu.VMEM)
SMEM = pl.BlockSpec(memory_space=pltpu.SMEM)


def halves(table):
    high = table.astype(BF16)
    return np.stack([high, (table - high.astype(np.float32)).astype(BF16)])


HF2 = halves(HF)
BY_SLAB = np.arange(NF).reshape(8, 48).T.reshape(-1)
HF_OUT2 = halves(HF[:, BY_SLAB])
HF_BACK2 = halves(HF[BY_SLAB, :])
PLANE = np.arange(NC).reshape(16, 12).T.reshape(-1)
LIFT_X2 = halves(LIFT[:, np.arange(NC).reshape(64, 3).T.reshape(-1)])
HC2 = halves(HC)
HC_WIDE2 = halves(np.pad(HC, ((0, 64), (0, 64))))
EVOLVE2 = halves(EVOLVE)
EVOLVE_Y2 = halves(np.pad(EVOLVE, ((0, 0), (0, 64))))
EVOLVE_X2 = halves(np.concatenate([EVOLVE[PLANE, :]] * 2, axis=1))
LIFT_Z2 = halves(LIFT[BY_SLAB, :])
LIFT_Y2 = np.stack(
    [
        halves(np.pad(LIFT.reshape(8, 2, 24, NC)[:, core].reshape(NC, NC).T, ((0, 0), (0, 64))))
        for core in range(2)
    ]
)
TURNED = (((1,), (1,)), ((), ()))
PLAIN = (((1,), (0,)), ((), ()))


def split(x):
    high = x.astype(BF16)
    return high, (x - high.astype(F32)).astype(BF16)


def dot3(a, b, dims=PLAIN):
    (ah, al), (bh, bl) = a, b

    def dot(p, q):
        return lax.dot_general(p, q, dims, preferred_element_type=F32)

    return dot(ah, bh) + (dot(al, bh) + dot(ah, bl))


def pair(ref):
    return ref[0], ref[1]


def tiles_of(row):
    return [row[:, 128 * t : 128 * t + 128] for t in range(row.shape[1] // 128)]


def turn_blocks(rows, count, lead=0):
    lane = lax.broadcasted_iota(jnp.int32, rows[0][0].shape, 1)
    shifted = []
    for a, row in enumerate(rows):
        shift = (24 * a - lead) % NF
        whole = jnp.concatenate(row, axis=1)
        shifted.append(tiles_of(pltpu.roll(whole, shift, 1) if shift else whole))
    result = []
    for b in range(count):
        tiles = []
        for t in range(3):
            tile = None
            for p in range(128 * t // 24, (128 * t + 127) // 24 + 1):
                a = (p - b) % 16
                if a < len(rows):
                    piece = shifted[a][t]
                    tile = piece if tile is None else jnp.where(lane < 24 * p - 128 * t, tile, piece)
            tiles.append(shifted[0][t] if tile is None else tile)
        whole = jnp.concatenate(tiles, axis=1)
        result.append(pltpu.roll(whole, NF - 24 * b, 1) if b else whole)
    return result


def coarse_pencil_kernel(wave_ref, matrix_ref, out_ref):
    high, low = split(wave_ref[...])
    pieces = []
    for k in range(3):
        lead = 32 * k

        def padded(x):
            parts = [jnp.zeros((lead, NC), BF16)] * (k > 0) + [x]
            return jnp.concatenate(parts + [jnp.zeros((96 - lead, NC), BF16)], axis=0)

        rows = slice(64 * k, 64 * k + 64)
        matrix = (matrix_ref[0, rows, :], matrix_ref[1, rows, :])
        pieces.append(tiles_of(dot3(matrix, (padded(high), padded(low)), TURNED)))
    (a0, a1, a2), (b0, b1, b2), (c0, c1, c2) = pieces
    for t, tile in enumerate([a0, a1, a2 + b0, b1, b2 + c0, c1, c2]):
        for p in range(8):
            for core in range(2):
                out_ref[pl.ds(p * 112 + core * 56 + t, 8, stride=7), :] = tile[8 * p : 8 * p + 8, :]


def coarse_pencil(wave):
    return pl.pallas_call(
        coarse_pencil_kernel,
        out_shape=jax.ShapeDtypeStruct((896, 128), F32),
        in_specs=[VMEM] * 2,
        out_specs=VMEM,
    )(wave, jnp.asarray(EVOLVE2))


def coarse_z_kernel(got_ref, ey_ref, ex_ref, matrix_ref, out_ref, plane_ref):
    lane = lax.broadcasted_iota(jnp.int32, (64, 128), 1)
    for k in range(3):
        for g in range(2):
            rows = [
                [got_ref[pl.ds(g * 448 + c * 7 + 2 * k + t, 8, stride=56), :] for t in range(3)]
                for c in range(8)
            ]
            for i, row in enumerate(turn_blocks(rows, 12, 32 * k)):
                plane_ref[16 * i + 8 * g : 16 * i + 8 * g + 8, :] = row[:, :256]
        half = dot3(pair(ey_ref), split(plane_ref[...]), TURNED)
        evolved = dot3(split(half), pair(ex_ref))
        density = evolved[:, :256] * evolved[:, :256]
        turned = dot3(pair(matrix_ref), split(density))
        for j in range(3):
            f = tiles_of(turned[64 * j : 64 * j + 64, :])
            e = tiles_of(evolved[64 * j : 64 * j + 64, :])
            for t, tile in enumerate([f[0], jnp.where(lane < 64, f[1], e[1]), e[2]]):
                out_ref[pl.ds(k * 9 + j * 3 + t, 64, stride=27), :] = tile


def coarse_z(got):
    return pl.pallas_call(
        coarse_z_kernel,
        out_shape=jax.ShapeDtypeStruct((1728, 128), F32),
        in_specs=[VMEM] * 4,
        out_specs=VMEM,
        scratch_shapes=[pltpu.VMEM((NC, 256), F32)],
    )(got, jnp.asarray(EVOLVE_Y2), jnp.asarray(EVOLVE_X2), jnp.asarray(HC2))


def rows_of_plane(got_ref, base):
    rows = []
    for j in range(3):
        tiles = [got_ref[pl.ds(base + 9 * j + t, 64, stride=27), :] for t in range(3)]
        rows.append(jnp.concatenate(tiles, axis=1))
    return jnp.concatenate(rows, axis=0)


def coarse_y_kernel(chip_ref, got_ref, matrix_ref, wide_ref, out_ref):
    lane = lax.broadcasted_iota(jnp.int32, (NC, 128), 1)
    wx = squares(lax.broadcasted_iota(jnp.int32, (NC, 256), 0), NC, 2.0)
    wz = squares(lax.broadcasted_iota(jnp.int32, (NC, 256), 1), NC, 2.0)
    for k in range(3):
        both = rows_of_plane(got_ref, 3 * k)
        both = jnp.concatenate([both, jnp.zeros((64, 384), F32)], axis=0).T
        mid = dot3(pair(matrix_ref), split(both[:NC, :]))
        mid = dot3(split(mid), pair(wide_ref))
        wy = squares(jnp.full((1, 1), 64 * k + chip_ref[0], jnp.int32), NC, 2.0)
        mid = mid * dipolar(wx, wy, wz, NC)
        mid = dot3(split(mid), pair(wide_ref))
        q = tiles_of(dot3(pair(matrix_ref), split(mid)))
        e = [pltpu.roll(tile, 64, 1) for tile in tiles_of(both[NC:, :])]
        pieces = [q[0], jnp.where(lane < 64, q[1], e[0]), jnp.where(lane < 64, e[0], e[1])]
        for t, tile in enumerate(pieces):
            out_ref[pl.ds(3 * k + t, NC, stride=9), :] = tile


def coarse_y(chip, got):
    return pl.pallas_call(
        coarse_y_kernel,
        out_shape=jax.ShapeDtypeStruct((1728, 128), F32),
        in_specs=[SMEM] + [VMEM] * 3,
        out_specs=VMEM,
    )(chip, got, jnp.asarray(HC2), jnp.asarray(HC_WIDE2))


def coarse_x_kernel(core_ref, got_ref, potential_ref, matrix_ref, lz_ref, ly_ref, out_ref, lifted_ref):
    lane = lax.broadcasted_iota(jnp.int32, (NC, 128), 1)
    core = core_ref[0]
    lift_y = (ly_ref[core, 0], ly_ref[core, 1])
    part = jnp.zeros((1, 1), F32)
    blank = jnp.zeros((8, 128), F32)
    for k in range(3):
        rows = []
        for j in range(3):
            tiles = [got_ref[pl.ds(9 * k + 3 * j + t, 64, stride=27), :] for t in range(3)]
            rows.append(jnp.concatenate(tiles, axis=1))
        both = jnp.concatenate(rows, axis=0)
        field = dot3(pair(matrix_ref), split(both[:, :256]))
        e1, e2 = [pltpu.roll(tile, 64, 1) for tile in tiles_of(both)[1:]]
        evolved = [jnp.where(lane < 64, e1, e2), e2[:, :64]]
        pieces = []
        for t, e in enumerate(evolved):
            lanes = slice(128 * t, 128 * t + e.shape[1])
            v = jnp.concatenate([potential_ref[c, 24 * k : 24 * k + 24, lanes] for c in range(8)], axis=0)
            d = jnp.exp(-TIME_STEP * (v + CONTACT * e * e + field[:, lanes])) * e
            part = part + jnp.sum(d * d, keepdims=True)
            pieces.append(d)
        damped = split(jnp.concatenate(pieces, axis=1))
        lifted = dot3(pair(lz_ref), damped, TURNED)
        lifted_ref[...] = dot3(split(lifted), lift_y)
        for g in range(3):
            rows = []
            for i in range(16):
                row = lifted_ref[128 * g + 8 * i : 128 * g + 8 * i + 8, :]
                rows.append(tiles_of(row) + [blank])
            for p, row in enumerate(turn_blocks(rows, 8)):
                for t, tile in enumerate(tiles_of(row)):
                    out_ref[pl.ds(p * 224 + k * 9 + g * 3 + t, 8, stride=28), :] = tile
    out_ref[pl.ds(27, 64, stride=28), :] = jnp.broadcast_to(part, (64, 128))


def coarse_x(core, got, potential):
    return pl.pallas_call(
        coarse_x_kernel,
        out_shape=jax.ShapeDtypeStruct((1792, 128), F32),
        in_specs=[SMEM] + [VMEM] * 5,
        out_specs=VMEM,
        scratch_shapes=[pltpu.VMEM((NF, 256), F32)],
    )(core, got, potential, jnp.asarray(HC2), jnp.asarray(LIFT_Z2), jnp.asarray(LIFT_Y2))


def fine_in_kernel(got_ref, lift_ref, matrix_ref, evolved_ref, out_ref):
    parts = got_ref[pl.ds(27, 64, stride=28), :]
    total = jnp.sum(parts, axis=0, keepdims=True)
    scale = lax.rsqrt(total / float(NC) ** 3 + EPSILON)
    scale = jnp.concatenate([scale] * 3, axis=1)

    def body(n, carry):
        rows = []
        for k in range(3):
            tiles = [got_ref[pl.ds(k * 9 + 3 * n + t, 64, stride=28), :] for t in range(3)]
            rows.append(jnp.concatenate(tiles, axis=1))
        spectrum = split(jnp.concatenate(rows, axis=0))
        evolved = dot3(pair(lift_ref), spectrum) * scale
        evolved_ref[:, pl.ds(pl.multiple_of(n * 384, 128), 384)] = evolved
        turned = dot3(pair(matrix_ref), split(evolved * evolved))
        for k in range(3):
            for t in range(3):
                piece = turned[128 * k : 128 * k + 128, 128 * t : 128 * t + 128]
                out_ref[pl.ds(k * 9 + 3 * n + t, 128, stride=27), :] = piece
        return carry

    lax.fori_loop(0, 3, body, 0)


def fine_in(got):
    return pl.pallas_call(
        fine_in_kernel,
        out_shape=[
            jax.ShapeDtypeStruct((NF, 1152), F32),
            jax.ShapeDtypeStruct((3456, 128), F32),
        ],
        in_specs=[VMEM] * 3,
        out_specs=[VMEM] * 2,
    )(got, jnp.asarray(LIFT_X2), jnp.asarray(HF2))


def fine_slab_kernel(device_ref, got_ref, out_m_ref, back_m_ref, matrix_ref, out_ref, plane_ref):
    wz = squares(lax.broadcasted_iota(jnp.int32, (NF, NF), 0), NF, 1.0)
    wy = squares(lax.broadcasted_iota(jnp.int32, (NF, NF), 1), NF, 1.0)

    def body(k, carry):
        def unpack(g, carry):
            base = k * 9 + g * 3
            rows = [
                [got_ref[pl.ds(r * 216 + base + t, 8, stride=27), :] for t in range(3)]
                for r in range(16)
            ]
            for i, row in enumerate(turn_blocks(rows, 16)):
                plane_ref[pl.ds(pl.multiple_of(g * 128 + 8 * i, 8), 8), :] = row
            return carry

        lax.fori_loop(0, 3, unpack, 0)
        mid = dot3(pair(out_m_ref), split(plane_ref[...]))
        mid = dot3(split(mid), pair(matrix_ref))
        kx = 128 * k + device_ref[0]
        wx = squares(jnp.full((1, 1), kx, jnp.int32), NF, 1.0)
        mid = mid * dipolar(wx, wy, wz, NF)
        mid = dot3(split(mid), pair(matrix_ref))
        plane_ref[...] = dot3(pair(back_m_ref), split(mid))

        def pack(g, carry):
            base = k * 9 + g * 3
            rows = []
            for i in range(16):
                rows.append(tiles_of(plane_ref[pl.ds(pl.multiple_of(g * 128 + 8 * i, 8), 8), :]))
            for r, row in enumerate(turn_blocks(rows, 16)):
                for t, tile in enumerate(tiles_of(row)):
                    out_ref[pl.ds(r * 216 + base + t, 8, stride=27), :] = tile
            return carry

        lax.fori_loop(0, 3, pack, 0)
        return carry

    lax.fori_loop(0, 3, body, 0)


def fine_slab(device, got):
    return pl.pallas_call(
        fine_slab_kernel,
        out_shape=jax.ShapeDtypeStruct((3456, 128), F32),
        in_specs=[SMEM] + [VMEM] * 4,
        out_specs=VMEM,
        scratch_shapes=[pltpu.VMEM((NF, NF), F32)],
    )(device, got, jnp.asarray(HF_OUT2), jnp.asarray(HF_BACK2), jnp.asarray(HF2))


def fine_out_kernel(got_ref, evolved_ref, potential_ref, matrix_ref, damped_ref, part_ref):
    part_ref[...] = jnp.zeros_like(part_ref)

    def body(n, carry):
        rows = []
        for k in range(3):
            tiles = [got_ref[pl.ds(k * 9 + 3 * n + t, 128, stride=27), :] for t in range(3)]
            rows.append(jnp.concatenate(tiles, axis=1))
        field = dot3(pair(matrix_ref), split(jnp.concatenate(rows, axis=0)))
        columns = pl.ds(pl.multiple_of(n * 384, 128), 384)
        evolved = evolved_ref[:, columns]
        potential = potential_ref[columns, :].T
        exponent = -TIME_STEP * (potential + CONTACT * evolved * evolved + field)
        damped = jnp.exp(exponent) * evolved
        part_ref[...] += jnp.sum(damped * damped)
        damped_ref[columns, :] = damped.T
        return carry

    lax.fori_loop(0, 3, body, 0)


def fine_out(got, evolved, potential):
    return pl.pallas_call(
        fine_out_kernel,
        out_shape=[
            jax.ShapeDtypeStruct((1152, NF), F32),
            jax.ShapeDtypeStruct((8, 128), F32),
        ],
        in_specs=[VMEM] * 4,
        out_specs=[VMEM] * 2,
    )(got, evolved, potential, jnp.asarray(HF2))


def exchange(buffer, axes, count):
    flat = buffer.reshape(count, 1, -1)
    return lax.all_to_all(flat, axes, split_axis=0, concat_axis=0, tiled=False)


def move_potential(potential, core):
    other = lax.ppermute(potential, CORE, [(0, 1), (1, 0)])
    low = jnp.where(core == 0, potential, other)
    high = jnp.where(core == 0, other, potential)
    both = jnp.concatenate([low, high], axis=0).reshape(8, 72, NC)
    return lax.all_to_all(both, COLS, split_axis=0, concat_axis=0, tiled=False)


def per_device(wave_coarse, potential_coarse, potential_fine):
    core = lax.axis_index(CORE)
    chip = lax.axis_index(CHIPS)
    device = lax.axis_index(ALL)
    v_slab = move_potential(potential_coarse, core)

    turned = coarse_pencil(wave_coarse.reshape(288, NC))
    turned = coarse_z(exchange(turned, ALL, 128).reshape(896, 128))
    turned = coarse_y(chip.reshape(1), exchange(turned, CHIPS, 64).reshape(1728, 128))
    got = exchange(turned, CHIPS, 64).reshape(1728, 128)
    turned = coarse_x(core.reshape(1), got, v_slab)
    got = exchange(turned, CHIPS, 64).reshape(1792, 128)

    evolved, spectrum = fine_in(got)
    got = exchange(spectrum, ALL, 128).reshape(3456, 128)
    spectrum = fine_slab(device.reshape(1), got)
    got = exchange(spectrum, ALL, 128).reshape(3456, 128)
    damped, part = fine_out(got, evolved, potential_fine.reshape(1152, NF))
    parts = exchange(jnp.broadcast_to(part[:1], (128, 128)), ALL, 128).reshape(128, 128)
    total = jnp.sum(parts[:, 0])
    return (damped * lax.rsqrt(total / float(NF) ** 3 + EPSILON)).reshape(48, 24, NF)


def solution(mesh):
    torus = Mesh(
        mesh.devices.reshape(4, 2, 2, 4, 2), ("rows_0", "rows_1", "rows_2", "cols_0", "cols_1")
    )
    return jax.shard_map(
        per_device,
        mesh=torus,
        in_specs=(P(ROWS, COLS, None), P(ROWS, COLS, None), P(COLS, ROWS, None)),
        out_specs=P(COLS, ROWS, None),
        check_vma=False,
    )
```

time: 322 us -> 226 us (0.70); the launches traced: 318 us -> 225 us
  local copies, waits for them, and re-layouts: 93 us -> 1.93 us
  Pallas kernels: 0 us -> 46.5 us
  matrix products: 27.6 us -> 0 us
  other arithmetic: 27.9 us -> 4.32 us
  blocking collectives: 90.4 us -> 109 us
  starting transfers between devices: 25.2 us -> 17.6 us
  waiting for transfers between devices: 51.5 us -> 45 us
    pallas_call x0 -> x7, Pallas kernels: none -> 46.5 us  [the longest x1 16.7 us: fine_slab(): pl.pallas_call(fine_slab_kernel, out_shape=jax.ShapeDtypeStruct((3456, 12...]
    reshape x15 -> x0, local copies, waits for them, and re-layouts: 37.3 us -> none  [the longest x3 8.59 us: per_device(): lifted.reshape(3, 8, 48, 8, 24).transpose(3, 1, 0, 2, 4).reshape(64, 3456)]
    dot_general x18 -> x0, matrix products: 27.6 us -> none  [es(): return jnp.einsum(spec, *args, precision=PREC)]
    reshape x9 -> x1, local copies, waits for them, and re-layouts: 24.7 us -> 0.04 us  [exchange(): flat = buffer.reshape(count, 1, -1)]
    all_to_all x6 -> x0, other arithmetic: 21 us -> none  [exchange(): return lax.all_to_all(flat, axes, split_axis=0, concat_axis=0, tiled=False)]
    transpose x6 -> x0, local copies, waits for them, and re-layouts: 20 us -> none  [the longest x1 8.22 us: per_device(): plane = got.transpose(2, 1, 3, 0, 4).reshape(3, NF, NF)]
    all_to_all x4 -> x5, blocking collectives: 90.4 us -> 109 us  [exchange(): return lax.all_to_all(flat, axes, split_axis=0, concat_axis=0, tiled=False)]
    all_to_all x4 -> x2, starting transfers between devices: 24.5 us -> 13.5 us  [exchange(): return lax.all_to_all(flat, axes, split_axis=0, concat_axis=0, tiled=False)]
  transfers between devices with their start and end apart: 5 -> 4, of which waited for: 4 -> 4; matrix products, arithmetic and copies ran while one was open for 5% -> 0% of each run, Pallas kernels for 0% -> 2%
where the time goes in v2:
time: 226 us; the launch traced here: 225 us
  blocking collectives  109 us (48%)
  Pallas kernels  46.5 us (21%)
  waiting for transfers between devices  45 us (20%)
  starting transfers between devices  17.6 us (8%)
  other arithmetic  4.32 us (2%)
    all_to_all x5, blocking collectives, exchange(): return lax.all_to_all(flat, axes, split_axis=0, concat_axis=0, tiled=False)  109 us
    all_to_all x2, waiting for transfers between devices, exchange(): return lax.all_to_all(flat, axes, split_axis=0, concat_axis=0, tiled=False)  39.5 us
    pallas_call x1, Pallas kernels, fine_slab(): pl.pallas_call(fine_slab_kernel, out_shape=jax.ShapeDtypeStruct((3456, 12...  16.7 us
    all_to_all x2, starting transfers between devices, exchange(): return lax.all_to_all(flat, axes, split_axis=0, concat_axis=0, tiled=False)  13.5 us
    pallas_call x1, Pallas kernels, fine_out(): pl.pallas_call(fine_out_kernel, out_shape=[jax.ShapeDtypeStruct((1152, NF...  6.98 us
    pallas_call x1, Pallas kernels, fine_in(): pl.pallas_call(fine_in_kernel, out_shape=[jax.ShapeDtypeStruct((NF, 1152)...  6.05 us
    pallas_call x1, Pallas kernels, coarse_x(): pl.pallas_call(coarse_x_kernel, out_shape=jax.ShapeDtypeStruct((1792, 128...  5.18 us
    pallas_call x1, Pallas kernels, coarse_y(): pl.pallas_call(coarse_y_kernel, out_shape=jax.ShapeDtypeStruct((1728, 128...  4.67 us
  transfers between devices with their start and end apart: 4, of which 4 were waited for; matrix products, arithmetic and copies ran while one was open for 0% of the time, Pallas kernels for 2%

profile of v2, /device:TPU:1, one launch (start us, length us, event | category | flops | bytes accessed | tf_op | source)
XLA Modules:
  0.0 225.4 jit_solution(10405426609172898907)
XLA Ops:
  0.0 2.4 %shard_map.136 = f32[896,128]{1,0:T(8,128)} custom-call(f32[288,192]{1,0:T(8,128)} %bitcast.35, bf16[2,192,192]{2,1,0:T(8,128)(2,1)} %constant.58.clone.matrix_ref), custom_call_target="tpu_custom_call" | custom-call | tf_op jit(solution)/shard_map/pallas_call | solution.py:162
  2.4 24.5 %all_to_all.40 = f32[128,1,896]{2,1,0:T(1,128)} all-to-all(f32[128,1,896]{2,1,0:T(1,128)} %bitcast.31), channel_id=1, replica_groups=mesh['rows_0'=4,'rows_1'=2,'rows_2'=2,'cols_0'=4,'cols_1'=2] {'rows_0','..., dimensions={0} | all-to-all | bytes 917504 | tf_op jit(solution)/shard_map/all_to_all | solution.py:404
  26.9 4.6 %shard_map.137 = f32[1728,128]{1,0:T(8,128)} custom-call(f32[896,128]{1,0:T(8,128)} %bitcast.32, bf16[2,192,256]{2,1,0:T(8,128)(2,1)} %constant.59.clone.ey_ref, bf16[2,192,384]{2,1,0:T(8,128)(2,1)} %constant.60.clone.ex_ref, bf16[2,192,192]{2,1,0:T(8,128)(2,1)} %constant.61.clone.matrix_ref), custom_call_target="tpu_custom_call" | custom-call | tf_op jit(solution)/shard_map/pallas_call | solution.py:192
  31.4 5.2 %all-to-all-start.1 = ((f32[64,1,3456]{2,1,0:T(1,128)}), f32[64,1,3456]{2,1,0:T(1,128)S(1)}, u32[]{:S(2)}, u32[]{:S(2)}) async-start(f32[64,1,3456]{2,1,0:T(1,128)} %bitcast.30), calls=%async_computation.1 | async-start | bytes 1769472 | tf_op jit(solution)/shard_map/all_to_all | solution.py:404
  37.2 1.2 collective-permute-done
  38.4 0.9 pad_maximum_fusion
  39.3 13.2 %all-to-all-done.1 = f32[64,1,3456]{2,1,0:T(1,128)S(1)} async-done(((f32[64,1,3456]{2,1,0:T(1,128)}), f32[64,1,3456]{2,1,0:T(1,128)S(1)}, u32[]{:S(2)}, u32[]{:S(2)}) %all-to-all-start.1) | async-done | bytes 884768 | tf_op jit(solution)/shard_map/all_to_all | solution.py:404
  52.5 3.5 %all-to-all-start.3 = ((f32[8,72,192]{2,1,0:T(8,128)}), f32[8,72,192]{2,1,0:T(8,128)S(1)}, u32[]{:S(2)}, u32[]{:S(2)}) async-start(f32[8,72,192]{2,1,0:T(8,128)} %bitcast.10), calls=%async_computation.3 | async-start | bytes 1179648 | tf_op jit(solution)/shard_map/all_to_all | solution.py:412
  56.1 4.7 %shard_map.138 = f32[1728,128]{1,0:T(8,128)} custom-call(s32[1]{0:T(128)} %bitcast.2.chip_ref, f32[1728,128]{1,0:T(8,128)} %bitcast.27, bf16[2,192,192]{2,1,0:T(8,128)(2,1)} %constant.61.clone.matrix_ref, bf16[2,256,256]{2,1,0:T(8,128)(2,1)} %constant.62.clone.wide_ref), custom_call_target="tpu_custom_call" | custom-call | tf_op jit(solution)/shard_map/pallas_call | solution.py:229
  60.7 4.3 %all-to-all-done.3.potential_ref = f32[8,72,192]{2,1,0:T(8,128)S(1)} async-done(((f32[8,72,192]{2,1,0:T(8,128)}), f32[8,72,192]{2,1,0:T(8,128)S(1)}, u32[]{:S(2)}, u32[]{:S(2)}) %all-to-all-start.3) | async-done | bytes 442400 | tf_op jit(solution)/shard_map/all_to_all | solution.py:412
  65.0 19.3 %all_to_all.41 = f32[64,1,3456]{2,1,0:T(1,128)} all-to-all(f32[64,1,3456]{2,1,0:T(1,128)} %bitcast.28), channel_id=1, replica_groups=mesh['rows_0'=4,'rows_1'=2,'rows_2'=2,'cols_0'=4,'cols_1'=2] {'rows_0','..., dimensions={0} | all-to-all | bytes 1769472 | tf_op jit(solution)/shard_map/all_to_all | solution.py:404
  84.3 5.2 %shard_map.139 = f32[1792,128]{1,0:T(8,128)} custom-call(s32[1]{0:T(128)} %bitcast.1.core_ref, f32[1728,128]{1,0:T(8,128)} %bitcast.29, f32[8,72,192]{2,1,0:T(8,128)} %copy-done.2, bf16[2,192,192]{2,1,0:T(8,128)(2,1)} %constant.61.clone.matrix_ref, bf16[2,384,192]{2,1,0:T(8,128)(2,1)} %constant.63.clone.lz_ref, bf16[2,2,192,256]{3,2,1,0:T(8,128)(2,1)} %constant.64.clone.ly_ref), custom_call_target="tpu_custom_call" | custom-call | tf_op jit(solution)/shard_map/pallas_call | solution.py:274
  89.5 18.8 %all_to_all.42 = f32[64,1,3584]{2,1,0:T(1,128)} all-to-all(f32[64,1,3584]{2,1,0:T(1,128)} %bitcast.25), channel_id=1, replica_groups=mesh['rows_0'=4,'rows_1'=2,'rows_2'=2,'cols_0'=4,'cols_1'=2] {'rows_0','..., dimensions={0} | all-to-all | bytes 1835008 | tf_op jit(solution)/shard_map/all_to_all | solution.py:404
  108.3 6.0 %shard_map.140 = (f32[384,1152]{1,0:T(8,128)}, f32[3456,128]{1,0:T(8,128)}) custom-call(f32[1792,128]{1,0:T(8,128)} %bitcast.26, bf16[2,384,192]{2,1,0:T(8,128)(2,1)} %constant.65.clone.lift_ref, bf16[2,384,384]{2,1,0:T(8,128)(2,1)} %constant.66.clone.matrix_ref), custom_call_target="tpu_custom_call" | custom-call | tf_op jit(solution)/shard_map/pallas_call | solution.py:308
  114.4 8.3 %all-to-all-start.5 = ((f32[128,1,3456]{2,1,0:T(1,128)}), f32[128,1,3456]{2,1,0:T(1,128)S(1)}, u32[]{:S(2)}, u32[]{:S(2)}) async-start(f32[128,1,3456]{2,1,0:T(1,128)} %bitcast.34), calls=%async_computation.5 | async-start | bytes 3538944 | tf_op jit(solution)/shard_map/all_to_all | solution.py:404
  122.7 26.4 %all-to-all-done.5 = f32[128,1,3456]{2,1,0:T(1,128)S(1)} async-done(((f32[128,1,3456]{2,1,0:T(1,128)}), f32[128,1,3456]{2,1,0:T(1,128)S(1)}, u32[]{:S(2)}, u32[]{:S(2)}) %all-to-all-start.5) | async-done | bytes 1769504 | tf_op jit(solution)/shard_map/all_to_all | solution.py:404
  149.1 1.2 copy-done
  150.3 16.7 %shard_map.141 = f32[3456,128]{1,0:T(8,128)} custom-call(s32[1]{0:T(128)} %bitcast.device_ref, f32[3456,128]{1,0:T(8,128)} %bitcast.22, bf16[2,384,384]{2,1,0:T(8,128)(2,1)} %constant.67.clone.out_m_ref, bf16[2,384,384]{2,1,0:T(8,128)(2,1)} %constant.68.clone.back_m_ref, bf16[2,384,384]{2,1,0:T(8,128)(2,1)} %constant.66.clone.matrix_ref), custom_call_target="tpu_custom_call" | custom-call | tf_op jit(solution)/shard_map/pallas_call | solution.py:360
  166.9 32.4 %all_to_all.43 = f32[128,1,3456]{2,1,0:T(1,128)} all-to-all(f32[128,1,3456]{2,1,0:T(1,128)} %bitcast.24), channel_id=1, replica_groups=mesh['rows_0'=4,'rows_1'=2,'rows_2'=2,'cols_0'=4,'cols_1'=2] {'rows_0','..., dimensions={0} | all-to-all | bytes 3538944 | tf_op jit(solution)/shard_map/all_to_all | solution.py:404
  199.4 7.0 %shard_map.142 = (f32[1152,384]{1,0:T(8,128)}, f32[8,128]{1,0:T(8,128)}) custom-call(f32[3456,128]{1,0:T(8,128)} %bitcast.23, f32[384,1152]{1,0:T(8,128)} %get-tuple-element.10.evolved_ref, f32[1152,384]{1,0:T(8,128)} %bitcast.33, bf16[2,384,384]{2,1,0:T(8,128)(2,1)} %constant.66.clone.matrix_ref), custom_call_target="tpu_custom_call" | custom-call | tf_op jit(solution)/shard_map/pallas_call | solution.py:391
  206.4 0.7 slice_bitcast_fusion
  207.1 14.2 %all_to_all.44 = f32[128,1,128]{2,1,0:T(1,128)S(1)} all-to-all(f32[128,1,128]{2,1,0:T(1,128)S(1)} %reshape.81), channel_id=1, replica_groups=mesh['rows_0'=4,'rows_1'=2,'rows_2'=2,'cols_0'=4,'cols_1'=2] {'rows_0','..., dimensions={0} | all-to-all | bytes 131072 | tf_op jit(solution)/shard_map/all_to_all | solution.py:404
  221.3 0.6 slice_reduce_fusion
  222.6 2.8 %broadcast_multiply_fusion = f32[1152,384]{1,0:T(8,128)} fusion(f32[1152,384]{1,0:T(8,128)} %get-tuple-element.11, f32[]{:T(128)S(6)} %rsqrt.3), kind=kLoop, calls=%fused_computation | loop fusion | flops 442368 | bytes 3538948 | tf_op jit(solution)/shard_map/mul | solution.py:435
  (10 shorter events, 0.7 us)
Async XLA Ops:
  26.8 9.8 %copy-start.3 = (f32[12,24,192]{2,1,0:T(8,128)S(1)}, f32[12,24,192]{2,1,0:T(8,128)}, u32[]{:S(2)}) copy-start(f32[12,24,192]{2,1,0:T(8,128)} %param.15) | copy-start | bytes 663556
  31.4 21.1 %all-to-all-start.1 = ((f32[64,1,3456]{2,1,0:T(1,128)}), f32[64,1,3456]{2,1,0:T(1,128)S(1)}, u32[]{:S(2)}, u32[]{:S(2)}) async-start(f32[64,1,3456]{2,1,0:T(1,128)} %bitcast.30), calls=%async_computation.1 | async-start | bytes 1769472 | tf_op jit(solution)/shard_map/all_to_all | solution.py:404
  36.6 1.8 collective-permute-start
  52.5 3.6 %copy-start.1 = (f32[64,1,3456]{2,1,0:T(1,128)}, f32[64,1,3456]{2,1,0:T(1,128)S(1)}, u32[]{:S(2)}) copy-start(f32[64,1,3456]{2,1,0:T(1,128)S(1)} %all-to-all-done.1) | copy-start | bytes 2654212
  52.5 12.5 %all-to-all-start.3 = ((f32[8,72,192]{2,1,0:T(8,128)}), f32[8,72,192]{2,1,0:T(8,128)S(1)}, u32[]{:S(2)}, u32[]{:S(2)}) async-start(f32[8,72,192]{2,1,0:T(8,128)} %bitcast.10), calls=%async_computation.3 | async-start | bytes 1179648 | tf_op jit(solution)/shard_map/all_to_all | solution.py:412
  65.0 19.3 %copy-start.2 = (f32[8,72,192]{2,1,0:T(8,128)}, f32[8,72,192]{2,1,0:T(8,128)S(1)}, u32[]{:S(2)}) copy-start(f32[8,72,192]{2,1,0:T(8,128)S(1)} %all-to-all-done.3.potential_ref) | copy-start | bytes 1327108
  114.4 34.7 %all-to-all-start.5 = ((f32[128,1,3456]{2,1,0:T(1,128)}), f32[128,1,3456]{2,1,0:T(1,128)S(1)}, u32[]{:S(2)}, u32[]{:S(2)}) async-start(f32[128,1,3456]{2,1,0:T(1,128)} %bitcast.34), calls=%async_computation.5 | async-start | bytes 3538944 | tf_op jit(solution)/shard_map/all_to_all | solution.py:404
  149.1 1.2 copy-start

commit v3 on v2

--- a/solution.py
+++ b/solution.py
@@ -64,6 +64,8 @@
 BF16 = jnp.bfloat16
 VMEM = pl.BlockSpec(memory_space=pltpu.VMEM)
 SMEM = pl.BlockSpec(memory_space=pltpu.SMEM)
+HBM = pl.BlockSpec(memory_space=pltpu.HBM)
+LIMIT = pltpu.CompilerParams(vmem_limit_bytes=20 * 1024 * 1024)
 
 
 def halves(table):
@@ -105,6 +107,46 @@
         return lax.dot_general(p, q, dims, preferred_element_type=F32)
 
     return dot(ah, bh) + (dot(al, bh) + dot(ah, bl))
+
+
+def dot(a, b):
+    return jnp.dot(a, b, preferred_element_type=F32)
+
+
+def left3(x):
+    high, low = split(x)
+    return jnp.concatenate([high, low, high], axis=1)
+
+
+def right3(x):
+    high, low = split(x)
+    return jnp.concatenate([high, high, low], axis=0)
+
+
+def fetch_left(table, wide, sems):
+    size = table.shape[2]
+    return [
+        pltpu.make_async_copy(table.at[part], wide.at[:, pl.ds(i * size, size)], sems.at[i])
+        for i, part in enumerate((0, 1, 0))
+    ]
+
+
+def fetch_right(table, tall, sems):
+    size = table.shape[1]
+    return [
+        pltpu.make_async_copy(table.at[part], tall.at[pl.ds(i * size, size), :], sems.at[i])
+        for i, part in enumerate((0, 0, 1))
+    ]
+
+
+def begin(copies):
+    for copy in copies:
+        copy.start()
+
+
+def finish(copies):
+    for copy in copies:
+        copy.wait()
 
 
 def pair(ref):
@@ -138,7 +180,13 @@
     return result
 
 
-def coarse_pencil_kernel(wave_ref, matrix_ref, out_ref):
+def coarse_pencil_kernel(wave_hbm, matrix_hbm, out_ref, wave_ref, matrix_ref, sems):
+    copies = [
+        pltpu.make_async_copy(wave_hbm, wave_ref, sems.at[0]),
+        pltpu.make_async_copy(matrix_hbm, matrix_ref, sems.at[1]),
+    ]
+    begin(copies)
+    finish(copies)
     high, low = split(wave_ref[...])
     pieces = []
     for k in range(3):
@@ -162,8 +210,14 @@
     return pl.pallas_call(
         coarse_pencil_kernel,
         out_shape=jax.ShapeDtypeStruct((896, 128), F32),
-        in_specs=[VMEM] * 2,
+        compiler_params=LIMIT,
+        in_specs=[HBM] * 2,
         out_specs=VMEM,
+        scratch_shapes=[
+            pltpu.VMEM((288, NC), F32),
+            pltpu.VMEM((2, NC, NC), BF16),
+            pltpu.SemaphoreType.DMA((2,)),
+        ],
     )(wave, jnp.asarray(EVOLVE2))
 
 
@@ -192,6 +246,7 @@
     return pl.pallas_call(
         coarse_z_kernel,
         out_shape=jax.ShapeDtypeStruct((1728, 128), F32),
+        compiler_params=LIMIT,
         in_specs=[VMEM] * 4,
         out_specs=VMEM,
         scratch_shapes=[pltpu.VMEM((NC, 256), F32)],
@@ -206,7 +261,7 @@
     return jnp.concatenate(rows, axis=0)
 
 
-def coarse_y_kernel(chip_ref, got_ref, matrix_ref, wide_ref, out_ref):
+def coarse_y_kernel(place_ref, got_ref, matrix_ref, wide_ref, out_ref):
     lane = lax.broadcasted_iota(jnp.int32, (NC, 128), 1)
     wx = squares(lax.broadcasted_iota(jnp.int32, (NC, 256), 0), NC, 2.0)
     wz = squares(lax.broadcasted_iota(jnp.int32, (NC, 256), 1), NC, 2.0)
@@ -215,7 +270,7 @@
         both = jnp.concatenate([both, jnp.zeros((64, 384), F32)], axis=0).T
         mid = dot3(pair(matrix_ref), split(both[:NC, :]))
         mid = dot3(split(mid), pair(wide_ref))
-        wy = squares(jnp.full((1, 1), 64 * k + chip_ref[0], jnp.int32), NC, 2.0)
+        wy = squares(jnp.full((1, 1), 64 * k + place_ref[3], jnp.int32), NC, 2.0)
         mid = mid * dipolar(wx, wy, wz, NC)
         mid = dot3(split(mid), pair(wide_ref))
         q = tiles_of(dot3(pair(matrix_ref), split(mid)))
@@ -225,18 +280,22 @@
             out_ref[pl.ds(3 * k + t, NC, stride=9), :] = tile
 
 
-def coarse_y(chip, got):
+def coarse_y(place, got):
     return pl.pallas_call(
         coarse_y_kernel,
         out_shape=jax.ShapeDtypeStruct((1728, 128), F32),
+        compiler_params=LIMIT,
         in_specs=[SMEM] + [VMEM] * 3,
         out_specs=VMEM,
-    )(chip, got, jnp.asarray(HC2), jnp.asarray(HC_WIDE2))
-
-
-def coarse_x_kernel(core_ref, got_ref, potential_ref, matrix_ref, lz_ref, ly_ref, out_ref, lifted_ref):
+    )(place, got, jnp.asarray(HC2), jnp.asarray(HC_WIDE2))
+
+
+def coarse_x_kernel(place_ref, got_ref, potential_ref, matrix_ref, lz_ref, ly_ref, out_ref, lifted_ref):
     lane = lax.broadcasted_iota(jnp.int32, (NC, 128), 1)
-    core = core_ref[0]
+    core = place_ref[0]
+    slots = []
+    for c in range(8):
+        slots.append(lax.rem(place_ref[1] - c // 2 + 4, 4) + 4 * (place_ref[2] ^ (c % 2)))
     lift_y = (ly_ref[core, 0], ly_ref[core, 1])
     part = jnp.zeros((1, 1), F32)
     blank = jnp.zeros((8, 128), F32)
@@ -252,7 +311,7 @@
         pieces = []
         for t, e in enumerate(evolved):
             lanes = slice(128 * t, 128 * t + e.shape[1])
-            v = jnp.concatenate([potential_ref[c, 24 * k : 24 * k + 24, lanes] for c in range(8)], axis=0)
+            v = jnp.concatenate([potential_ref[c, 24 * k : 24 * k + 24, lanes] for c in slots], axis=0)
             d = jnp.exp(-TIME_STEP * (v + CONTACT * e * e + field[:, lanes])) * e
             part = part + jnp.sum(d * d, keepdims=True)
             pieces.append(d)
@@ -270,21 +329,32 @@
     out_ref[pl.ds(27, 64, stride=28), :] = jnp.broadcast_to(part, (64, 128))
 
 
-def coarse_x(core, got, potential):
+def coarse_x(place, got, potential):
     return pl.pallas_call(
         coarse_x_kernel,
         out_shape=jax.ShapeDtypeStruct((1792, 128), F32),
+        compiler_params=LIMIT,
         in_specs=[SMEM] + [VMEM] * 5,
         out_specs=VMEM,
         scratch_shapes=[pltpu.VMEM((NF, 256), F32)],
-    )(core, got, potential, jnp.asarray(HC2), jnp.asarray(LIFT_Z2), jnp.asarray(LIFT_Y2))
-
-
-def fine_in_kernel(got_ref, lift_ref, matrix_ref, evolved_ref, out_ref):
+    )(place, got, potential, jnp.asarray(HC2), jnp.asarray(LIFT_Z2), jnp.asarray(LIFT_Y2))
+
+
+def fine_in_kernel(
+    got_ref, lift_ref, matrix_hbm, evolved_hbm, out_ref, evolved_ref, matrix_ref, sems, saved
+):
+    copies = fetch_left(matrix_hbm, matrix_ref, sems)
+    begin(copies)
     parts = got_ref[pl.ds(27, 64, stride=28), :]
     total = jnp.sum(parts, axis=0, keepdims=True)
     scale = lax.rsqrt(total / float(NC) ** 3 + EPSILON)
     scale = jnp.concatenate([scale] * 3, axis=1)
+    finish(copies)
+
+    def save(n):
+        columns = pl.ds(pl.multiple_of(n * 384, 128), 384)
+        source, target = evolved_ref.at[:, columns], evolved_hbm.at[:, columns]
+        return pltpu.make_async_copy(source, target, saved.at[n])
 
     def body(n, carry):
         rows = []
@@ -294,29 +364,45 @@
         spectrum = split(jnp.concatenate(rows, axis=0))
         evolved = dot3(pair(lift_ref), spectrum) * scale
         evolved_ref[:, pl.ds(pl.multiple_of(n * 384, 128), 384)] = evolved
-        turned = dot3(pair(matrix_ref), split(evolved * evolved))
+        turned = dot(matrix_ref[...], right3(evolved * evolved))
         for k in range(3):
             for t in range(3):
                 piece = turned[128 * k : 128 * k + 128, 128 * t : 128 * t + 128]
                 out_ref[pl.ds(k * 9 + 3 * n + t, 128, stride=27), :] = piece
+        save(n).start()
         return carry
 
     lax.fori_loop(0, 3, body, 0)
+    for n in range(3):
+        save(n).wait()
 
 
 def fine_in(got):
     return pl.pallas_call(
         fine_in_kernel,
         out_shape=[
-            jax.ShapeDtypeStruct((NF, 1152), F32),
+            pltpu.HBM((NF, 1152), F32),
             jax.ShapeDtypeStruct((3456, 128), F32),
         ],
-        in_specs=[VMEM] * 3,
-        out_specs=[VMEM] * 2,
+        compiler_params=LIMIT,
+        in_specs=[VMEM, VMEM, HBM],
+        out_specs=[HBM, VMEM],
+        scratch_shapes=[
+            pltpu.VMEM((NF, 1152), F32),
+            pltpu.VMEM((NF, 1152), BF16),
+            pltpu.SemaphoreType.DMA((3,)),
+            pltpu.SemaphoreType.DMA((3,)),
+        ],
     )(got, jnp.asarray(LIFT_X2), jnp.asarray(HF2))
 
 
-def fine_slab_kernel(device_ref, got_ref, out_m_ref, back_m_ref, matrix_ref, out_ref, plane_ref):
+def fine_slab_kernel(
+    place_ref, got_ref, out_hbm, back_hbm, matrix_hbm, out_ref, plane_ref, out_m, back_m, matrix, sems
+):
+    out_copies = fetch_left(out_hbm, out_m, sems.at[0])
+    back_copies = fetch_left(back_hbm, back_m, sems.at[1])
+    copies = fetch_right(matrix_hbm, matrix, sems.at[2])
+    begin(out_copies + copies + back_copies)
     wz = squares(lax.broadcasted_iota(jnp.int32, (NF, NF), 0), NF, 1.0)
     wy = squares(lax.broadcasted_iota(jnp.int32, (NF, NF), 1), NF, 1.0)
 
@@ -332,13 +418,18 @@
             return carry
 
         lax.fori_loop(0, 3, unpack, 0)
-        mid = dot3(pair(out_m_ref), split(plane_ref[...]))
-        mid = dot3(split(mid), pair(matrix_ref))
-        kx = 128 * k + device_ref[0]
+
+        @pl.when(k == 0)
+        def _():
+            finish(out_copies + copies + back_copies)
+
+        mid = dot(out_m[...], right3(plane_ref[...]))
+        mid = dot(left3(mid), matrix[...])
+        kx = 128 * k + place_ref[4]
         wx = squares(jnp.full((1, 1), kx, jnp.int32), NF, 1.0)
         mid = mid * dipolar(wx, wy, wz, NF)
-        mid = dot3(split(mid), pair(matrix_ref))
-        plane_ref[...] = dot3(pair(back_m_ref), split(mid))
+        mid = dot(left3(mid), matrix[...])
+        plane_ref[...] = dot(back_m[...], right3(mid))
 
         def pack(g, carry):
             base = k * 9 + g * 3
@@ -356,14 +447,21 @@
     lax.fori_loop(0, 3, body, 0)
 
 
-def fine_slab(device, got):
+def fine_slab(place, got):
     return pl.pallas_call(
         fine_slab_kernel,
         out_shape=jax.ShapeDtypeStruct((3456, 128), F32),
-        in_specs=[SMEM] + [VMEM] * 4,
+        compiler_params=LIMIT,
+        in_specs=[SMEM, VMEM] + [HBM] * 3,
         out_specs=VMEM,
-        scratch_shapes=[pltpu.VMEM((NF, NF), F32)],
-    )(device, got, jnp.asarray(HF_OUT2), jnp.asarray(HF_BACK2), jnp.asarray(HF2))
+        scratch_shapes=[
+            pltpu.VMEM((NF, NF), F32),
+            pltpu.VMEM((NF, 1152), BF16),
+            pltpu.VMEM((NF, 1152), BF16),
+            pltpu.VMEM((1152, NF), BF16),
+            pltpu.SemaphoreType.DMA((3, 3)),
+        ],
+    )(place, got, jnp.asarray(HF_OUT2), jnp.asarray(HF_BACK2), jnp.asarray(HF2))
 
 
 def fine_out_kernel(got_ref, evolved_ref, potential_ref, matrix_ref, damped_ref, part_ref):
@@ -392,47 +490,92 @@
         fine_out_kernel,
         out_shape=[
             jax.ShapeDtypeStruct((1152, NF), F32),
-            jax.ShapeDtypeStruct((8, 128), F32),
+            jax.ShapeDtypeStruct((128, 128), F32),
         ],
+        compiler_params=LIMIT,
         in_specs=[VMEM] * 4,
         out_specs=[VMEM] * 2,
     )(got, evolved, potential, jnp.asarray(HF2))
 
 
+def scale_kernel(parts_ref, damped_ref, out_hbm, scaled_ref, sems):
+    total = jnp.sum(parts_ref[...], axis=0, keepdims=True)
+    scale = lax.rsqrt(total / float(NF) ** 3 + EPSILON)
+    scale = jnp.concatenate([scale] * 3, axis=1)
+    copies = []
+    for i in range(4):
+        rows = pl.ds(288 * i, 288)
+        copies.append(pltpu.make_async_copy(scaled_ref.at[rows], out_hbm.at[rows], sems.at[i]))
+        scaled_ref[rows, :] = damped_ref[rows, :] * scale
+        if i:
+            copies[i - 1].start()
+    copies[3].start()
+    finish(copies)
+
+
+def scaled(parts, damped):
+    return pl.pallas_call(
+        scale_kernel,
+        out_shape=jax.ShapeDtypeStruct((1152, NF), F32),
+        compiler_params=LIMIT,
+        in_specs=[VMEM] * 2,
+        out_specs=HBM,
+        scratch_shapes=[pltpu.VMEM((1152, NF), F32), pltpu.SemaphoreType.DMA((4,))],
+    )(parts, damped)
+
+
 def exchange(buffer, axes, count):
     flat = buffer.reshape(count, 1, -1)
     return lax.all_to_all(flat, axes, split_axis=0, concat_axis=0, tiled=False)
 
 
-def move_potential(potential, core):
+def pair_planes(potential, core):
     other = lax.ppermute(potential, CORE, [(0, 1), (1, 0)])
     low = jnp.where(core == 0, potential, other)
     high = jnp.where(core == 0, other, potential)
-    both = jnp.concatenate([low, high], axis=0).reshape(8, 72, NC)
-    return lax.all_to_all(both, COLS, split_axis=0, concat_axis=0, tiled=False)
+    return jnp.concatenate([low, high], axis=0).reshape(4, 2, 72, NC)
+
+
+def spread_planes(both):
+    across = lax.axis_index("cols_0")
+    slots = []
+    for i in range(4):
+        chunk = lax.dynamic_index_in_dim(both, (across + i) % 4, 0, keepdims=False)
+        if i:
+            chunk = lax.ppermute(chunk, "cols_0", [(s, (s + i) % 4) for s in range(4)])
+        slots.append(chunk)
+    return jnp.stack(slots, axis=1)
+
+
+def join_planes(slots):
+    near = lax.axis_index("cols_1")
+    mine = lax.dynamic_index_in_dim(slots, near, 0, keepdims=False)
+    theirs = lax.dynamic_index_in_dim(slots, 1 - near, 0, keepdims=False)
+    return jnp.concatenate([mine, lax.ppermute(theirs, "cols_1", [(0, 1), (1, 0)])], axis=0)
 
 
 def per_device(wave_coarse, potential_coarse, potential_fine):
     core = lax.axis_index(CORE)
     chip = lax.axis_index(CHIPS)
     device = lax.axis_index(ALL)
-    v_slab = move_potential(potential_coarse, core)
-
-    turned = coarse_pencil(wave_coarse.reshape(288, NC))
-    turned = coarse_z(exchange(turned, ALL, 128).reshape(896, 128))
-    turned = coarse_y(chip.reshape(1), exchange(turned, CHIPS, 64).reshape(1728, 128))
-    got = exchange(turned, CHIPS, 64).reshape(1728, 128)
-    turned = coarse_x(core.reshape(1), got, v_slab)
+    across, near = lax.axis_index("cols_0"), lax.axis_index("cols_1")
+    place = jnp.stack([core, across, near, chip, device])
+
+    got = exchange(coarse_pencil(wave_coarse.reshape(288, NC)), ALL, 128).reshape(896, 128)
+    got, planes = lax.optimization_barrier((got, pair_planes(potential_coarse, core)))
+    got = exchange(coarse_z(got), CHIPS, 64).reshape(1728, 128)
+    got, planes = lax.optimization_barrier((got, spread_planes(planes)))
+    got = exchange(coarse_y(place, got), CHIPS, 64).reshape(1728, 128)
+    turned = coarse_x(place, got, join_planes(planes))
     got = exchange(turned, CHIPS, 64).reshape(1792, 128)
 
     evolved, spectrum = fine_in(got)
     got = exchange(spectrum, ALL, 128).reshape(3456, 128)
-    spectrum = fine_slab(device.reshape(1), got)
+    spectrum = fine_slab(place, got)
     got = exchange(spectrum, ALL, 128).reshape(3456, 128)
     damped, part = fine_out(got, evolved, potential_fine.reshape(1152, NF))
-    parts = exchange(jnp.broadcast_to(part[:1], (128, 128)), ALL, 128).reshape(128, 128)
-    total = jnp.sum(parts[:, 0])
-    return (damped * lax.rsqrt(total / float(NF) ** 3 + EPSILON)).reshape(48, 24, NF)
+    parts = exchange(part, ALL, 128).reshape(128, 128)
+    return scaled(parts, damped).reshape(48, 24, NF)
 
 
 def solution(mesh):

time: 226 us -> 212 us (0.938)
  Pallas kernels: 46.5 us -> 32.8 us
  starting transfers between devices: 17.6 us -> 29.4 us
  blocking collectives: 109 us -> 103 us
  other arithmetic: 4.32 us -> 0.16 us
    ppermute x1 -> x5, waiting for transfers between devices: 1.21 us -> 30.7 us  [the longest x3 15.6 us: spread_planes(): chunk = lax.ppermute(chunk, 'cols_0', [(s, (s + i) % 4) for s in range(4)])]
    all_to_all x2 -> x3, waiting for transfers between devices: 39.5 us -> 12.8 us  [exchange(): return lax.all_to_all(flat, axes, split_axis=0, concat_axis=0, tiled=False)]
    all_to_all x2 -> x3, starting transfers between devices: 13.5 us -> 23.5 us  [exchange(): return lax.all_to_all(flat, axes, split_axis=0, concat_axis=0, tiled=False)]
    all_to_all x5 -> x4, blocking collectives: 109 us -> 103 us  [exchange(): return lax.all_to_all(flat, axes, split_axis=0, concat_axis=0, tiled=False)]
    ppermute x1 -> x5, starting transfers between devices: 0.56 us -> 5.92 us  [the longest x3 3.45 us: spread_planes(): chunk = lax.ppermute(chunk, 'cols_0', [(s, (s + i) % 4) for s in range(4)])]
    all_to_all x1 -> x0, waiting for transfers between devices: 4.26 us -> none  [move_potential(): return lax.all_to_all(both, COLS, split_axis=0, concat_axis=0, tiled=False)]
    pallas_call x1, Pallas kernels: 6.98 us -> 3.08 us  [fine_out(): pl.pallas_call(fine_out_kernel, out_shape=[jax.ShapeDtypeStruct((1152, NF...]
    pallas_call x1, Pallas kernels: 16.7 us -> 12.8 us  [fine_slab(): pl.pallas_call(fine_slab_kernel, out_shape=jax.ShapeDtypeStruct((3456, 12...]
  transfers between devices with their start and end apart: 4 -> 8, of which waited for: 4 -> 5; matrix products, arithmetic and copies ran while one was open for 0% -> 0% of each run, Pallas kernels for 2% -> 1%
where the time goes in v3:
time: 212 us; the launch traced here: 211 us
  blocking collectives  103 us (49%)
  waiting for transfers between devices  43.5 us (21%)
  Pallas kernels  32.8 us (15%)
  starting transfers between devices  29.4 us (14%)
  local copies, waits for them, and re-layouts  2.14 us (1%)
    all_to_all x4, blocking collectives, exchange(): return lax.all_to_all(flat, axes, split_axis=0, concat_axis=0, tiled=False)  103 us
    all_to_all x3, starting transfers between devices, exchange(): return lax.all_to_all(flat, axes, split_axis=0, concat_axis=0, tiled=False)  23.5 us
    ppermute x3, waiting for transfers between devices, spread_planes(): chunk = lax.ppermute(chunk, 'cols_0', [(s, (s + i) % 4) for s in range(4)])  15.6 us
    ppermute x1, waiting for transfers between devices, join_planes(): lax.ppermute(theirs, 'cols_1', [(0, 1), (1, 0)])  15.1 us
    pallas_call x1, Pallas kernels, fine_slab(): pl.pallas_call(fine_slab_kernel, out_shape=jax.ShapeDtypeStruct((3456, 12...  12.8 us
    all_to_all x3, waiting for transfers between devices, exchange(): return lax.all_to_all(flat, axes, split_axis=0, concat_axis=0, tiled=False)  12.8 us
  transfers between devices with their start and end apart: 8, of which 5 were waited for; matrix products, arithmetic and copies ran while one was open for 0% of the time, Pallas kernels for 1%

profile of v3, /device:TPU:1, one launch (start us, length us, event | category | flops | bytes accessed | tf_op | source)
XLA Modules:
  0.0 211.2 jit_solution(12069694172975277548)
XLA Ops:
  0.0 1.4 collective-permute-start
  1.4 1.0 copy-done.9
  3.3 1.7 shard_map.136
  5.0 10.2 %all-to-all-start = ((f32[128,1,896]{2,1,0:T(1,128)}), f32[128,1,896]{2,1,0:T(1,128)S(1)}, u32[]{:S(2)}, u32[]{:S(2)}) async-start(f32[128,1,896]{2,1,0:T(1,128)} %bitcast.6), calls=%async_computation | async-start | bytes 917504 | tf_op jit(solution)/shard_map/all_to_all | solution.py:529
  15.3 12.8 %all-to-all-done = f32[128,1,896]{2,1,0:T(1,128)S(1)} async-done(((f32[128,1,896]{2,1,0:T(1,128)}), f32[128,1,896]{2,1,0:T(1,128)S(1)}, u32[]{:S(2)}, u32[]{:S(2)}) %all-to-all-start) | async-done | bytes 458784 | tf_op jit(solution)/shard_map/all_to_all | solution.py:529
  28.1 3.3 %shard_map.137 = f32[1728,128]{1,0:T(8,128)} custom-call(f32[896,128]{1,0:T(8,128)S(1)} %bitcast.47, bf16[2,192,256]{2,1,0:T(8,128)(2,1)S(1)} %copy-done.13, bf16[2,192,384]{2,1,0:T(8,128)(2,1)S(1)} %copy-done.10, bf16[2,192,192]{2,1,0:T(8,128)(2,1)S(1)} %copy-done.3), custom_call_target="tpu_custom_call" | custom-call | tf_op jit(solution)/shard_map/pallas_call | solution.py:246
  31.4 5.3 %all-to-all-start.1 = ((f32[64,1,3456]{2,1,0:T(1,128)}), f32[64,1,3456]{2,1,0:T(1,128)S(1)}, u32[]{:S(2)}, u32[]{:S(2)}) async-start(f32[64,1,3456]{2,1,0:T(1,128)} %bitcast.9), calls=%async_computation.1 | async-start | bytes 1769472 | tf_op jit(solution)/shard_map/all_to_all | solution.py:529
  36.8 2.3 %collective-permute-start.3 = (f32[2,72,192]{2,1,0:T(8,128)S(1)}, f32[2,72,192]{2,1,0:T(8,128)S(1)}, u32[]{:S(2)}, u32[]{:S(2)}) collective-permute-start(f32[2,72,192]{2,1,0:T(8,128)S(1)} %get-tuple-element.24), channel_id=1, source_target_pairs={{0,6},{2,0},{4,2},{6,4},{1,7},{3,1},{5,3},{7,5},{8,14},{10,8},{12,... | collective-permute-start | bytes 331784 | tf_op jit(solution)/shard_map/ppermute | solution.py:545
  40.4 9.9 %collective-permute-done.3 = f32[2,72,192]{2,1,0:T(8,128)S(1)} collective-permute-done((f32[2,72,192]{2,1,0:T(8,128)S(1)}, f32[2,72,192]{2,1,0:T(8,128)S(1)}, u32[]{:S(2)}, u32[]{:S(2)}) %collective-permute-start.3) | collective-permute-done | bytes 110624 | tf_op jit(solution)/shard_map/ppermute | solution.py:545
  50.3 2.6 %collective-permute-done.2 = f32[2,72,192]{2,1,0:T(8,128)S(1)} collective-permute-done((f32[2,72,192]{2,1,0:T(8,128)S(1)}, f32[2,72,192]{2,1,0:T(8,128)S(1)}, u32[]{:S(2)}, u32[]{:S(2)}) %collective-permute-start.2) | collective-permute-done | bytes 110624 | tf_op jit(solution)/shard_map/ppermute | solution.py:545
  52.9 3.1 %collective-permute-done.1 = f32[2,72,192]{2,1,0:T(8,128)S(1)} collective-permute-done((f32[2,72,192]{2,1,0:T(8,128)S(1)}, f32[2,72,192]{2,1,0:T(8,128)S(1)}, u32[]{:S(2)}, u32[]{:S(2)}) %collective-permute-start.1) | collective-permute-done | bytes 110624 | tf_op jit(solution)/shard_map/ppermute | solution.py:545
  56.0 3.9 %shard_map.138 = f32[1728,128]{1,0:T(8,128)} custom-call(s32[5]{0:T(128)S(1)} %stack.38.place_ref, f32[1728,128]{1,0:T(8,128)S(1)} %bitcast.45, bf16[2,192,192]{2,1,0:T(8,128)(2,1)S(1)} %copy-done.3, bf16[2,256,256]{2,1,0:T(8,128)(2,1)S(1)} %copy-done.11), custom_call_target="tpu_custom_call" | custom-call | tf_op jit(solution)/shard_map/pallas_call | solution.py:284
  59.9 7.9 %all-to-all-start.2 = ((f32[64,1,3456]{2,1,0:T(1,128)}), f32[64,1,3456]{2,1,0:T(1,128)S(1)}, u32[]{:S(2)}, u32[]{:S(2)}) async-start(f32[64,1,3456]{2,1,0:T(1,128)} %bitcast.18), calls=%async_computation.2 | async-start | bytes 1769472 | tf_op jit(solution)/shard_map/all_to_all | solution.py:529
  67.9 1.1 collective-permute-start.4
  69.0 15.1 %collective-permute-done.4 = f32[4,72,192]{2,1,0:T(8,128)S(1)} collective-permute-done((f32[4,72,192]{2,1,0:T(8,128)S(1)}, f32[4,72,192]{2,1,0:T(8,128)S(1)}, u32[]{:S(2)}, u32[]{:S(2)}) %collective-permute-start.4) | collective-permute-done | bytes 221216 | tf_op jit(solution)/shard_map/ppermute | solution.py:554
  84.2 3.2 %shard_map.139 = f32[1792,128]{1,0:T(8,128)S(1)} custom-call(s32[5]{0:T(128)S(1)} %stack.38.place_ref, f32[1728,128]{1,0:T(8,128)S(1)} %bitcast.46, f32[8,72,192]{2,1,0:T(8,128)S(1)} %pad_maximum_fusion.2.potential_ref, bf16[2,192,192]{2,1,0:T(8,128)(2,1)S(1)} %copy-done.3, bf16[2,384,192]{2,1,0:T(8,128)(2,1)S(1)} %copy-done.8, ...), custom_call_target="tpu_custom_call" | custom-call | tf_op jit(solution)/shard_map/pallas_call | solution.py:333
  87.4 23.8 %all_to_all.35 = f32[64,1,3584]{2,1,0:T(1,128)S(1)} all-to-all(f32[64,1,3584]{2,1,0:T(1,128)S(1)} %bitcast.43), channel_id=1, replica_groups=mesh['rows_0'=4,'rows_1'=2,'rows_2'=2,'cols_0'=4,'cols_1'=2] {'rows_0','..., dimensions={0} | all-to-all | bytes 1835008 | tf_op jit(solution)/shard_map/all_to_all | solution.py:529
  111.2 3.6 %shard_map.140 = (f32[384,1152]{1,0:T(8,128)}, f32[3456,128]{1,0:T(8,128)S(1)}) custom-call(f32[1792,128]{1,0:T(8,128)S(1)} %bitcast.44, bf16[2,384,192]{2,1,0:T(8,128)(2,1)S(1)} %copy-done.6, bf16[2,384,384]{2,1,0:T(8,128)(2,1)S(1)} %copy-done), custom_call_target="tpu_custom_call" | custom-call | tf_op jit(solution)/shard_map/pallas_call | solution.py:381
  114.8 33.6 %all_to_all.36 = f32[128,1,3456]{2,1,0:T(1,128)S(1)} all-to-all(f32[128,1,3456]{2,1,0:T(1,128)S(1)} %bitcast.49), channel_id=1, replica_groups=mesh['rows_0'=4,'rows_1'=2,'rows_2'=2,'cols_0'=4,'cols_1'=2] {'rows_0','..., dimensions={0} | all-to-all | bytes 3538944 | tf_op jit(solution)/shard_map/all_to_all | solution.py:529
  148.5 12.8 %shard_map.141 = f32[3456,128]{1,0:T(8,128)S(1)} custom-call(s32[5]{0:T(128)S(1)} %stack.38.place_ref, f32[3456,128]{1,0:T(8,128)S(1)} %bitcast.41, bf16[2,384,384]{2,1,0:T(8,128)(2,1)S(1)} %copy-done.5, bf16[2,384,384]{2,1,0:T(8,128)(2,1)S(1)} %copy-done.4, bf16[2,384,384]{2,1,0:T(8,128)(2,1)S(1)} %copy-done), custom_call_target="tpu_custom_call" | custom-call | tf_op jit(solution)/shard_map/pallas_call | solution.py:451
  161.3 31.1 %all_to_all.37 = f32[128,1,3456]{2,1,0:T(1,128)S(1)} all-to-all(f32[128,1,3456]{2,1,0:T(1,128)S(1)} %bitcast.42), channel_id=1, replica_groups=mesh['rows_0'=4,'rows_1'=2,'rows_2'=2,'cols_0'=4,'cols_1'=2] {'rows_0','..., dimensions={0} | all-to-all | bytes 3538944 | tf_op jit(solution)/shard_map/all_to_all | solution.py:529
  192.4 3.1 %shard_map.142 = (f32[1152,384]{1,0:T(8,128)S(1)}, f32[128,128]{1,0:T(8,128)S(1)}) custom-call(f32[3456,128]{1,0:T(8,128)S(1)} %bitcast.40, f32[384,1152]{1,0:T(8,128)S(1)} %copy-done.2, f32[1152,384]{1,0:T(8,128)S(1)} %bitcast.48, bf16[2,384,384]{2,1,0:T(8,128)(2,1)S(1)} %copy-done), custom_call_target="tpu_custom_call" | custom-call | tf_op jit(solution)/shard_map/pallas_call | solution.py:489
  195.5 14.2 %all_to_all.38 = f32[128,1,128]{2,1,0:T(1,128)S(1)} all-to-all(f32[128,1,128]{2,1,0:T(1,128)S(1)} %bitcast.52), channel_id=1, replica_groups=mesh['rows_0'=4,'rows_1'=2,'rows_2'=2,'cols_0'=4,'cols_1'=2] {'rows_0','..., dimensions={0} | all-to-all | bytes 131072 | tf_op jit(solution)/shard_map/all_to_all | solution.py:529
  209.7 1.3 shard_map.143
  (41 shorter events, 2.5 us)
Async XLA Ops:
  0.0 15.2 %collective-permute-start = (f32[12,24,192]{2,1,0:T(8,128)}, f32[12,24,192]{2,1,0:T(8,128)S(1)}, u32[]{:S(2)}, u32[]{:S(2)}) collective-permute-start(f32[12,24,192]{2,1,0:T(8,128)} %param.15), channel_id=1, source_target_pairs={{0,8},{8,0},{1,9},{9,1},{2,10},{10,2},{3,11},{11,3},{4,12},{12,4},... | collective-permute-start | bytes 663560 | tf_op jit(solution)/shard_map/ppermute | solution.py:533
  1.4 1.0 copy-start.9
  2.3 0.9 copy-start.12
  3.3 12.0 %copy-start.14 = (f32[12,24,192]{2,1,0:T(8,128)S(1)}, f32[12,24,192]{2,1,0:T(8,128)}, u32[]{:S(2)}) copy-start(f32[12,24,192]{2,1,0:T(8,128)} %param.15) | copy-start | bytes 663556
  4.9 23.2 %copy-start.3 = (bf16[2,192,192]{2,1,0:T(8,128)(2,1)S(1)}, bf16[2,192,192]{2,1,0:T(8,128)(2,1)}, u32[]{:S(2)}) copy-start(bf16[2,192,192]{2,1,0:T(8,128)(2,1)} %constant.98.clone.matrix_ref) | copy-start | bytes 442372
  5.0 23.2 %copy-start.10 = (bf16[2,192,384]{2,1,0:T(8,128)(2,1)S(1)}, bf16[2,192,384]{2,1,0:T(8,128)(2,1)}, u32[]{:S(2)}) copy-start(bf16[2,192,384]{2,1,0:T(8,128)(2,1)} %constant.97.clone.ex_ref) | copy-start | bytes 884740
  5.0 23.1 %copy-start.13 = (bf16[2,192,256]{2,1,0:T(8,128)(2,1)S(1)}, bf16[2,192,256]{2,1,0:T(8,128)(2,1)}, u32[]{:S(2)}) copy-start(bf16[2,192,256]{2,1,0:T(8,128)(2,1)} %constant.96.clone.ey_ref) | copy-start | bytes 589828
  5.0 23.1 %all-to-all-start = ((f32[128,1,896]{2,1,0:T(1,128)}), f32[128,1,896]{2,1,0:T(1,128)S(1)}, u32[]{:S(2)}, u32[]{:S(2)}) async-start(f32[128,1,896]{2,1,0:T(1,128)} %bitcast.6), calls=%async_computation | async-start | bytes 917504 | tf_op jit(solution)/shard_map/all_to_all | solution.py:529
  31.4 24.6 %copy-start.11 = (bf16[2,256,256]{2,1,0:T(8,128)(2,1)S(1)}, bf16[2,256,256]{2,1,0:T(8,128)(2,1)}, u32[]{:S(2)}) copy-start(bf16[2,256,256]{2,1,0:T(8,128)(2,1)} %constant.99.clone.wide_ref) | copy-start | bytes 786436
  31.4 24.6 %all-to-all-start.1 = ((f32[64,1,3456]{2,1,0:T(1,128)}), f32[64,1,3456]{2,1,0:T(1,128)S(1)}, u32[]{:S(2)}, u32[]{:S(2)}) async-start(f32[64,1,3456]{2,1,0:T(1,128)} %bitcast.9), calls=%async_computation.1 | async-start | bytes 1769472 | tf_op jit(solution)/shard_map/all_to_all | solution.py:529
  36.8 13.4 %collective-permute-start.3 = (f32[2,72,192]{2,1,0:T(8,128)S(1)}, f32[2,72,192]{2,1,0:T(8,128)S(1)}, u32[]{:S(2)}, u32[]{:S(2)}) collective-permute-start(f32[2,72,192]{2,1,0:T(8,128)S(1)} %get-tuple-element.24), channel_id=1, source_target_pairs={{0,6},{2,0},{4,2},{6,4},{1,7},{3,1},{5,3},{7,5},{8,14},{10,8},{12,... | collective-permute-start | bytes 331784 | tf_op jit(solution)/shard_map/ppermute | solution.py:545
  39.1 13.8 %collective-permute-start.2 = (f32[2,72,192]{2,1,0:T(8,128)S(1)}, f32[2,72,192]{2,1,0:T(8,128)S(1)}, u32[]{:S(2)}, u32[]{:S(2)}) collective-permute-start(f32[2,72,192]{2,1,0:T(8,128)S(1)} %get-tuple-element.25), channel_id=1, source_target_pairs={{0,4},{2,6},{4,0},{6,2},{1,5},{3,7},{5,1},{7,3},{8,12},{10,14},{12... | collective-permute-start | bytes 331784 | tf_op jit(solution)/shard_map/ppermute | solution.py:545
  39.7 16.3 %collective-permute-start.1 = (f32[2,72,192]{2,1,0:T(8,128)S(1)}, f32[2,72,192]{2,1,0:T(8,128)S(1)}, u32[]{:S(2)}, u32[]{:S(2)}) collective-permute-start(f32[2,72,192]{2,1,0:T(8,128)S(1)} %get-tuple-element.26), channel_id=1, source_target_pairs={{0,2},{2,4},{4,6},{6,0},{1,3},{3,5},{5,7},{7,1},{8,10},{10,12},{12... | collective-permute-start | bytes 331784 | tf_op jit(solution)/shard_map/ppermute | solution.py:545
  59.9 24.3 %copy-start.7 = (bf16[2,2,192,256]{3,2,1,0:T(8,128)(2,1)S(1)}, bf16[2,2,192,256]{3,2,1,0:T(8,128)(2,1)}, u32[]{:S(2)}) copy-start(bf16[2,2,192,256]{3,2,1,0:T(8,128)(2,1)} %constant.101.clone.ly_ref) | copy-start | bytes 1179652
  59.9 24.3 %copy-start.8 = (bf16[2,384,192]{2,1,0:T(8,128)(2,1)S(1)}, bf16[2,384,192]{2,1,0:T(8,128)(2,1)}, u32[]{:S(2)}) copy-start(bf16[2,384,192]{2,1,0:T(8,128)(2,1)} %constant.100.clone.lz_ref) | copy-start | bytes 884740
  59.9 24.3 %all-to-all-start.2 = ((f32[64,1,3456]{2,1,0:T(1,128)}), f32[64,1,3456]{2,1,0:T(1,128)S(1)}, u32[]{:S(2)}, u32[]{:S(2)}) async-start(f32[64,1,3456]{2,1,0:T(1,128)} %bitcast.18), calls=%async_computation.2 | async-start | bytes 1769472 | tf_op jit(solution)/shard_map/all_to_all | solution.py:529
  67.9 16.2 %collective-permute-start.4 = (f32[4,72,192]{2,1,0:T(8,128)S(1)}, f32[4,72,192]{2,1,0:T(8,128)S(1)}, u32[]{:S(2)}, u32[]{:S(2)}) collective-permute-start(f32[4,72,192]{2,1,0:T(8,128)S(1)} %get-tuple-element.22), channel_id=1, source_target_pairs={{0,1},{1,0},{2,3},{3,2},{4,5},{5,4},{6,7},{7,6},{8,9},{9,8},{10,11... | collective-permute-start | bytes 663560 | tf_op jit(solution)/shard_map/ppermute | solution.py:554
  84.2 27.0 %copy-start = (bf16[2,384,384]{2,1,0:T(8,128)(2,1)S(1)}, bf16[2,384,384]{2,1,0:T(8,128)(2,1)}, u32[]{:S(2)}) copy-start(bf16[2,384,384]{2,1,0:T(8,128)(2,1)} %constant.103.clone.matrix_hbm.matrix_ref) | copy-start | bytes 1769476
  84.2 27.0 %copy-start.6 = (bf16[2,384,192]{2,1,0:T(8,128)(2,1)S(1)}, bf16[2,384,192]{2,1,0:T(8,128)(2,1)}, u32[]{:S(2)}) copy-start(bf16[2,384,192]{2,1,0:T(8,128)(2,1)} %constant.102.clone.lift_ref) | copy-start | bytes 884740
  114.8 33.6 %copy-start.4 = (bf16[2,384,384]{2,1,0:T(8,128)(2,1)S(1)}, bf16[2,384,384]{2,1,0:T(8,128)(2,1)}, u32[]{:S(2)}) copy-start(bf16[2,384,384]{2,1,0:T(8,128)(2,1)} %constant.105.clone.back_hbm) | copy-start | bytes 1769476
  114.8 33.6 %copy-start.5 = (bf16[2,384,384]{2,1,0:T(8,128)(2,1)S(1)}, bf16[2,384,384]{2,1,0:T(8,128)(2,1)}, u32[]{:S(2)}) copy-start(bf16[2,384,384]{2,1,0:T(8,128)(2,1)} %constant.104.clone.out_hbm) | copy-start | bytes 1769476
  161.3 31.2 %copy-start.1 = (f32[48,24,384]{2,1,0:T(8,128)S(1)}, f32[48,24,384]{2,1,0:T(8,128)}, u32[]{:S(2)}) copy-start(f32[48,24,384]{2,1,0:T(8,128)} %param.16) | copy-start | bytes 5308420
  161.3 31.1 %copy-start.2 = (f32[384,1152]{1,0:T(8,128)S(1)}, f32[384,1152]{1,0:T(8,128)}, u32[]{:S(2)}) copy-start(f32[384,1152]{1,0:T(8,128)} %get-tuple-element.18.evolved_ref) | copy-start | bytes 5308420

commit v4 on v3

--- a/solution.py
+++ b/solution.py
@@ -180,6 +180,10 @@
     return result
 
 
+def in_hbm(x):
+    return pltpu.with_memory_space_constraint(x, pltpu.HBM)
+
+
 def coarse_pencil_kernel(wave_hbm, matrix_hbm, out_ref, wave_ref, matrix_ref, sems):
     copies = [
         pltpu.make_async_copy(wave_hbm, wave_ref, sems.at[0]),
@@ -218,7 +222,7 @@
             pltpu.VMEM((2, NC, NC), BF16),
             pltpu.SemaphoreType.DMA((2,)),
         ],
-    )(wave, jnp.asarray(EVOLVE2))
+    )(in_hbm(wave), in_hbm(jnp.asarray(EVOLVE2)))
 
 
 def coarse_z_kernel(got_ref, ey_ref, ex_ref, matrix_ref, out_ref, plane_ref):
@@ -295,7 +299,7 @@
     core = place_ref[0]
     slots = []
     for c in range(8):
-        slots.append(lax.rem(place_ref[1] - c // 2 + 4, 4) + 4 * (place_ref[2] ^ (c % 2)))
+        slots.append(2 * lax.rem(place_ref[1] - c // 2 + 4, 4) + (place_ref[2] ^ (c % 2)))
     lift_y = (ly_ref[core, 0], ly_ref[core, 1])
     part = jnp.zeros((1, 1), F32)
     blank = jnp.zeros((8, 128), F32)
@@ -529,29 +533,28 @@
     return lax.all_to_all(flat, axes, split_axis=0, concat_axis=0, tiled=False)
 
 
-def pair_planes(potential, core):
-    other = lax.ppermute(potential, CORE, [(0, 1), (1, 0)])
-    low = jnp.where(core == 0, potential, other)
-    high = jnp.where(core == 0, other, potential)
-    return jnp.concatenate([low, high], axis=0).reshape(4, 2, 72, NC)
-
-
-def spread_planes(both):
-    across = lax.axis_index("cols_0")
+def swap_planes(potential, near):
+    planes = potential.reshape(2, 2, 72, NC)
+    mine = lax.dynamic_index_in_dim(planes, near, 1, keepdims=False)
+    theirs = lax.dynamic_index_in_dim(planes, 1 - near, 1, keepdims=False)
+    return jnp.stack([mine, lax.ppermute(theirs, "cols_1", [(0, 1), (1, 0)])], axis=1)
+
+
+def spread_planes(planes, across):
     slots = []
     for i in range(4):
-        chunk = lax.dynamic_index_in_dim(both, (across + i) % 4, 0, keepdims=False)
+        chunk = lax.dynamic_index_in_dim(planes, (across + i) % 2, 0, keepdims=False)
         if i:
-            chunk = lax.ppermute(chunk, "cols_0", [(s, (s + i) % 4) for s in range(4)])
+            moves = [(c * 4 + (y - i) % 4, c * 4 + y) for c in range(2) for y in (2 * c, 2 * c + 1)]
+            chunk = lax.ppermute(chunk, (CORE, "cols_0"), moves)
         slots.append(chunk)
-    return jnp.stack(slots, axis=1)
-
-
-def join_planes(slots):
-    near = lax.axis_index("cols_1")
-    mine = lax.dynamic_index_in_dim(slots, near, 0, keepdims=False)
-    theirs = lax.dynamic_index_in_dim(slots, 1 - near, 0, keepdims=False)
-    return jnp.concatenate([mine, lax.ppermute(theirs, "cols_1", [(0, 1), (1, 0)])], axis=0)
+    return jnp.stack(slots)
+
+
+def share_planes(slots, core, across):
+    moves = [(y // 2 * 4 + y, (1 - y // 2) * 4 + y) for y in range(4)]
+    other = lax.ppermute(slots, (CORE, "cols_0"), moves)
+    return jnp.where(core == across // 2, slots, other).reshape(8, 72, NC)
 
 
 def per_device(wave_coarse, potential_coarse, potential_fine):
@@ -562,11 +565,11 @@
     place = jnp.stack([core, across, near, chip, device])
 
     got = exchange(coarse_pencil(wave_coarse.reshape(288, NC)), ALL, 128).reshape(896, 128)
-    got, planes = lax.optimization_barrier((got, pair_planes(potential_coarse, core)))
+    got, planes = lax.optimization_barrier((got, swap_planes(potential_coarse, near)))
     got = exchange(coarse_z(got), CHIPS, 64).reshape(1728, 128)
-    got, planes = lax.optimization_barrier((got, spread_planes(planes)))
+    got, planes = lax.optimization_barrier((got, spread_planes(planes, across)))
     got = exchange(coarse_y(place, got), CHIPS, 64).reshape(1728, 128)
-    turned = coarse_x(place, got, join_planes(planes))
+    turned = coarse_x(place, got, share_planes(planes, core, across))
     got = exchange(turned, CHIPS, 64).reshape(1792, 128)
 
     evolved, spectrum = fine_in(got)

time: 212 us -> 203 us (0.958)
  waiting for transfers between devices: 43.5 us -> 32.9 us
  starting transfers between devices: 29.4 us -> 35.9 us
  blocking collectives: 103 us -> 98.2 us
    ppermute x5, waiting for transfers between devices: 30.7 us -> 16.9 us  [the longest x1 7.94 us: swap_planes(): lax.ppermute(theirs, 'cols_1', [(0, 1), (1, 0)])]
    all_to_all x4, blocking collectives: 103 us -> 98.2 us  [exchange(): return lax.all_to_all(flat, axes, split_axis=0, concat_axis=0, tiled=False)]
    all_to_all x3, starting transfers between devices: 23.5 us -> 26.8 us  [exchange(): return lax.all_to_all(flat, axes, split_axis=0, concat_axis=0, tiled=False)]
    all_to_all x3, waiting for transfers between devices: 12.8 us -> 16 us  [exchange(): return lax.all_to_all(flat, axes, split_axis=0, concat_axis=0, tiled=False)]
    ppermute x5, starting transfers between devices: 5.92 us -> 9.11 us  [the longest x3 6.39 us: spread_planes(): chunk = lax.ppermute(chunk, (CORE, 'cols_0'), moves)]
  transfers between devices with their start and end apart: 8 -> 8, of which waited for: 5 -> 6; matrix products, arithmetic and copies ran while one was open for 0% -> 1% of each run, Pallas kernels for 1% -> 0%
where the time goes in v4:
time: 203 us
  blocking collectives  98.2 us (48%)
  starting transfers between devices  35.9 us (18%)
  Pallas kernels  33.6 us (17%)
  waiting for transfers between devices  32.9 us (16%)
    all_to_all x4, blocking collectives, exchange(): return lax.all_to_all(flat, axes, split_axis=0, concat_axis=0, tiled=False)  98.2 us
    all_to_all x3, starting transfers between devices, exchange(): return lax.all_to_all(flat, axes, split_axis=0, concat_axis=0, tiled=False)  26.8 us
    all_to_all x3, waiting for transfers between devices, exchange(): return lax.all_to_all(flat, axes, split_axis=0, concat_axis=0, tiled=False)  16 us
    pallas_call x1, Pallas kernels, fine_slab(): pl.pallas_call(fine_slab_kernel, out_shape=jax.ShapeDtypeStruct((3456, 12...  12.8 us
    ppermute x1, waiting for transfers between devices, swap_planes(): lax.ppermute(theirs, 'cols_1', [(0, 1), (1, 0)])  7.94 us
    ppermute x3, starting transfers between devices, spread_planes(): chunk = lax.ppermute(chunk, (CORE, 'cols_0'), moves)  6.39 us
    ppermute x3, waiting for transfers between devices, spread_planes(): chunk = lax.ppermute(chunk, (CORE, 'cols_0'), moves)  6.24 us
  transfers between devices with their start and end apart: 8, of which 6 were waited for; matrix products, arithmetic and copies ran while one was open for 1% of the time, Pallas kernels for 0%

profile of v4, /device:TPU:1, one launch (start us, length us, event | category | flops | bytes accessed | tf_op | source)
XLA Modules:
  0.0 202.5 jit_solution(3975794264445351020)
XLA Ops:
  0.0 2.5 %shard_map.136 = f32[896,128]{1,0:T(8,128)} custom-call(f32[288,192]{1,0:T(8,128)} %bitcast.52, bf16[2,192,192]{2,1,0:T(8,128)(2,1)} %constant.103.clone.matrix_hbm), custom_call_target="tpu_custom_call" | custom-call | tf_op jit(solution)/shard_map/pallas_call | solution.py:214
  2.5 11.5 %all-to-all-start = ((f32[128,1,896]{2,1,0:T(1,128)}), f32[128,1,896]{2,1,0:T(1,128)S(1)}, u32[]{:S(2)}, u32[]{:S(2)}) async-start(f32[128,1,896]{2,1,0:T(1,128)} %bitcast.6), calls=%async_computation | async-start | bytes 917504 | tf_op jit(solution)/shard_map/all_to_all | solution.py:533
  14.0 1.4 collective-permute-start
  15.5 7.9 %collective-permute-done = f32[2,72,192]{2,1,0:T(8,128)S(1)} collective-permute-done((f32[2,72,192]{2,1,0:T(8,128)S(1)}, f32[2,72,192]{2,1,0:T(8,128)S(1)}, u32[]{:S(2)}, u32[]{:S(2)}) %collective-permute-start) | collective-permute-done | bytes 110624 | tf_op jit(solution)/shard_map/ppermute | solution.py:540
  23.4 3.5 %all-to-all-done = f32[128,1,896]{2,1,0:T(1,128)S(1)} async-done(((f32[128,1,896]{2,1,0:T(1,128)}), f32[128,1,896]{2,1,0:T(1,128)S(1)}, u32[]{:S(2)}, u32[]{:S(2)}) %all-to-all-start) | async-done | bytes 458784 | tf_op jit(solution)/shard_map/all_to_all | solution.py:533
  26.9 3.3 %shard_map.137 = f32[1728,128]{1,0:T(8,128)} custom-call(f32[896,128]{1,0:T(8,128)S(1)} %bitcast.46, bf16[2,192,256]{2,1,0:T(8,128)(2,1)S(1)} %copy-done.11, bf16[2,192,384]{2,1,0:T(8,128)(2,1)S(1)} %copy-done.9, bf16[2,192,192]{2,1,0:T(8,128)(2,1)S(1)} %copy-done.3), custom_call_target="tpu_custom_call" | custom-call | tf_op jit(solution)/shard_map/pallas_call | solution.py:250
  30.2 6.8 %all-to-all-start.1 = ((f32[64,1,3456]{2,1,0:T(1,128)}), f32[64,1,3456]{2,1,0:T(1,128)S(1)}, u32[]{:S(2)}, u32[]{:S(2)}) async-start(f32[64,1,3456]{2,1,0:T(1,128)} %bitcast.11), calls=%async_computation.1 | async-start | bytes 1769472 | tf_op jit(solution)/shard_map/all_to_all | solution.py:533
  37.1 4.1 %collective-permute-start.3 = (f32[2,72,192]{2,1,0:T(8,128)S(1)}, f32[2,72,192]{2,1,0:T(8,128)S(1)}, u32[]{:S(2)}, u32[]{:S(2)}) collective-permute-start(f32[2,72,192]{2,1,0:T(8,128)S(1)} %get-tuple-element.22), channel_id=1, source_target_pairs={{2,0},{4,2},{14,12},{8,14},{3,1},{5,3},{15,13},{9,15},{18,16},{20,... | collective-permute-start | bytes 331784 | tf_op jit(solution)/shard_map/ppermute | solution.py:549
  41.2 1.6 collective-permute-start.2
  43.6 6.2 %collective-permute-done.3 = f32[2,72,192]{2,1,0:T(8,128)S(1)} collective-permute-done((f32[2,72,192]{2,1,0:T(8,128)S(1)}, f32[2,72,192]{2,1,0:T(8,128)S(1)}, u32[]{:S(2)}, u32[]{:S(2)}) %collective-permute-start.3) | collective-permute-done | bytes 110624 | tf_op jit(solution)/shard_map/ppermute | solution.py:549
  49.9 2.3 %all-to-all-done.1 = f32[64,1,3456]{2,1,0:T(1,128)S(1)} async-done(((f32[64,1,3456]{2,1,0:T(1,128)}), f32[64,1,3456]{2,1,0:T(1,128)S(1)}, u32[]{:S(2)}, u32[]{:S(2)}) %all-to-all-start.1) | async-done | bytes 884768 | tf_op jit(solution)/shard_map/all_to_all | solution.py:533
  52.3 3.9 %shard_map.138 = f32[1728,128]{1,0:T(8,128)} custom-call(s32[5]{0:T(128)S(1)} %stack.43.place_ref, f32[1728,128]{1,0:T(8,128)S(1)} %bitcast.43, bf16[2,192,192]{2,1,0:T(8,128)(2,1)S(1)} %copy-done.3, bf16[2,256,256]{2,1,0:T(8,128)(2,1)S(1)} %copy-done.10), custom_call_target="tpu_custom_call" | custom-call | tf_op jit(solution)/shard_map/pallas_call | solution.py:288
  56.1 8.6 %all-to-all-start.2 = ((f32[64,1,3456]{2,1,0:T(1,128)}), f32[64,1,3456]{2,1,0:T(1,128)S(1)}, u32[]{:S(2)}, u32[]{:S(2)}) async-start(f32[64,1,3456]{2,1,0:T(1,128)} %bitcast.19), calls=%async_computation.2 | async-start | bytes 1769472 | tf_op jit(solution)/shard_map/all_to_all | solution.py:533
  66.0 2.7 %collective-permute-done.4 = f32[4,2,72,192]{3,2,1,0:T(8,128)} collective-permute-done((f32[4,2,72,192]{3,2,1,0:T(8,128)S(1)}, f32[4,2,72,192]{3,2,1,0:T(8,128)}, u32[]{:S(2)}, u32[]{:S(2)}) %collective-permute-start.4) | collective-permute-done | bytes 442400 | tf_op jit(solution)/shard_map/ppermute | solution.py:556
  69.9 10.2 %all-to-all-done.2 = f32[64,1,3456]{2,1,0:T(1,128)S(1)} async-done(((f32[64,1,3456]{2,1,0:T(1,128)}), f32[64,1,3456]{2,1,0:T(1,128)S(1)}, u32[]{:S(2)}, u32[]{:S(2)}) %all-to-all-start.2) | async-done | bytes 884768 | tf_op jit(solution)/shard_map/all_to_all | solution.py:533
  80.1 3.2 %shard_map.139 = f32[1792,128]{1,0:T(8,128)S(1)} custom-call(s32[5]{0:T(128)S(1)} %stack.43.place_ref, f32[1728,128]{1,0:T(8,128)S(1)} %bitcast.44, f32[8,72,192]{2,1,0:T(8,128)S(1)} %bitcast.45, bf16[2,192,192]{2,1,0:T(8,128)(2,1)S(1)} %copy-done.3, bf16[2,384,192]{2,1,0:T(8,128)(2,1)S(1)} %copy-done.8, bf16[2,2,192,256]{3,2,1,0:T(8,128)(2,1)S(1)} %copy-done.7), custom_call_target="tpu_custom_call" | custom-call | tf_op jit(solution)/shard_map/pallas_call | solution.py:337
  83.3 19.3 %all_to_all.35 = f32[64,1,3584]{2,1,0:T(1,128)S(1)} all-to-all(f32[64,1,3584]{2,1,0:T(1,128)S(1)} %bitcast.41), channel_id=1, replica_groups=mesh['rows_0'=4,'rows_1'=2,'rows_2'=2,'cols_0'=4,'cols_1'=2] {'rows_0','..., dimensions={0} | all-to-all | bytes 1835008 | tf_op jit(solution)/shard_map/all_to_all | solution.py:533
  102.5 3.6 %shard_map.140 = (f32[384,1152]{1,0:T(8,128)}, f32[3456,128]{1,0:T(8,128)S(1)}) custom-call(f32[1792,128]{1,0:T(8,128)S(1)} %bitcast.42, bf16[2,384,192]{2,1,0:T(8,128)(2,1)S(1)} %copy-done.6, bf16[2,384,384]{2,1,0:T(8,128)(2,1)S(1)} %copy-done), custom_call_target="tpu_custom_call" | custom-call | tf_op jit(solution)/shard_map/pallas_call | solution.py:385
  106.1 33.6 %all_to_all.36 = f32[128,1,3456]{2,1,0:T(1,128)S(1)} all-to-all(f32[128,1,3456]{2,1,0:T(1,128)S(1)} %bitcast.48), channel_id=1, replica_groups=mesh['rows_0'=4,'rows_1'=2,'rows_2'=2,'cols_0'=4,'cols_1'=2] {'rows_0','..., dimensions={0} | all-to-all | bytes 3538944 | tf_op jit(solution)/shard_map/all_to_all | solution.py:533
  139.8 12.8 %shard_map.141 = f32[3456,128]{1,0:T(8,128)S(1)} custom-call(s32[5]{0:T(128)S(1)} %stack.43.place_ref, f32[3456,128]{1,0:T(8,128)S(1)} %bitcast.39, bf16[2,384,384]{2,1,0:T(8,128)(2,1)S(1)} %copy-done.5, bf16[2,384,384]{2,1,0:T(8,128)(2,1)S(1)} %copy-done.4, bf16[2,384,384]{2,1,0:T(8,128)(2,1)S(1)} %copy-done), custom_call_target="tpu_custom_call" | custom-call | tf_op jit(solution)/shard_map/pallas_call | solution.py:455
  152.6 31.1 %all_to_all.37 = f32[128,1,3456]{2,1,0:T(1,128)S(1)} all-to-all(f32[128,1,3456]{2,1,0:T(1,128)S(1)} %bitcast.40), channel_id=1, replica_groups=mesh['rows_0'=4,'rows_1'=2,'rows_2'=2,'cols_0'=4,'cols_1'=2] {'rows_0','..., dimensions={0} | all-to-all | bytes 3538944 | tf_op jit(solution)/shard_map/all_to_all | solution.py:533
  183.7 3.1 %shard_map.142 = (f32[1152,384]{1,0:T(8,128)S(1)}, f32[128,128]{1,0:T(8,128)S(1)}) custom-call(f32[3456,128]{1,0:T(8,128)S(1)} %bitcast.38, f32[384,1152]{1,0:T(8,128)S(1)} %copy-done.2, f32[1152,384]{1,0:T(8,128)S(1)} %bitcast.47, bf16[2,384,384]{2,1,0:T(8,128)(2,1)S(1)} %copy-done), custom_call_target="tpu_custom_call" | custom-call | tf_op jit(solution)/shard_map/pallas_call | solution.py:493
  186.8 14.2 %all_to_all.38 = f32[128,1,128]{2,1,0:T(1,128)S(1)} all-to-all(f32[128,1,128]{2,1,0:T(1,128)S(1)} %bitcast.50), channel_id=1, replica_groups=mesh['rows_0'=4,'rows_1'=2,'rows_2'=2,'cols_0'=4,'cols_1'=2] {'rows_0','..., dimensions={0} | all-to-all | bytes 131072 | tf_op jit(solution)/shard_map/all_to_all | solution.py:533
  201.0 1.3 shard_map.143
  (36 shorter events, 3.4 us)
Async XLA Ops:
  0.0 26.9 %copy-start.3 = (bf16[2,192,192]{2,1,0:T(8,128)(2,1)S(1)}, bf16[2,192,192]{2,1,0:T(8,128)(2,1)}, u32[]{:S(2)}) copy-start(bf16[2,192,192]{2,1,0:T(8,128)(2,1)} %constant.106.clone.matrix_ref) | copy-start | bytes 442372
  0.0 26.9 %copy-start.9 = (bf16[2,192,384]{2,1,0:T(8,128)(2,1)S(1)}, bf16[2,192,384]{2,1,0:T(8,128)(2,1)}, u32[]{:S(2)}) copy-start(bf16[2,192,384]{2,1,0:T(8,128)(2,1)} %constant.105.clone.ex_ref) | copy-start | bytes 884740
  0.0 26.9 %copy-start.11 = (bf16[2,192,256]{2,1,0:T(8,128)(2,1)S(1)}, bf16[2,192,256]{2,1,0:T(8,128)(2,1)}, u32[]{:S(2)}) copy-start(bf16[2,192,256]{2,1,0:T(8,128)(2,1)} %constant.104.clone.ey_ref) | copy-start | bytes 589828
  0.0 14.0 %copy-start.12 = (f32[12,24,192]{2,1,0:T(8,128)S(1)}, f32[12,24,192]{2,1,0:T(8,128)}, u32[]{:S(2)}) copy-start(f32[12,24,192]{2,1,0:T(8,128)} %param.15) | copy-start | bytes 663556
  2.5 24.4 %all-to-all-start = ((f32[128,1,896]{2,1,0:T(1,128)}), f32[128,1,896]{2,1,0:T(1,128)S(1)}, u32[]{:S(2)}, u32[]{:S(2)}) async-start(f32[128,1,896]{2,1,0:T(1,128)} %bitcast.6), calls=%async_computation | async-start | bytes 917504 | tf_op jit(solution)/shard_map/all_to_all | solution.py:533
  14.0 9.4 %collective-permute-start = (f32[2,72,192]{2,1,0:T(8,128)S(1)}, f32[2,72,192]{2,1,0:T(8,128)S(1)}, u32[]{:S(2)}, u32[]{:S(2)}) collective-permute-start(f32[2,72,192]{2,1,0:T(8,128)S(1)} %get-tuple-element.26), channel_id=1, source_target_pairs={{0,1},{1,0},{2,3},{3,2},{4,5},{5,4},{6,7},{7,6},{8,9},{9,8},{10,11... | collective-permute-start | bytes 331784 | tf_op jit(solution)/shard_map/ppermute | solution.py:540
  30.2 22.0 %copy-start.10 = (bf16[2,256,256]{2,1,0:T(8,128)(2,1)S(1)}, bf16[2,256,256]{2,1,0:T(8,128)(2,1)}, u32[]{:S(2)}) copy-start(bf16[2,256,256]{2,1,0:T(8,128)(2,1)} %constant.107.clone.wide_ref) | copy-start | bytes 786436
  30.2 22.0 %all-to-all-start.1 = ((f32[64,1,3456]{2,1,0:T(1,128)}), f32[64,1,3456]{2,1,0:T(1,128)S(1)}, u32[]{:S(2)}, u32[]{:S(2)}) async-start(f32[64,1,3456]{2,1,0:T(1,128)} %bitcast.11), calls=%async_computation.1 | async-start | bytes 1769472 | tf_op jit(solution)/shard_map/all_to_all | solution.py:533
  37.1 12.7 %collective-permute-start.3 = (f32[2,72,192]{2,1,0:T(8,128)S(1)}, f32[2,72,192]{2,1,0:T(8,128)S(1)}, u32[]{:S(2)}, u32[]{:S(2)}) collective-permute-start(f32[2,72,192]{2,1,0:T(8,128)S(1)} %get-tuple-element.22), channel_id=1, source_target_pairs={{2,0},{4,2},{14,12},{8,14},{3,1},{5,3},{15,13},{9,15},{18,16},{20,... | collective-permute-start | bytes 331784 | tf_op jit(solution)/shard_map/ppermute | solution.py:549
  41.2 8.6 %collective-permute-start.2 = (f32[2,72,192]{2,1,0:T(8,128)S(1)}, f32[2,72,192]{2,1,0:T(8,128)S(1)}, u32[]{:S(2)}, u32[]{:S(2)}) collective-permute-start(f32[2,72,192]{2,1,0:T(8,128)S(1)} %get-tuple-element.23), channel_id=1, source_target_pairs={{4,0},{6,2},{8,12},{10,14},{5,1},{7,3},{9,13},{11,15},{20,16},{22,... | collective-permute-start | bytes 331784 | tf_op jit(solution)/shard_map/ppermute | solution.py:549
  42.8 7.0 %collective-permute-start.1 = (f32[2,72,192]{2,1,0:T(8,128)S(1)}, f32[2,72,192]{2,1,0:T(8,128)S(1)}, u32[]{:S(2)}, u32[]{:S(2)}) collective-permute-start(f32[2,72,192]{2,1,0:T(8,128)S(1)} %get-tuple-element.24), channel_id=1, source_target_pairs={{6,0},{0,2},{10,12},{12,14},{7,1},{1,3},{11,13},{13,15},{22,16},{1... | collective-permute-start | bytes 331784 | tf_op jit(solution)/shard_map/ppermute | solution.py:549
  56.1 23.9 %copy-start.7 = (bf16[2,2,192,256]{3,2,1,0:T(8,128)(2,1)S(1)}, bf16[2,2,192,256]{3,2,1,0:T(8,128)(2,1)}, u32[]{:S(2)}) copy-start(bf16[2,2,192,256]{3,2,1,0:T(8,128)(2,1)} %constant.109.clone.ly_ref) | copy-start | bytes 1179652
  56.1 23.9 %copy-start.8 = (bf16[2,384,192]{2,1,0:T(8,128)(2,1)S(1)}, bf16[2,384,192]{2,1,0:T(8,128)(2,1)}, u32[]{:S(2)}) copy-start(bf16[2,384,192]{2,1,0:T(8,128)(2,1)} %constant.108.clone.lz_ref) | copy-start | bytes 884740
  56.1 23.9 %all-to-all-start.2 = ((f32[64,1,3456]{2,1,0:T(1,128)}), f32[64,1,3456]{2,1,0:T(1,128)S(1)}, u32[]{:S(2)}, u32[]{:S(2)}) async-start(f32[64,1,3456]{2,1,0:T(1,128)} %bitcast.19), calls=%async_computation.2 | async-start | bytes 1769472 | tf_op jit(solution)/shard_map/all_to_all | solution.py:533
  64.7 4.0 %collective-permute-start.4 = (f32[4,2,72,192]{3,2,1,0:T(8,128)S(1)}, f32[4,2,72,192]{3,2,1,0:T(8,128)}, u32[]{:S(2)}, u32[]{:S(2)}) collective-permute-start(f32[4,2,72,192]{3,2,1,0:T(8,128)S(1)} %pad_maximum_fusion), channel_id=1, source_target_pairs={{0,8},{2,10},{12,4},{14,6},{1,9},{3,11},{13,5},{15,7},{16,24},{18,... | collective-permute-start | bytes 1327112 | tf_op jit(solution)/shard_map/ppermute | solution.py:556
  80.1 22.4 %copy-start = (bf16[2,384,384]{2,1,0:T(8,128)(2,1)S(1)}, bf16[2,384,384]{2,1,0:T(8,128)(2,1)}, u32[]{:S(2)}) copy-start(bf16[2,384,384]{2,1,0:T(8,128)(2,1)} %constant.111.clone.matrix_hbm.matrix_ref) | copy-start | bytes 1769476
  80.1 22.4 %copy-start.6 = (bf16[2,384,192]{2,1,0:T(8,128)(2,1)S(1)}, bf16[2,384,192]{2,1,0:T(8,128)(2,1)}, u32[]{:S(2)}) copy-start(bf16[2,384,192]{2,1,0:T(8,128)(2,1)} %constant.110.clone.lift_ref) | copy-start | bytes 884740
  106.1 33.6 %copy-start.4 = (bf16[2,384,384]{2,1,0:T(8,128)(2,1)S(1)}, bf16[2,384,384]{2,1,0:T(8,128)(2,1)}, u32[]{:S(2)}) copy-start(bf16[2,384,384]{2,1,0:T(8,128)(2,1)} %constant.113.clone.back_hbm) | copy-start | bytes 1769476
  106.1 33.6 %copy-start.5 = (bf16[2,384,384]{2,1,0:T(8,128)(2,1)S(1)}, bf16[2,384,384]{2,1,0:T(8,128)(2,1)}, u32[]{:S(2)}) copy-start(bf16[2,384,384]{2,1,0:T(8,128)(2,1)} %constant.112.clone.out_hbm) | copy-start | bytes 1769476
  152.6 31.2 %copy-start.1 = (f32[48,24,384]{2,1,0:T(8,128)S(1)}, f32[48,24,384]{2,1,0:T(8,128)}, u32[]{:S(2)}) copy-start(f32[48,24,384]{2,1,0:T(8,128)} %param.16) | copy-start | bytes 5308420
  152.6 31.1 %copy-start.2 = (f32[384,1152]{1,0:T(8,128)S(1)}, f32[384,1152]{1,0:T(8,128)}, u32[]{:S(2)}) copy-start(f32[384,1152]{1,0:T(8,128)} %get-tuple-element.18.evolved_ref) | copy-start | bytes 5308420

commit v5 on v4

--- a/solution.py
+++ b/solution.py
@@ -157,13 +157,17 @@
     return [row[:, 128 * t : 128 * t + 128] for t in range(row.shape[1] // 128)]
 
 
-def turn_blocks(rows, count, lead=0):
-    lane = lax.broadcasted_iota(jnp.int32, rows[0][0].shape, 1)
-    shifted = []
-    for a, row in enumerate(rows):
-        shift = (24 * a - lead) % NF
-        whole = jnp.concatenate(row, axis=1)
-        shifted.append(tiles_of(pltpu.roll(whole, shift, 1) if shift else whole))
+def shift_runs(row, lanes):
+    lanes %= NF
+    return pltpu.roll(row, lanes, 1) if lanes else row
+
+
+def skew(rows, lead=0):
+    return [tiles_of(shift_runs(row, 24 * a - lead)) for a, row in enumerate(rows)]
+
+
+def diagonals(skewed, count):
+    lane = lax.broadcasted_iota(jnp.int32, skewed[0][0].shape, 1)
     result = []
     for b in range(count):
         tiles = []
@@ -171,12 +175,11 @@
             tile = None
             for p in range(128 * t // 24, (128 * t + 127) // 24 + 1):
                 a = (p - b) % 16
-                if a < len(rows):
-                    piece = shifted[a][t]
+                if a < len(skewed):
+                    piece = skewed[a][t]
                     tile = piece if tile is None else jnp.where(lane < 24 * p - 128 * t, tile, piece)
-            tiles.append(shifted[0][t] if tile is None else tile)
-        whole = jnp.concatenate(tiles, axis=1)
-        result.append(pltpu.roll(whole, NF - 24 * b, 1) if b else whole)
+            tiles.append(skewed[0][t] if tile is None else tile)
+        result.append(jnp.concatenate(tiles, axis=1))
     return result
 
 
@@ -229,11 +232,12 @@
     lane = lax.broadcasted_iota(jnp.int32, (64, 128), 1)
     for k in range(3):
         for g in range(2):
-            rows = [
-                [got_ref[pl.ds(g * 448 + c * 7 + 2 * k + t, 8, stride=56), :] for t in range(3)]
-                for c in range(8)
-            ]
-            for i, row in enumerate(turn_blocks(rows, 12, 32 * k)):
+            rows = []
+            for c in range(8):
+                tiles = [got_ref[pl.ds(g * 448 + c * 7 + 2 * k + t, 8, stride=56), :] for t in range(3)]
+                rows.append(jnp.concatenate(tiles, axis=1))
+            for i, row in enumerate(diagonals(skew(rows, 32 * k), 12)):
+                row = shift_runs(row, -24 * i)
                 plane_ref[16 * i + 8 * g : 16 * i + 8 * g + 8, :] = row[:, :256]
         half = dot3(pair(ey_ref), split(plane_ref[...]), TURNED)
         evolved = dot3(split(half), pair(ex_ref))
@@ -326,8 +330,9 @@
             rows = []
             for i in range(16):
                 row = lifted_ref[128 * g + 8 * i : 128 * g + 8 * i + 8, :]
-                rows.append(tiles_of(row) + [blank])
-            for p, row in enumerate(turn_blocks(rows, 8)):
+                rows.append(jnp.concatenate([row, blank], axis=1))
+            for p, row in enumerate(diagonals(skew(rows), 8)):
+                row = jnp.where(core == 0, shift_runs(row, 24 * p), shift_runs(row, 24 * p + 24))
                 for t, tile in enumerate(tiles_of(row)):
                     out_ref[pl.ds(p * 224 + k * 9 + g * 3 + t, 8, stride=28), :] = tile
     out_ref[pl.ds(27, 64, stride=28), :] = jnp.broadcast_to(part, (64, 128))
@@ -401,7 +406,7 @@
 
 
 def fine_slab_kernel(
-    place_ref, got_ref, out_hbm, back_hbm, matrix_hbm, out_ref, plane_ref, out_m, back_m, matrix, sems
+    place_ref, got_ref, out_hbm, back_hbm, matrix_hbm, out_ref, plane_ref, back_ref, out_m, back_m, matrix, sems
 ):
     out_copies = fetch_left(out_hbm, out_m, sems.at[0])
     back_copies = fetch_left(back_hbm, back_m, sems.at[1])
@@ -410,45 +415,43 @@
     wz = squares(lax.broadcasted_iota(jnp.int32, (NF, NF), 0), NF, 1.0)
     wy = squares(lax.broadcasted_iota(jnp.int32, (NF, NF), 1), NF, 1.0)
 
-    def body(k, carry):
-        def unpack(g, carry):
+
+    def unpack(k):
+        for g in range(3):
             base = k * 9 + g * 3
-            rows = [
+            skewed = [
                 [got_ref[pl.ds(r * 216 + base + t, 8, stride=27), :] for t in range(3)]
                 for r in range(16)
             ]
-            for i, row in enumerate(turn_blocks(rows, 16)):
-                plane_ref[pl.ds(pl.multiple_of(g * 128 + 8 * i, 8), 8), :] = row
-            return carry
-
-        lax.fori_loop(0, 3, unpack, 0)
-
-        @pl.when(k == 0)
-        def _():
-            finish(out_copies + copies + back_copies)
-
+            for i, row in enumerate(diagonals(skewed, 16)):
+                start = 128 * g + 8 * i
+                plane_ref[start : start + 8, :] = shift_runs(row, -24 * i)
+
+    def pack(k):
+        for g in range(3):
+            base = k * 9 + g * 3
+            rows = [back_ref[128 * g + 8 * i : 128 * g + 8 * i + 8, :] for i in range(16)]
+            for r, row in enumerate(diagonals(skew(rows), 16)):
+                for t, tile in enumerate(tiles_of(row)):
+                    out_ref[pl.ds(r * 216 + base + t, 8, stride=27), :] = tile
+
+    def body(k, carry):
         mid = dot(out_m[...], right3(plane_ref[...]))
+        pack(jnp.maximum(k - 1, 0))
+        unpack(jnp.minimum(k + 1, 2))
         mid = dot(left3(mid), matrix[...])
         kx = 128 * k + place_ref[4]
         wx = squares(jnp.full((1, 1), kx, jnp.int32), NF, 1.0)
         mid = mid * dipolar(wx, wy, wz, NF)
         mid = dot(left3(mid), matrix[...])
-        plane_ref[...] = dot(back_m[...], right3(mid))
-
-        def pack(g, carry):
-            base = k * 9 + g * 3
-            rows = []
-            for i in range(16):
-                rows.append(tiles_of(plane_ref[pl.ds(pl.multiple_of(g * 128 + 8 * i, 8), 8), :]))
-            for r, row in enumerate(turn_blocks(rows, 16)):
-                for t, tile in enumerate(tiles_of(row)):
-                    out_ref[pl.ds(r * 216 + base + t, 8, stride=27), :] = tile
-            return carry
-
-        lax.fori_loop(0, 3, pack, 0)
+        back_ref[...] = dot(back_m[...], right3(mid))
         return carry
 
+    back_ref[...] = jnp.zeros_like(back_ref)
+    unpack(0)
+    finish(out_copies + copies + back_copies)
     lax.fori_loop(0, 3, body, 0)
+    pack(2)
 
 
 def fine_slab(place, got):
@@ -459,6 +462,7 @@
         in_specs=[SMEM, VMEM] + [HBM] * 3,
         out_specs=VMEM,
         scratch_shapes=[
+            pltpu.VMEM((NF, NF), F32),
             pltpu.VMEM((NF, NF), F32),
             pltpu.VMEM((NF, 1152), BF16),
             pltpu.VMEM((NF, 1152), BF16),
@@ -468,8 +472,12 @@
     )(place, got, jnp.asarray(HF_OUT2), jnp.asarray(HF_BACK2), jnp.asarray(HF2))
 
 
-def fine_out_kernel(got_ref, evolved_ref, potential_ref, matrix_ref, damped_ref, part_ref):
+def fine_out_kernel(place_ref, got_ref, evolved_ref, potential_ref, matrix_ref, damped_ref, part_ref):
     part_ref[...] = jnp.zeros_like(part_ref)
+    row = place_ref[5]
+
+    def block(n, p):
+        return pl.ds(pl.multiple_of(384 * n + 24 * lax.rem(p + 16 - row, 16), 8), 24)
 
     def body(n, carry):
         rows = []
@@ -479,17 +487,19 @@
         field = dot3(pair(matrix_ref), split(jnp.concatenate(rows, axis=0)))
         columns = pl.ds(pl.multiple_of(n * 384, 128), 384)
         evolved = evolved_ref[:, columns]
-        potential = potential_ref[columns, :].T
+        potential = jnp.concatenate([potential_ref[block(n, p), :] for p in range(16)], axis=0).T
         exponent = -TIME_STEP * (potential + CONTACT * evolved * evolved + field)
         damped = jnp.exp(exponent) * evolved
         part_ref[...] += jnp.sum(damped * damped)
-        damped_ref[columns, :] = damped.T
+        turned = damped.T
+        for p in range(16):
+            damped_ref[block(n, p), :] = turned[24 * p : 24 * p + 24, :]
         return carry
 
     lax.fori_loop(0, 3, body, 0)
 
 
-def fine_out(got, evolved, potential):
+def fine_out(place, got, evolved, potential):
     return pl.pallas_call(
         fine_out_kernel,
         out_shape=[
@@ -497,9 +507,9 @@
             jax.ShapeDtypeStruct((128, 128), F32),
         ],
         compiler_params=LIMIT,
-        in_specs=[VMEM] * 4,
+        in_specs=[SMEM] + [VMEM] * 4,
         out_specs=[VMEM] * 2,
-    )(got, evolved, potential, jnp.asarray(HF2))
+    )(place, got, evolved, potential, jnp.asarray(HF2))
 
 
 def scale_kernel(parts_ref, damped_ref, out_hbm, scaled_ref, sems):
@@ -562,7 +572,7 @@
     chip = lax.axis_index(CHIPS)
     device = lax.axis_index(ALL)
     across, near = lax.axis_index("cols_0"), lax.axis_index("cols_1")
-    place = jnp.stack([core, across, near, chip, device])
+    place = jnp.stack([core, across, near, chip, device, lax.axis_index(ROWS)])
 
     got = exchange(coarse_pencil(wave_coarse.reshape(288, NC)), ALL, 128).reshape(896, 128)
     got, planes = lax.optimization_barrier((got, swap_planes(potential_coarse, near)))
@@ -576,7 +586,7 @@
     got = exchange(spectrum, ALL, 128).reshape(3456, 128)
     spectrum = fine_slab(place, got)
     got = exchange(spectrum, ALL, 128).reshape(3456, 128)
-    damped, part = fine_out(got, evolved, potential_fine.reshape(1152, NF))
+    damped, part = fine_out(place, got, evolved, potential_fine.reshape(1152, NF))
     parts = exchange(part, ALL, 128).reshape(128, 128)
     return scaled(parts, damped).reshape(48, 24, NF)
 

time: 203 us -> 200 us (0.985)
  Pallas kernels: 33.6 us -> 30.6 us
    pallas_call x1, Pallas kernels: 12.8 us -> 9.16 us  [fine_slab(): pl.pallas_call(fine_slab_kernel, out_shape=jax.ShapeDtypeStruct((3456, 12...]
where the time goes in v5:
time: 200 us
  blocking collectives  98.2 us (49%)
  starting transfers between devices  35.9 us (18%)
  waiting for transfers between devices  32.9 us (16%)
  Pallas kernels  30.6 us (15%)
    all_to_all x4, blocking collectives, exchange(): return lax.all_to_all(flat, axes, split_axis=0, concat_axis=0, tiled=False)  98.2 us
    all_to_all x3, starting transfers between devices, exchange(): return lax.all_to_all(flat, axes, split_axis=0, concat_axis=0, tiled=False)  26.8 us
    all_to_all x3, waiting for transfers between devices, exchange(): return lax.all_to_all(flat, axes, split_axis=0, concat_axis=0, tiled=False)  16 us
    pallas_call x1, Pallas kernels, fine_slab(): pl.pallas_call(fine_slab_kernel, out_shape=jax.ShapeDtypeStruct((3456, 12...  9.16 us
    ppermute x1, waiting for transfers between devices, swap_planes(): lax.ppermute(theirs, 'cols_1', [(0, 1), (1, 0)])  7.94 us
    ppermute x3, starting transfers between devices, spread_planes(): chunk = lax.ppermute(chunk, (CORE, 'cols_0'), moves)  6.39 us
    ppermute x3, waiting for transfers between devices, spread_planes(): chunk = lax.ppermute(chunk, (CORE, 'cols_0'), moves)  6.23 us
  transfers between devices with their start and end apart: 8, of which 6 were waited for; matrix products, arithmetic and copies ran while one was open for 1% of the time, Pallas kernels for 0%

profile of v5, /device:TPU:1, one launch (start us, length us, event | category | flops | bytes accessed | tf_op | source)
XLA Modules:
  0.0 199.5 jit_solution(6044805579222434775)
XLA Ops:
  0.0 2.5 %shard_map.136 = f32[896,128]{1,0:T(8,128)} custom-call(f32[288,192]{1,0:T(8,128)} %bitcast.53, bf16[2,192,192]{2,1,0:T(8,128)(2,1)} %constant.105.clone.matrix_hbm), custom_call_target="tpu_custom_call" | custom-call | tf_op jit(solution)/shard_map/pallas_call | solution.py:217
  2.5 11.5 %all-to-all-start = ((f32[128,1,896]{2,1,0:T(1,128)}), f32[128,1,896]{2,1,0:T(1,128)S(1)}, u32[]{:S(2)}, u32[]{:S(2)}) async-start(f32[128,1,896]{2,1,0:T(1,128)} %bitcast.7), calls=%async_computation | async-start | bytes 917504 | tf_op jit(solution)/shard_map/all_to_all | solution.py:543
  14.0 1.4 collective-permute-start
  15.5 7.9 %collective-permute-done = f32[2,72,192]{2,1,0:T(8,128)S(1)} collective-permute-done((f32[2,72,192]{2,1,0:T(8,128)S(1)}, f32[2,72,192]{2,1,0:T(8,128)S(1)}, u32[]{:S(2)}, u32[]{:S(2)}) %collective-permute-start) | collective-permute-done | bytes 110624 | tf_op jit(solution)/shard_map/ppermute | solution.py:550
  23.4 3.5 %all-to-all-done = f32[128,1,896]{2,1,0:T(1,128)S(1)} async-done(((f32[128,1,896]{2,1,0:T(1,128)}), f32[128,1,896]{2,1,0:T(1,128)S(1)}, u32[]{:S(2)}, u32[]{:S(2)}) %all-to-all-start) | async-done | bytes 458784 | tf_op jit(solution)/shard_map/all_to_all | solution.py:543
  26.9 3.3 %shard_map.137 = f32[1728,128]{1,0:T(8,128)} custom-call(f32[896,128]{1,0:T(8,128)S(1)} %bitcast.47, bf16[2,192,256]{2,1,0:T(8,128)(2,1)S(1)} %copy-done.11, bf16[2,192,384]{2,1,0:T(8,128)(2,1)S(1)} %copy-done.9, bf16[2,192,192]{2,1,0:T(8,128)(2,1)S(1)} %copy-done.3), custom_call_target="tpu_custom_call" | custom-call | tf_op jit(solution)/shard_map/pallas_call | solution.py:254
  30.2 6.8 %all-to-all-start.1 = ((f32[64,1,3456]{2,1,0:T(1,128)}), f32[64,1,3456]{2,1,0:T(1,128)S(1)}, u32[]{:S(2)}, u32[]{:S(2)}) async-start(f32[64,1,3456]{2,1,0:T(1,128)} %bitcast.12), calls=%async_computation.1 | async-start | bytes 1769472 | tf_op jit(solution)/shard_map/all_to_all | solution.py:543
  37.1 4.1 %collective-permute-start.3 = (f32[2,72,192]{2,1,0:T(8,128)S(1)}, f32[2,72,192]{2,1,0:T(8,128)S(1)}, u32[]{:S(2)}, u32[]{:S(2)}) collective-permute-start(f32[2,72,192]{2,1,0:T(8,128)S(1)} %get-tuple-element.22), channel_id=1, source_target_pairs={{2,0},{4,2},{14,12},{8,14},{3,1},{5,3},{15,13},{9,15},{18,16},{20,... | collective-permute-start | bytes 331784 | tf_op jit(solution)/shard_map/ppermute | solution.py:559
  41.2 1.6 collective-permute-start.2
  43.6 6.2 %collective-permute-done.3 = f32[2,72,192]{2,1,0:T(8,128)S(1)} collective-permute-done((f32[2,72,192]{2,1,0:T(8,128)S(1)}, f32[2,72,192]{2,1,0:T(8,128)S(1)}, u32[]{:S(2)}, u32[]{:S(2)}) %collective-permute-start.3) | collective-permute-done | bytes 110624 | tf_op jit(solution)/shard_map/ppermute | solution.py:559
  49.9 2.3 %all-to-all-done.1 = f32[64,1,3456]{2,1,0:T(1,128)S(1)} async-done(((f32[64,1,3456]{2,1,0:T(1,128)}), f32[64,1,3456]{2,1,0:T(1,128)S(1)}, u32[]{:S(2)}, u32[]{:S(2)}) %all-to-all-start.1) | async-done | bytes 884768 | tf_op jit(solution)/shard_map/all_to_all | solution.py:543
  52.3 3.9 %shard_map.138 = f32[1728,128]{1,0:T(8,128)} custom-call(s32[6]{0:T(128)S(1)} %stack.47.place_ref, f32[1728,128]{1,0:T(8,128)S(1)} %bitcast.44, bf16[2,192,192]{2,1,0:T(8,128)(2,1)S(1)} %copy-done.3, bf16[2,256,256]{2,1,0:T(8,128)(2,1)S(1)} %copy-done.10), custom_call_target="tpu_custom_call" | custom-call | tf_op jit(solution)/shard_map/pallas_call | solution.py:292
  56.1 8.6 %all-to-all-start.2 = ((f32[64,1,3456]{2,1,0:T(1,128)}), f32[64,1,3456]{2,1,0:T(1,128)S(1)}, u32[]{:S(2)}, u32[]{:S(2)}) async-start(f32[64,1,3456]{2,1,0:T(1,128)} %bitcast.20), calls=%async_computation.2 | async-start | bytes 1769472 | tf_op jit(solution)/shard_map/all_to_all | solution.py:543
  66.0 2.7 %collective-permute-done.4 = f32[4,2,72,192]{3,2,1,0:T(8,128)} collective-permute-done((f32[4,2,72,192]{3,2,1,0:T(8,128)S(1)}, f32[4,2,72,192]{3,2,1,0:T(8,128)}, u32[]{:S(2)}, u32[]{:S(2)}) %collective-permute-start.4) | collective-permute-done | bytes 442400 | tf_op jit(solution)/shard_map/ppermute | solution.py:566
  69.9 10.2 %all-to-all-done.2 = f32[64,1,3456]{2,1,0:T(1,128)S(1)} async-done(((f32[64,1,3456]{2,1,0:T(1,128)}), f32[64,1,3456]{2,1,0:T(1,128)S(1)}, u32[]{:S(2)}, u32[]{:S(2)}) %all-to-all-start.2) | async-done | bytes 884768 | tf_op jit(solution)/shard_map/all_to_all | solution.py:543
  80.1 3.2 %shard_map.139 = f32[1792,128]{1,0:T(8,128)S(1)} custom-call(s32[6]{0:T(128)S(1)} %stack.47.place_ref, f32[1728,128]{1,0:T(8,128)S(1)} %bitcast.45, f32[8,72,192]{2,1,0:T(8,128)S(1)} %bitcast.46, bf16[2,192,192]{2,1,0:T(8,128)(2,1)S(1)} %copy-done.3, bf16[2,384,192]{2,1,0:T(8,128)(2,1)S(1)} %copy-done.8, bf16[2,2,192,256]{3,2,1,0:T(8,128)(2,1)S(1)} %copy-done.7), custom_call_target="tpu_custom_call" | custom-call | tf_op jit(solution)/shard_map/pallas_call | solution.py:342
  83.3 19.3 %all_to_all.35 = f32[64,1,3584]{2,1,0:T(1,128)S(1)} all-to-all(f32[64,1,3584]{2,1,0:T(1,128)S(1)} %bitcast.42), channel_id=1, replica_groups=mesh['rows_0'=4,'rows_1'=2,'rows_2'=2,'cols_0'=4,'cols_1'=2] {'rows_0','..., dimensions={0} | all-to-all | bytes 1835008 | tf_op jit(solution)/shard_map/all_to_all | solution.py:543
  102.6 3.6 %shard_map.140 = (f32[384,1152]{1,0:T(8,128)}, f32[3456,128]{1,0:T(8,128)S(1)}) custom-call(f32[1792,128]{1,0:T(8,128)S(1)} %bitcast.43, bf16[2,384,192]{2,1,0:T(8,128)(2,1)S(1)} %copy-done.6, bf16[2,384,384]{2,1,0:T(8,128)(2,1)S(1)} %copy-done), custom_call_target="tpu_custom_call" | custom-call | tf_op jit(solution)/shard_map/pallas_call | solution.py:390
  106.2 33.6 %all_to_all.36 = f32[128,1,3456]{2,1,0:T(1,128)S(1)} all-to-all(f32[128,1,3456]{2,1,0:T(1,128)S(1)} %bitcast.49), channel_id=1, replica_groups=mesh['rows_0'=4,'rows_1'=2,'rows_2'=2,'cols_0'=4,'cols_1'=2] {'rows_0','..., dimensions={0} | all-to-all | bytes 3538944 | tf_op jit(solution)/shard_map/all_to_all | solution.py:543
  139.8 9.2 %shard_map.141 = f32[3456,128]{1,0:T(8,128)S(1)} custom-call(s32[6]{0:T(128)S(1)} %stack.47.place_ref, f32[3456,128]{1,0:T(8,128)S(1)} %bitcast.40, bf16[2,384,384]{2,1,0:T(8,128)(2,1)S(1)} %copy-done.5, bf16[2,384,384]{2,1,0:T(8,128)(2,1)S(1)} %copy-done.4, bf16[2,384,384]{2,1,0:T(8,128)(2,1)S(1)} %copy-done), custom_call_target="tpu_custom_call" | custom-call | tf_op jit(solution)/shard_map/pallas_call | solution.py:458
  149.0 31.1 %all_to_all.37 = f32[128,1,3456]{2,1,0:T(1,128)S(1)} all-to-all(f32[128,1,3456]{2,1,0:T(1,128)S(1)} %bitcast.41), channel_id=1, replica_groups=mesh['rows_0'=4,'rows_1'=2,'rows_2'=2,'cols_0'=4,'cols_1'=2] {'rows_0','..., dimensions={0} | all-to-all | bytes 3538944 | tf_op jit(solution)/shard_map/all_to_all | solution.py:543
  180.1 3.7 %shard_map.142 = (f32[1152,384]{1,0:T(8,128)S(1)}, f32[128,128]{1,0:T(8,128)S(1)}) custom-call(s32[6]{0:T(128)S(1)} %stack.47.place_ref, f32[3456,128]{1,0:T(8,128)S(1)} %bitcast.39, f32[384,1152]{1,0:T(8,128)S(1)} %copy-done.2, f32[1152,384]{1,0:T(8,128)S(1)} %bitcast.48, bf16[2,384,384]{2,1,0:T(8,128)(2,1)S(1)} %copy-done), custom_call_target="tpu_custom_call" | custom-call | tf_op jit(solution)/shard_map/pallas_call | solution.py:503
  183.9 14.2 %all_to_all.38 = f32[128,1,128]{2,1,0:T(1,128)S(1)} all-to-all(f32[128,1,128]{2,1,0:T(1,128)S(1)} %bitcast.51), channel_id=1, replica_groups=mesh['rows_0'=4,'rows_1'=2,'rows_2'=2,'cols_0'=4,'cols_1'=2] {'rows_0','..., dimensions={0} | all-to-all | bytes 131072 | tf_op jit(solution)/shard_map/all_to_all | solution.py:543
  198.0 1.3 shard_map.143
  (36 shorter events, 3.4 us)
Async XLA Ops:
  0.0 26.9 %copy-start.3 = (bf16[2,192,192]{2,1,0:T(8,128)(2,1)S(1)}, bf16[2,192,192]{2,1,0:T(8,128)(2,1)}, u32[]{:S(2)}) copy-start(bf16[2,192,192]{2,1,0:T(8,128)(2,1)} %constant.108.clone.matrix_ref) | copy-start | bytes 442372
  0.0 26.9 %copy-start.9 = (bf16[2,192,384]{2,1,0:T(8,128)(2,1)S(1)}, bf16[2,192,384]{2,1,0:T(8,128)(2,1)}, u32[]{:S(2)}) copy-start(bf16[2,192,384]{2,1,0:T(8,128)(2,1)} %constant.107.clone.ex_ref) | copy-start | bytes 884740
  0.0 26.9 %copy-start.11 = (bf16[2,192,256]{2,1,0:T(8,128)(2,1)S(1)}, bf16[2,192,256]{2,1,0:T(8,128)(2,1)}, u32[]{:S(2)}) copy-start(bf16[2,192,256]{2,1,0:T(8,128)(2,1)} %constant.106.clone.ey_ref) | copy-start | bytes 589828
  0.0 14.0 %copy-start.12 = (f32[12,24,192]{2,1,0:T(8,128)S(1)}, f32[12,24,192]{2,1,0:T(8,128)}, u32[]{:S(2)}) copy-start(f32[12,24,192]{2,1,0:T(8,128)} %param.15) | copy-start | bytes 663556
  2.5 24.4 %all-to-all-start = ((f32[128,1,896]{2,1,0:T(1,128)}), f32[128,1,896]{2,1,0:T(1,128)S(1)}, u32[]{:S(2)}, u32[]{:S(2)}) async-start(f32[128,1,896]{2,1,0:T(1,128)} %bitcast.7), calls=%async_computation | async-start | bytes 917504 | tf_op jit(solution)/shard_map/all_to_all | solution.py:543
  14.0 9.4 %collective-permute-start = (f32[2,72,192]{2,1,0:T(8,128)S(1)}, f32[2,72,192]{2,1,0:T(8,128)S(1)}, u32[]{:S(2)}, u32[]{:S(2)}) collective-permute-start(f32[2,72,192]{2,1,0:T(8,128)S(1)} %get-tuple-element.26), channel_id=1, source_target_pairs={{0,1},{1,0},{2,3},{3,2},{4,5},{5,4},{6,7},{7,6},{8,9},{9,8},{10,11... | collective-permute-start | bytes 331784 | tf_op jit(solution)/shard_map/ppermute | solution.py:550
  30.2 22.0 %copy-start.10 = (bf16[2,256,256]{2,1,0:T(8,128)(2,1)S(1)}, bf16[2,256,256]{2,1,0:T(8,128)(2,1)}, u32[]{:S(2)}) copy-start(bf16[2,256,256]{2,1,0:T(8,128)(2,1)} %constant.109.clone.wide_ref) | copy-start | bytes 786436
  30.2 22.0 %all-to-all-start.1 = ((f32[64,1,3456]{2,1,0:T(1,128)}), f32[64,1,3456]{2,1,0:T(1,128)S(1)}, u32[]{:S(2)}, u32[]{:S(2)}) async-start(f32[64,1,3456]{2,1,0:T(1,128)} %bitcast.12), calls=%async_computation.1 | async-start | bytes 1769472 | tf_op jit(solution)/shard_map/all_to_all | solution.py:543
  37.1 12.7 %collective-permute-start.3 = (f32[2,72,192]{2,1,0:T(8,128)S(1)}, f32[2,72,192]{2,1,0:T(8,128)S(1)}, u32[]{:S(2)}, u32[]{:S(2)}) collective-permute-start(f32[2,72,192]{2,1,0:T(8,128)S(1)} %get-tuple-element.22), channel_id=1, source_target_pairs={{2,0},{4,2},{14,12},{8,14},{3,1},{5,3},{15,13},{9,15},{18,16},{20,... | collective-permute-start | bytes 331784 | tf_op jit(solution)/shard_map/ppermute | solution.py:559
  41.2 8.6 %collective-permute-start.2 = (f32[2,72,192]{2,1,0:T(8,128)S(1)}, f32[2,72,192]{2,1,0:T(8,128)S(1)}, u32[]{:S(2)}, u32[]{:S(2)}) collective-permute-start(f32[2,72,192]{2,1,0:T(8,128)S(1)} %get-tuple-element.23), channel_id=1, source_target_pairs={{4,0},{6,2},{8,12},{10,14},{5,1},{7,3},{9,13},{11,15},{20,16},{22,... | collective-permute-start | bytes 331784 | tf_op jit(solution)/shard_map/ppermute | solution.py:559
  42.8 7.0 %collective-permute-start.1 = (f32[2,72,192]{2,1,0:T(8,128)S(1)}, f32[2,72,192]{2,1,0:T(8,128)S(1)}, u32[]{:S(2)}, u32[]{:S(2)}) collective-permute-start(f32[2,72,192]{2,1,0:T(8,128)S(1)} %get-tuple-element.24), channel_id=1, source_target_pairs={{6,0},{0,2},{10,12},{12,14},{7,1},{1,3},{11,13},{13,15},{22,16},{1... | collective-permute-start | bytes 331784 | tf_op jit(solution)/shard_map/ppermute | solution.py:559
  56.1 23.9 %copy-start.7 = (bf16[2,2,192,256]{3,2,1,0:T(8,128)(2,1)S(1)}, bf16[2,2,192,256]{3,2,1,0:T(8,128)(2,1)}, u32[]{:S(2)}) copy-start(bf16[2,2,192,256]{3,2,1,0:T(8,128)(2,1)} %constant.111.clone.ly_ref) | copy-start | bytes 1179652
  56.1 23.9 %copy-start.8 = (bf16[2,384,192]{2,1,0:T(8,128)(2,1)S(1)}, bf16[2,384,192]{2,1,0:T(8,128)(2,1)}, u32[]{:S(2)}) copy-start(bf16[2,384,192]{2,1,0:T(8,128)(2,1)} %constant.110.clone.lz_ref) | copy-start | bytes 884740
  56.1 23.9 %all-to-all-start.2 = ((f32[64,1,3456]{2,1,0:T(1,128)}), f32[64,1,3456]{2,1,0:T(1,128)S(1)}, u32[]{:S(2)}, u32[]{:S(2)}) async-start(f32[64,1,3456]{2,1,0:T(1,128)} %bitcast.20), calls=%async_computation.2 | async-start | bytes 1769472 | tf_op jit(solution)/shard_map/all_to_all | solution.py:543
  64.7 4.0 %collective-permute-start.4 = (f32[4,2,72,192]{3,2,1,0:T(8,128)S(1)}, f32[4,2,72,192]{3,2,1,0:T(8,128)}, u32[]{:S(2)}, u32[]{:S(2)}) collective-permute-start(f32[4,2,72,192]{3,2,1,0:T(8,128)S(1)} %pad_maximum_fusion), channel_id=1, source_target_pairs={{0,8},{2,10},{12,4},{14,6},{1,9},{3,11},{13,5},{15,7},{16,24},{18,... | collective-permute-start | bytes 1327112 | tf_op jit(solution)/shard_map/ppermute | solution.py:566
  80.1 22.5 %copy-start = (bf16[2,384,384]{2,1,0:T(8,128)(2,1)S(1)}, bf16[2,384,384]{2,1,0:T(8,128)(2,1)}, u32[]{:S(2)}) copy-start(bf16[2,384,384]{2,1,0:T(8,128)(2,1)} %constant.113.clone.matrix_hbm.matrix_ref) | copy-start | bytes 1769476
  80.1 22.5 %copy-start.6 = (bf16[2,384,192]{2,1,0:T(8,128)(2,1)S(1)}, bf16[2,384,192]{2,1,0:T(8,128)(2,1)}, u32[]{:S(2)}) copy-start(bf16[2,384,192]{2,1,0:T(8,128)(2,1)} %constant.112.clone.lift_ref) | copy-start | bytes 884740
  106.2 33.6 %copy-start.4 = (bf16[2,384,384]{2,1,0:T(8,128)(2,1)S(1)}, bf16[2,384,384]{2,1,0:T(8,128)(2,1)}, u32[]{:S(2)}) copy-start(bf16[2,384,384]{2,1,0:T(8,128)(2,1)} %constant.115.clone.back_hbm) | copy-start | bytes 1769476
  106.2 33.6 %copy-start.5 = (bf16[2,384,384]{2,1,0:T(8,128)(2,1)S(1)}, bf16[2,384,384]{2,1,0:T(8,128)(2,1)}, u32[]{:S(2)}) copy-start(bf16[2,384,384]{2,1,0:T(8,128)(2,1)} %constant.114.clone.out_hbm) | copy-start | bytes 1769476
  149.0 31.2 %copy-start.1 = (f32[48,24,384]{2,1,0:T(8,128)S(1)}, f32[48,24,384]{2,1,0:T(8,128)}, u32[]{:S(2)}) copy-start(f32[48,24,384]{2,1,0:T(8,128)} %param.16) | copy-start | bytes 5308420
  149.0 31.1 %copy-start.2 = (f32[384,1152]{1,0:T(8,128)S(1)}, f32[384,1152]{1,0:T(8,128)}, u32[]{:S(2)}) copy-start(f32[384,1152]{1,0:T(8,128)} %get-tuple-element.18.evolved_ref) | copy-start | bytes 5308420

commit v6 on v5

--- a/solution.py
+++ b/solution.py
@@ -83,7 +83,7 @@
 HC_WIDE2 = halves(np.pad(HC, ((0, 64), (0, 64))))
 EVOLVE2 = halves(EVOLVE)
 EVOLVE_Y2 = halves(np.pad(EVOLVE, ((0, 0), (0, 64))))
-EVOLVE_X2 = halves(np.concatenate([EVOLVE[PLANE, :]] * 2, axis=1))
+EVOLVE_X2 = halves(np.pad(EVOLVE[PLANE, :], ((0, 0), (0, 64))))
 LIFT_Z2 = halves(LIFT[BY_SLAB, :])
 LIFT_Y2 = np.stack(
     [
@@ -228,8 +228,23 @@
     )(in_hbm(wave), in_hbm(jnp.asarray(EVOLVE2)))
 
 
-def coarse_z_kernel(got_ref, ey_ref, ex_ref, matrix_ref, out_ref, plane_ref):
-    lane = lax.broadcasted_iota(jnp.int32, (64, 128), 1)
+def pack_rows(planes):
+    (a0, a1), (b0, b1), (c0, c1) = [tiles_of(plane) for plane in planes]
+    low = lax.broadcasted_iota(jnp.int32, a0.shape, 1) < 64
+    b0, b1 = pltpu.roll(b0, 64, 1), pltpu.roll(b1, 64, 1)
+    return [a0, jnp.where(low, a1, b0), jnp.where(low, b0, b1), c0, c1]
+
+
+def unpack_rows(tiles):
+    a0, mixed, b1, c0, c1 = tiles
+    low = lax.broadcasted_iota(jnp.int32, a0.shape, 1) < 64
+    b1 = pltpu.roll(b1, 64, 1)
+    b0 = jnp.where(low, pltpu.roll(mixed, 64, 1), b1)
+    return [jnp.concatenate(p, axis=1) for p in ((a0, mixed), (b0, b1), (c0, c1))]
+
+
+def coarse_z_kernel(place_ref, got_ref, ey_ref, ex_ref, matrix_ref, out_ref, plane_ref):
+    core = place_ref[0]
     for k in range(3):
         for g in range(2):
             rows = []
@@ -241,65 +256,56 @@
                 plane_ref[16 * i + 8 * g : 16 * i + 8 * g + 8, :] = row[:, :256]
         half = dot3(pair(ey_ref), split(plane_ref[...]), TURNED)
         evolved = dot3(split(half), pair(ex_ref))
-        density = evolved[:, :256] * evolved[:, :256]
-        turned = dot3(pair(matrix_ref), split(density))
-        for j in range(3):
-            f = tiles_of(turned[64 * j : 64 * j + 64, :])
-            e = tiles_of(evolved[64 * j : 64 * j + 64, :])
-            for t, tile in enumerate([f[0], jnp.where(lane < 64, f[1], e[1]), e[2]]):
-                out_ref[pl.ds(k * 9 + j * 3 + t, 64, stride=27), :] = tile
-
-
-def coarse_z(got):
+        turned = dot3(pair(matrix_ref), split(evolved * evolved))
+        mine = jnp.where(core == 0, turned, evolved)
+        for i, tile in enumerate(pack_rows([mine[64 * j : 64 * j + 64, :] for j in range(3)])):
+            out_ref[pl.ds(k * 5 + i, 64, stride=15), :] = tile
+
+
+def coarse_z(place, got):
     return pl.pallas_call(
         coarse_z_kernel,
-        out_shape=jax.ShapeDtypeStruct((1728, 128), F32),
-        compiler_params=LIMIT,
-        in_specs=[VMEM] * 4,
+        out_shape=jax.ShapeDtypeStruct((960, 128), F32),
+        compiler_params=LIMIT,
+        in_specs=[SMEM] + [VMEM] * 4,
         out_specs=VMEM,
         scratch_shapes=[pltpu.VMEM((NC, 256), F32)],
-    )(got, jnp.asarray(EVOLVE_Y2), jnp.asarray(EVOLVE_X2), jnp.asarray(HC2))
-
-
-def rows_of_plane(got_ref, base):
-    rows = []
-    for j in range(3):
-        tiles = [got_ref[pl.ds(base + 9 * j + t, 64, stride=27), :] for t in range(3)]
-        rows.append(jnp.concatenate(tiles, axis=1))
-    return jnp.concatenate(rows, axis=0)
+    )(place, got, jnp.asarray(EVOLVE_Y2), jnp.asarray(EVOLVE_X2), jnp.asarray(HC2))
 
 
 def coarse_y_kernel(place_ref, got_ref, matrix_ref, wide_ref, out_ref):
-    lane = lax.broadcasted_iota(jnp.int32, (NC, 128), 1)
+    core = place_ref[0]
     wx = squares(lax.broadcasted_iota(jnp.int32, (NC, 256), 0), NC, 2.0)
     wz = squares(lax.broadcasted_iota(jnp.int32, (NC, 256), 1), NC, 2.0)
+    parts = []
+    for j in range(3):
+        parts.append(unpack_rows([got_ref[pl.ds(5 * j + i, 64, stride=15), :] for i in range(5)]))
+    planes = []
     for k in range(3):
-        both = rows_of_plane(got_ref, 3 * k)
-        both = jnp.concatenate([both, jnp.zeros((64, 384), F32)], axis=0).T
-        mid = dot3(pair(matrix_ref), split(both[:NC, :]))
+        both = jnp.concatenate([part[k] for part in parts] + [jnp.zeros((64, 256), F32)], axis=0)
+        both = both.T[:NC, :]
+        mid = dot3(pair(matrix_ref), split(both))
         mid = dot3(split(mid), pair(wide_ref))
         wy = squares(jnp.full((1, 1), 64 * k + place_ref[3], jnp.int32), NC, 2.0)
         mid = mid * dipolar(wx, wy, wz, NC)
         mid = dot3(split(mid), pair(wide_ref))
-        q = tiles_of(dot3(pair(matrix_ref), split(mid)))
-        e = [pltpu.roll(tile, 64, 1) for tile in tiles_of(both[NC:, :])]
-        pieces = [q[0], jnp.where(lane < 64, q[1], e[0]), jnp.where(lane < 64, e[0], e[1])]
-        for t, tile in enumerate(pieces):
-            out_ref[pl.ds(3 * k + t, NC, stride=9), :] = tile
+        mid = dot3(pair(matrix_ref), split(mid))
+        planes.append(jnp.where(core == 0, mid, both))
+    for i, tile in enumerate(pack_rows(planes)):
+        out_ref[pl.ds(i, NC, stride=5), :] = tile
 
 
 def coarse_y(place, got):
     return pl.pallas_call(
         coarse_y_kernel,
-        out_shape=jax.ShapeDtypeStruct((1728, 128), F32),
+        out_shape=jax.ShapeDtypeStruct((960, 128), F32),
         compiler_params=LIMIT,
         in_specs=[SMEM] + [VMEM] * 3,
         out_specs=VMEM,
     )(place, got, jnp.asarray(HC2), jnp.asarray(HC_WIDE2))
 
 
-def coarse_x_kernel(place_ref, got_ref, potential_ref, matrix_ref, lz_ref, ly_ref, out_ref, lifted_ref):
-    lane = lax.broadcasted_iota(jnp.int32, (NC, 128), 1)
+def coarse_x_kernel(place_ref, got_ref, other_ref, potential_ref, matrix_ref, lz_ref, ly_ref, out_ref, lifted_ref):
     core = place_ref[0]
     slots = []
     for c in range(8):
@@ -308,14 +314,15 @@
     part = jnp.zeros((1, 1), F32)
     blank = jnp.zeros((8, 128), F32)
     for k in range(3):
-        rows = []
-        for j in range(3):
-            tiles = [got_ref[pl.ds(9 * k + 3 * j + t, 64, stride=27), :] for t in range(3)]
-            rows.append(jnp.concatenate(tiles, axis=1))
-        both = jnp.concatenate(rows, axis=0)
-        field = dot3(pair(matrix_ref), split(both[:, :256]))
-        e1, e2 = [pltpu.roll(tile, 64, 1) for tile in tiles_of(both)[1:]]
-        evolved = [jnp.where(lane < 64, e1, e2), e2[:, :64]]
+        fields, waves = [], []
+        for i in range(5):
+            rows = pl.ds(5 * k + i, 64, stride=15)
+            mine, other = got_ref[rows, :], other_ref[rows, :]
+            fields.append(jnp.where(core == 0, mine, other))
+            waves.append(jnp.where(core == 0, other, mine))
+        field = dot3(pair(matrix_ref), split(jnp.concatenate(unpack_rows(fields), axis=0)))
+        wave = jnp.concatenate(unpack_rows(waves), axis=0)
+        evolved = [wave[:, :128], wave[:, 128:NC]]
         pieces = []
         for t, e in enumerate(evolved):
             lanes = slice(128 * t, 128 * t + e.shape[1])
@@ -338,15 +345,15 @@
     out_ref[pl.ds(27, 64, stride=28), :] = jnp.broadcast_to(part, (64, 128))
 
 
-def coarse_x(place, got, potential):
+def coarse_x(place, got, other, potential):
     return pl.pallas_call(
         coarse_x_kernel,
         out_shape=jax.ShapeDtypeStruct((1792, 128), F32),
         compiler_params=LIMIT,
-        in_specs=[SMEM] + [VMEM] * 5,
+        in_specs=[SMEM] + [VMEM] * 6,
         out_specs=VMEM,
         scratch_shapes=[pltpu.VMEM((NF, 256), F32)],
-    )(place, got, potential, jnp.asarray(HC2), jnp.asarray(LIFT_Z2), jnp.asarray(LIFT_Y2))
+    )(place, got, other, potential, jnp.asarray(HC2), jnp.asarray(LIFT_Z2), jnp.asarray(LIFT_Y2))
 
 
 def fine_in_kernel(
@@ -485,7 +492,7 @@
             tiles = [got_ref[pl.ds(k * 9 + 3 * n + t, 128, stride=27), :] for t in range(3)]
             rows.append(jnp.concatenate(tiles, axis=1))
         field = dot3(pair(matrix_ref), split(jnp.concatenate(rows, axis=0)))
-        columns = pl.ds(pl.multiple_of(n * 384, 128), 384)
+        columns = pl.ds(n * 384, 384)
         evolved = evolved_ref[:, columns]
         potential = jnp.concatenate([potential_ref[block(n, p), :] for p in range(16)], axis=0).T
         exponent = -TIME_STEP * (potential + CONTACT * evolved * evolved + field)
@@ -496,7 +503,8 @@
             damped_ref[block(n, p), :] = turned[24 * p : 24 * p + 24, :]
         return carry
 
-    lax.fori_loop(0, 3, body, 0)
+    for n in range(3):
+        body(n, 0)
 
 
 def fine_out(place, got, evolved, potential):
@@ -576,10 +584,11 @@
 
     got = exchange(coarse_pencil(wave_coarse.reshape(288, NC)), ALL, 128).reshape(896, 128)
     got, planes = lax.optimization_barrier((got, swap_planes(potential_coarse, near)))
-    got = exchange(coarse_z(got), CHIPS, 64).reshape(1728, 128)
+    got = exchange(coarse_z(place, got), CHIPS, 64).reshape(960, 128)
     got, planes = lax.optimization_barrier((got, spread_planes(planes, across)))
-    got = exchange(coarse_y(place, got), CHIPS, 64).reshape(1728, 128)
-    turned = coarse_x(place, got, share_planes(planes, core, across))
+    got = exchange(coarse_y(place, got), CHIPS, 64).reshape(960, 128)
+    other = lax.ppermute(got, CORE, [(0, 1), (1, 0)])
+    turned = coarse_x(place, got, other, share_planes(planes, core, across))
     got = exchange(turned, CHIPS, 64).reshape(1792, 128)
 
     evolved, spectrum = fine_in(got)

time: 200 us -> 195 us (0.975)
  waiting for transfers between devices: 32.9 us -> 26.7 us
  starting transfers between devices: 35.9 us -> 39.6 us
    ppermute x3, waiting for transfers between devices: 6.23 us -> 2.23 us  [spread_planes(): chunk = lax.ppermute(chunk, (CORE, 'cols_0'), moves)]
    ppermute x0 -> x1, starting transfers between devices: none -> 3.14 us  [per_device(): other = lax.ppermute(got, CORE, [(0, 1), (1, 0)])]
    ppermute x1, waiting for transfers between devices: 2.71 us -> 0.01 us  [share_planes(): other = lax.ppermute(slots, (CORE, 'cols_0'), moves)]
  transfers between devices with their start and end apart: 8 -> 9, of which waited for: 6 -> 6; matrix products, arithmetic and copies ran while one was open for 1% -> 0% of each run, Pallas kernels for 0% -> 0%
where the time goes in v6:
time: 195 us; the launch traced here: 194 us
  blocking collectives  97.8 us (50%)
  starting transfers between devices  39.6 us (20%)
  Pallas kernels  29.6 us (15%)
  waiting for transfers between devices  26.7 us (14%)
    all_to_all x4, blocking collectives, exchange(): return lax.all_to_all(flat, axes, split_axis=0, concat_axis=0, tiled=False)  97.8 us
    all_to_all x3, starting transfers between devices, exchange(): return lax.all_to_all(flat, axes, split_axis=0, concat_axis=0, tiled=False)  27.4 us
    all_to_all x3, waiting for transfers between devices, exchange(): return lax.all_to_all(flat, axes, split_axis=0, concat_axis=0, tiled=False)  15.2 us
    pallas_call x1, Pallas kernels, fine_slab(): pl.pallas_call(fine_slab_kernel, out_shape=jax.ShapeDtypeStruct((3456, 12...  9.17 us
    ppermute x1, waiting for transfers between devices, swap_planes(): lax.ppermute(theirs, 'cols_1', [(0, 1), (1, 0)])  7.86 us
    ppermute x3, starting transfers between devices, spread_planes(): chunk = lax.ppermute(chunk, (CORE, 'cols_0'), moves)  6.39 us
  transfers between devices with their start and end apart: 9, of which 6 were waited for; matrix products, arithmetic and copies ran while one was open for 0% of the time, Pallas kernels for 0%

profile of v6, /device:TPU:1, one launch (start us, length us, event | category | flops | bytes accessed | tf_op | source)
XLA Modules:
  0.0 194.5 jit_solution(402874709651009835)
XLA Ops:
  0.0 2.5 %shard_map.136 = f32[896,128]{1,0:T(8,128)} custom-call(f32[288,192]{1,0:T(8,128)} %bitcast.54, bf16[2,192,192]{2,1,0:T(8,128)(2,1)} %constant.105.clone.matrix_hbm), custom_call_target="tpu_custom_call" | custom-call | tf_op jit(solution)/shard_map/pallas_call | solution.py:217
  2.5 11.5 %all-to-all-start = ((f32[128,1,896]{2,1,0:T(1,128)}), f32[128,1,896]{2,1,0:T(1,128)S(1)}, u32[]{:S(2)}, u32[]{:S(2)}) async-start(f32[128,1,896]{2,1,0:T(1,128)} %bitcast.7), calls=%async_computation | async-start | bytes 917504 | tf_op jit(solution)/shard_map/all_to_all | solution.py:551
  14.0 1.4 collective-permute-start
  15.5 7.9 %collective-permute-done = f32[2,72,192]{2,1,0:T(8,128)S(1)} collective-permute-done((f32[2,72,192]{2,1,0:T(8,128)S(1)}, f32[2,72,192]{2,1,0:T(8,128)S(1)}, u32[]{:S(2)}, u32[]{:S(2)}) %collective-permute-start) | collective-permute-done | bytes 110624 | tf_op jit(solution)/shard_map/ppermute | solution.py:558
  23.4 3.5 %all-to-all-done = f32[128,1,896]{2,1,0:T(1,128)S(1)} async-done(((f32[128,1,896]{2,1,0:T(1,128)}), f32[128,1,896]{2,1,0:T(1,128)S(1)}, u32[]{:S(2)}, u32[]{:S(2)}) %all-to-all-start) | async-done | bytes 458784 | tf_op jit(solution)/shard_map/all_to_all | solution.py:551
  26.9 3.2 %shard_map.137 = f32[960,128]{1,0:T(8,128)} custom-call(s32[6]{0:T(128)S(1)} %stack.47.place_ref, f32[896,128]{1,0:T(8,128)S(1)} %bitcast.48, bf16[2,192,256]{2,1,0:T(8,128)(2,1)S(1)} %copy-done.11, bf16[2,192,256]{2,1,0:T(8,128)(2,1)S(1)} %copy-done.10, bf16[2,192,192]{2,1,0:T(8,128)(2,1)S(1)} %copy-done.3), custom_call_target="tpu_custom_call" | custom-call | tf_op jit(solution)/shard_map/pallas_call | solution.py:266
  30.1 6.8 %all-to-all-start.1 = ((f32[64,1,1920]{2,1,0:T(1,128)}), f32[64,1,1920]{2,1,0:T(1,128)S(1)}, u32[]{:S(2)}, u32[]{:S(2)}) async-start(f32[64,1,1920]{2,1,0:T(1,128)} %bitcast.12), calls=%async_computation.1 | async-start | bytes 983040 | tf_op jit(solution)/shard_map/all_to_all | solution.py:551
  37.0 4.1 %collective-permute-start.3 = (f32[2,72,192]{2,1,0:T(8,128)S(1)}, f32[2,72,192]{2,1,0:T(8,128)S(1)}, u32[]{:S(2)}, u32[]{:S(2)}) collective-permute-start(f32[2,72,192]{2,1,0:T(8,128)S(1)} %get-tuple-element.22), channel_id=1, source_target_pairs={{2,0},{4,2},{14,12},{8,14},{3,1},{5,3},{15,13},{9,15},{18,16},{20,... | collective-permute-start | bytes 331784 | tf_op jit(solution)/shard_map/ppermute | solution.py:567
  41.2 1.6 collective-permute-start.2
  43.4 2.2 %collective-permute-done.3 = f32[2,72,192]{2,1,0:T(8,128)S(1)} collective-permute-done((f32[2,72,192]{2,1,0:T(8,128)S(1)}, f32[2,72,192]{2,1,0:T(8,128)S(1)}, u32[]{:S(2)}, u32[]{:S(2)}) %collective-permute-start.3) | collective-permute-done | bytes 110624 | tf_op jit(solution)/shard_map/ppermute | solution.py:567
  45.7 2.4 %all-to-all-done.1 = f32[64,1,1920]{2,1,0:T(1,128)S(1)} async-done(((f32[64,1,1920]{2,1,0:T(1,128)}), f32[64,1,1920]{2,1,0:T(1,128)S(1)}, u32[]{:S(2)}, u32[]{:S(2)}) %all-to-all-start.1) | async-done | bytes 491552 | tf_op jit(solution)/shard_map/all_to_all | solution.py:551
  48.1 3.7 %shard_map.138 = f32[960,128]{1,0:T(8,128)} custom-call(s32[6]{0:T(128)S(1)} %stack.47.place_ref, f32[960,128]{1,0:T(8,128)S(1)} %bitcast.47, bf16[2,192,192]{2,1,0:T(8,128)(2,1)S(1)} %copy-done.3, bf16[2,256,256]{2,1,0:T(8,128)(2,1)S(1)} %copy-done.9), custom_call_target="tpu_custom_call" | custom-call | tf_op jit(solution)/shard_map/pallas_call | solution.py:299
  51.8 9.1 %all-to-all-start.2 = ((f32[64,1,1920]{2,1,0:T(1,128)}), f32[64,1,1920]{2,1,0:T(1,128)S(1)}, u32[]{:S(2)}, u32[]{:S(2)}) async-start(f32[64,1,1920]{2,1,0:T(1,128)} %bitcast.20), calls=%async_computation.2 | async-start | bytes 983040 | tf_op jit(solution)/shard_map/all_to_all | solution.py:551
  62.2 9.3 %all-to-all-done.2 = f32[64,1,1920]{2,1,0:T(1,128)S(1)} async-done(((f32[64,1,1920]{2,1,0:T(1,128)}), f32[64,1,1920]{2,1,0:T(1,128)S(1)}, u32[]{:S(2)}, u32[]{:S(2)}) %all-to-all-start.2) | async-done | bytes 491552 | tf_op jit(solution)/shard_map/all_to_all | solution.py:551
  71.5 3.1 %collective-permute-start.4 = (f32[960,128]{1,0:T(8,128)S(1)}, f32[960,128]{1,0:T(8,128)S(1)}, u32[]{:S(2)}, u32[]{:S(2)}) collective-permute-start(f32[960,128]{1,0:T(8,128)S(1)} %bitcast.45), channel_id=1, source_target_pairs={{0,8},{8,0},{1,9},{9,1},{2,10},{10,2},{3,11},{11,3},{4,12},{12,4},... | collective-permute-start | bytes 1474568 | tf_op jit(solution)/shard_map/ppermute | solution.py:590
  74.8 1.4 collective-permute-done.4.other_ref
  76.2 3.3 %shard_map.139 = f32[1792,128]{1,0:T(8,128)S(1)} custom-call(s32[6]{0:T(128)S(1)} %stack.47.place_ref, f32[960,128]{1,0:T(8,128)S(1)} %bitcast.46, f32[960,128]{1,0:T(8,128)S(1)} %collective-permute-done.4.other_ref, f32[8,72,192]{2,1,0:T(8,128)S(1)} %bitcast.44, bf16[2,192,192]{2,1,0:T(8,128)(2,1)S(1)} %copy-done.3, bf16[2,384,192]{2,1,0:T(8,128)(2,1)S(1)} %copy-done.8, ...), custom_call_target="tpu_custom_call" | custom-call | tf_op jit(solution)/shard_map/pallas_call | solution.py:349
  79.5 20.5 %all_to_all.35 = f32[64,1,3584]{2,1,0:T(1,128)S(1)} all-to-all(f32[64,1,3584]{2,1,0:T(1,128)S(1)} %bitcast.42), channel_id=1, replica_groups=mesh['rows_0'=4,'rows_1'=2,'rows_2'=2,'cols_0'=4,'cols_1'=2] {'rows_0','..., dimensions={0} | all-to-all | bytes 1835008 | tf_op jit(solution)/shard_map/all_to_all | solution.py:551
  100.0 3.6 %shard_map.140 = (f32[384,1152]{1,0:T(8,128)}, f32[3456,128]{1,0:T(8,128)S(1)}) custom-call(f32[1792,128]{1,0:T(8,128)S(1)} %bitcast.43, bf16[2,384,192]{2,1,0:T(8,128)(2,1)S(1)} %copy-done.6, bf16[2,384,384]{2,1,0:T(8,128)(2,1)S(1)} %copy-done), custom_call_target="tpu_custom_call" | custom-call | tf_op jit(solution)/shard_map/pallas_call | solution.py:397
  103.6 32.0 %all_to_all.36 = f32[128,1,3456]{2,1,0:T(1,128)S(1)} all-to-all(f32[128,1,3456]{2,1,0:T(1,128)S(1)} %bitcast.50), channel_id=1, replica_groups=mesh['rows_0'=4,'rows_1'=2,'rows_2'=2,'cols_0'=4,'cols_1'=2] {'rows_0','..., dimensions={0} | all-to-all | bytes 3538944 | tf_op jit(solution)/shard_map/all_to_all | solution.py:551
  135.6 9.2 %shard_map.141 = f32[3456,128]{1,0:T(8,128)S(1)} custom-call(s32[6]{0:T(128)S(1)} %stack.47.place_ref, f32[3456,128]{1,0:T(8,128)S(1)} %bitcast.40, bf16[2,384,384]{2,1,0:T(8,128)(2,1)S(1)} %copy-done.5, bf16[2,384,384]{2,1,0:T(8,128)(2,1)S(1)} %copy-done.4, bf16[2,384,384]{2,1,0:T(8,128)(2,1)S(1)} %copy-done), custom_call_target="tpu_custom_call" | custom-call | tf_op jit(solution)/shard_map/pallas_call | solution.py:465
  144.8 31.1 %all_to_all.37 = f32[128,1,3456]{2,1,0:T(1,128)S(1)} all-to-all(f32[128,1,3456]{2,1,0:T(1,128)S(1)} %bitcast.41), channel_id=1, replica_groups=mesh['rows_0'=4,'rows_1'=2,'rows_2'=2,'cols_0'=4,'cols_1'=2] {'rows_0','..., dimensions={0} | all-to-all | bytes 3538944 | tf_op jit(solution)/shard_map/all_to_all | solution.py:551
  175.9 2.9 %shard_map.142 = (f32[1152,384]{1,0:T(8,128)S(1)}, f32[128,128]{1,0:T(8,128)S(1)}) custom-call(s32[6]{0:T(128)S(1)} %stack.47.place_ref, f32[3456,128]{1,0:T(8,128)S(1)} %bitcast.39, f32[384,1152]{1,0:T(8,128)S(1)} %copy-done.2, f32[1152,384]{1,0:T(8,128)S(1)} %bitcast.49, bf16[2,384,384]{2,1,0:T(8,128)(2,1)S(1)} %copy-done), custom_call_target="tpu_custom_call" | custom-call | tf_op jit(solution)/shard_map/pallas_call | solution.py:511
  178.8 14.2 %all_to_all.38 = f32[128,1,128]{2,1,0:T(1,128)S(1)} all-to-all(f32[128,1,128]{2,1,0:T(1,128)S(1)} %bitcast.52), channel_id=1, replica_groups=mesh['rows_0'=4,'rows_1'=2,'rows_2'=2,'cols_0'=4,'cols_1'=2] {'rows_0','..., dimensions={0} | all-to-all | bytes 131072 | tf_op jit(solution)/shard_map/all_to_all | solution.py:551
  (38 shorter events, 3.7 us)
Async XLA Ops:
  0.0 26.9 %copy-start.3 = (bf16[2,192,192]{2,1,0:T(8,128)(2,1)S(1)}, bf16[2,192,192]{2,1,0:T(8,128)(2,1)}, u32[]{:S(2)}) copy-start(bf16[2,192,192]{2,1,0:T(8,128)(2,1)} %constant.108.clone.matrix_ref) | copy-start | bytes 442372
  0.0 26.9 %copy-start.10 = (bf16[2,192,256]{2,1,0:T(8,128)(2,1)S(1)}, bf16[2,192,256]{2,1,0:T(8,128)(2,1)}, u32[]{:S(2)}) copy-start(bf16[2,192,256]{2,1,0:T(8,128)(2,1)} %constant.107.clone.ex_ref) | copy-start | bytes 589828
  0.0 26.9 %copy-start.11 = (bf16[2,192,256]{2,1,0:T(8,128)(2,1)S(1)}, bf16[2,192,256]{2,1,0:T(8,128)(2,1)}, u32[]{:S(2)}) copy-start(bf16[2,192,256]{2,1,0:T(8,128)(2,1)} %constant.106.clone.ey_ref) | copy-start | bytes 589828
  0.0 14.0 %copy-start.12 = (f32[12,24,192]{2,1,0:T(8,128)S(1)}, f32[12,24,192]{2,1,0:T(8,128)}, u32[]{:S(2)}) copy-start(f32[12,24,192]{2,1,0:T(8,128)} %param.15) | copy-start | bytes 663556
  2.5 24.4 %all-to-all-start = ((f32[128,1,896]{2,1,0:T(1,128)}), f32[128,1,896]{2,1,0:T(1,128)S(1)}, u32[]{:S(2)}, u32[]{:S(2)}) async-start(f32[128,1,896]{2,1,0:T(1,128)} %bitcast.7), calls=%async_computation | async-start | bytes 917504 | tf_op jit(solution)/shard_map/all_to_all | solution.py:551
  14.0 9.4 %collective-permute-start = (f32[2,72,192]{2,1,0:T(8,128)S(1)}, f32[2,72,192]{2,1,0:T(8,128)S(1)}, u32[]{:S(2)}, u32[]{:S(2)}) collective-permute-start(f32[2,72,192]{2,1,0:T(8,128)S(1)} %get-tuple-element.26), channel_id=1, source_target_pairs={{0,1},{1,0},{2,3},{3,2},{4,5},{5,4},{6,7},{7,6},{8,9},{9,8},{10,11... | collective-permute-start | bytes 331784 | tf_op jit(solution)/shard_map/ppermute | solution.py:558
  30.1 18.0 %copy-start.9 = (bf16[2,256,256]{2,1,0:T(8,128)(2,1)S(1)}, bf16[2,256,256]{2,1,0:T(8,128)(2,1)}, u32[]{:S(2)}) copy-start(bf16[2,256,256]{2,1,0:T(8,128)(2,1)} %constant.109.clone.wide_ref) | copy-start | bytes 786436
  30.1 18.0 %all-to-all-start.1 = ((f32[64,1,1920]{2,1,0:T(1,128)}), f32[64,1,1920]{2,1,0:T(1,128)S(1)}, u32[]{:S(2)}, u32[]{:S(2)}) async-start(f32[64,1,1920]{2,1,0:T(1,128)} %bitcast.12), calls=%async_computation.1 | async-start | bytes 983040 | tf_op jit(solution)/shard_map/all_to_all | solution.py:551
  37.0 8.6 %collective-permute-start.3 = (f32[2,72,192]{2,1,0:T(8,128)S(1)}, f32[2,72,192]{2,1,0:T(8,128)S(1)}, u32[]{:S(2)}, u32[]{:S(2)}) collective-permute-start(f32[2,72,192]{2,1,0:T(8,128)S(1)} %get-tuple-element.22), channel_id=1, source_target_pairs={{2,0},{4,2},{14,12},{8,14},{3,1},{5,3},{15,13},{9,15},{18,16},{20,... | collective-permute-start | bytes 331784 | tf_op jit(solution)/shard_map/ppermute | solution.py:567
  41.2 4.5 %collective-permute-start.2 = (f32[2,72,192]{2,1,0:T(8,128)S(1)}, f32[2,72,192]{2,1,0:T(8,128)S(1)}, u32[]{:S(2)}, u32[]{:S(2)}) collective-permute-start(f32[2,72,192]{2,1,0:T(8,128)S(1)} %get-tuple-element.23), channel_id=1, source_target_pairs={{4,0},{6,2},{8,12},{10,14},{5,1},{7,3},{9,13},{11,15},{20,16},{22,... | collective-permute-start | bytes 331784 | tf_op jit(solution)/shard_map/ppermute | solution.py:567
  42.7 2.9 %collective-permute-start.1 = (f32[2,72,192]{2,1,0:T(8,128)S(1)}, f32[2,72,192]{2,1,0:T(8,128)S(1)}, u32[]{:S(2)}, u32[]{:S(2)}) collective-permute-start(f32[2,72,192]{2,1,0:T(8,128)S(1)} %get-tuple-element.24), channel_id=1, source_target_pairs={{6,0},{0,2},{10,12},{12,14},{7,1},{1,3},{11,13},{13,15},{22,16},{1... | collective-permute-start | bytes 331784 | tf_op jit(solution)/shard_map/ppermute | solution.py:567
  48.1 28.1 %copy-start.7 = (bf16[2,2,192,256]{3,2,1,0:T(8,128)(2,1)S(1)}, bf16[2,2,192,256]{3,2,1,0:T(8,128)(2,1)}, u32[]{:S(2)}) copy-start(bf16[2,2,192,256]{3,2,1,0:T(8,128)(2,1)} %constant.111.clone.ly_ref) | copy-start | bytes 1179652
  48.1 28.1 %copy-start.8 = (bf16[2,384,192]{2,1,0:T(8,128)(2,1)S(1)}, bf16[2,384,192]{2,1,0:T(8,128)(2,1)}, u32[]{:S(2)}) copy-start(bf16[2,384,192]{2,1,0:T(8,128)(2,1)} %constant.110.clone.lz_ref) | copy-start | bytes 884740
  51.8 19.7 %all-to-all-start.2 = ((f32[64,1,1920]{2,1,0:T(1,128)}), f32[64,1,1920]{2,1,0:T(1,128)S(1)}, u32[]{:S(2)}, u32[]{:S(2)}) async-start(f32[64,1,1920]{2,1,0:T(1,128)} %bitcast.20), calls=%async_computation.2 | async-start | bytes 983040 | tf_op jit(solution)/shard_map/all_to_all | solution.py:551
  60.9 13.8 %collective-permute-start.5 = (f32[4,2,72,192]{3,2,1,0:T(8,128)S(1)}, f32[4,2,72,192]{3,2,1,0:T(8,128)S(1)}, u32[]{:S(2)}, u32[]{:S(2)}) collective-permute-start(f32[4,2,72,192]{3,2,1,0:T(8,128)S(1)} %pad_maximum_fusion), channel_id=1, source_target_pairs={{0,8},{2,10},{12,4},{14,6},{1,9},{3,11},{13,5},{15,7},{16,24},{18,... | collective-permute-start | bytes 1327112 | tf_op jit(solution)/shard_map/ppermute | solution.py:574
  71.5 4.6 %collective-permute-start.4 = (f32[960,128]{1,0:T(8,128)S(1)}, f32[960,128]{1,0:T(8,128)S(1)}, u32[]{:S(2)}, u32[]{:S(2)}) collective-permute-start(f32[960,128]{1,0:T(8,128)S(1)} %bitcast.45), channel_id=1, source_target_pairs={{0,8},{8,0},{1,9},{9,1},{2,10},{10,2},{3,11},{11,3},{4,12},{12,4},... | collective-permute-start | bytes 1474568 | tf_op jit(solution)/shard_map/ppermute | solution.py:590
  79.5 20.5 %copy-start = (bf16[2,384,384]{2,1,0:T(8,128)(2,1)S(1)}, bf16[2,384,384]{2,1,0:T(8,128)(2,1)}, u32[]{:S(2)}) copy-start(bf16[2,384,384]{2,1,0:T(8,128)(2,1)} %constant.113.clone.matrix_hbm.matrix_ref) | copy-start | bytes 1769476
  79.5 20.5 %copy-start.6 = (bf16[2,384,192]{2,1,0:T(8,128)(2,1)S(1)}, bf16[2,384,192]{2,1,0:T(8,128)(2,1)}, u32[]{:S(2)}) copy-start(bf16[2,384,192]{2,1,0:T(8,128)(2,1)} %constant.112.clone.lift_ref) | copy-start | bytes 884740
  103.6 32.0 %copy-start.4 = (bf16[2,384,384]{2,1,0:T(8,128)(2,1)S(1)}, bf16[2,384,384]{2,1,0:T(8,128)(2,1)}, u32[]{:S(2)}) copy-start(bf16[2,384,384]{2,1,0:T(8,128)(2,1)} %constant.115.clone.back_hbm) | copy-start | bytes 1769476
  103.6 32.0 %copy-start.5 = (bf16[2,384,384]{2,1,0:T(8,128)(2,1)S(1)}, bf16[2,384,384]{2,1,0:T(8,128)(2,1)}, u32[]{:S(2)}) copy-start(bf16[2,384,384]{2,1,0:T(8,128)(2,1)} %constant.114.clone.out_hbm) | copy-start | bytes 1769476
  144.8 31.2 %copy-start.1 = (f32[48,24,384]{2,1,0:T(8,128)S(1)}, f32[48,24,384]{2,1,0:T(8,128)}, u32[]{:S(2)}) copy-start(f32[48,24,384]{2,1,0:T(8,128)} %param.16) | copy-start | bytes 5308420
  144.8 31.1 %copy-start.2 = (f32[384,1152]{1,0:T(8,128)S(1)}, f32[384,1152]{1,0:T(8,128)}, u32[]{:S(2)}) copy-start(f32[384,1152]{1,0:T(8,128)} %get-tuple-element.18.evolved_ref) | copy-start | bytes 5308420

commit v7 on v6

--- a/solution.py
+++ b/solution.py
@@ -552,10 +552,12 @@
 
 
 def swap_planes(potential, near):
-    planes = potential.reshape(2, 2, 72, NC)
-    mine = lax.dynamic_index_in_dim(planes, near, 1, keepdims=False)
-    theirs = lax.dynamic_index_in_dim(planes, 1 - near, 1, keepdims=False)
-    return jnp.stack([mine, lax.ppermute(theirs, "cols_1", [(0, 1), (1, 0)])], axis=1)
+    other = lax.ppermute(potential, "cols_1", [(0, 1), (1, 0)])
+    planes = [
+        lax.dynamic_index_in_dim(held.reshape(2, 2, 72, NC), near, 1, keepdims=False)
+        for held in (potential, other)
+    ]
+    return jnp.stack(planes, axis=1)
 
 
 def spread_planes(planes, across):

time: 195 us -> 195 us (level)
  starting transfers between devices: 39.6 us -> 36.6 us
  waiting for transfers between devices: 26.7 us -> 29.5 us
    all_to_all x3, waiting for transfers between devices: 15.2 us -> 25.5 us  [exchange(): return lax.all_to_all(flat, axes, split_axis=0, concat_axis=0, tiled=False)]
    ppermute x1, waiting for transfers between devices: 7.86 us -> 0.01 us  [swap_planes(): other = lax.ppermute(potential, 'cols_1', [(0, 1), (1, 0)])]
    all_to_all x3, starting transfers between devices: 27.4 us -> 24.2 us  [exchange(): return lax.all_to_all(flat, axes, split_axis=0, concat_axis=0, tiled=False)]
  transfers between devices with their start and end apart: 9 -> 9, of which waited for: 6 -> 5; matrix products, arithmetic and copies ran while one was open for 0% -> 0% of each run, Pallas kernels for 0% -> 1%
where the time goes in v7:
time: 195 us; the launch traced here: 194 us
  blocking collectives  97.8 us (50%)
  starting transfers between devices  36.6 us (19%)
  Pallas kernels  29.5 us (15%)
  waiting for transfers between devices  29.5 us (15%)
    all_to_all x4, blocking collectives, exchange(): return lax.all_to_all(flat, axes, split_axis=0, concat_axis=0, tiled=False)  97.8 us
    all_to_all x3, waiting for transfers between devices, exchange(): return lax.all_to_all(flat, axes, split_axis=0, concat_axis=0, tiled=False)  25.5 us
    all_to_all x3, starting transfers between devices, exchange(): return lax.all_to_all(flat, axes, split_axis=0, concat_axis=0, tiled=False)  24.2 us
    pallas_call x1, Pallas kernels, fine_slab(): pl.pallas_call(fine_slab_kernel, out_shape=jax.ShapeDtypeStruct((3456, 12...  9.17 us
    ppermute x3, starting transfers between devices, spread_planes(): chunk = lax.ppermute(chunk, (CORE, 'cols_0'), moves)  6.39 us
  transfers between devices with their start and end apart: 9, of which 5 were waited for; matrix products, arithmetic and copies ran while one was open for 0% of the time, Pallas kernels for 1%

profile of v7, /device:TPU:1, one launch (start us, length us, event | category | flops | bytes accessed | tf_op | source)
XLA Modules:
  0.0 194.2 jit_solution(1214055971668611967)
XLA Ops:
  0.0 2.1 %collective-permute-start = (f32[12,24,192]{2,1,0:T(8,128)}, f32[12,24,192]{2,1,0:T(8,128)S(1)}, u32[]{:S(2)}, u32[]{:S(2)}) collective-permute-start(f32[12,24,192]{2,1,0:T(8,128)} %param.15), channel_id=1, source_target_pairs={{0,1},{1,0},{2,3},{3,2},{4,5},{5,4},{6,7},{7,6},{8,9},{9,8},{10,11... | collective-permute-start | bytes 663560 | tf_op jit(solution)/shard_map/ppermute | solution.py:555
  2.1 2.4 %shard_map.136 = f32[896,128]{1,0:T(8,128)} custom-call(f32[288,192]{1,0:T(8,128)} %bitcast.51, bf16[2,192,192]{2,1,0:T(8,128)(2,1)} %constant.104.clone.matrix_hbm), custom_call_target="tpu_custom_call" | custom-call | tf_op jit(solution)/shard_map/pallas_call | solution.py:217
  4.5 10.7 %all-to-all-start = ((f32[128,1,896]{2,1,0:T(1,128)}), f32[128,1,896]{2,1,0:T(1,128)S(1)}, u32[]{:S(2)}, u32[]{:S(2)}) async-start(f32[128,1,896]{2,1,0:T(1,128)} %bitcast.7), calls=%async_computation | async-start | bytes 917504 | tf_op jit(solution)/shard_map/all_to_all | solution.py:551
  15.4 12.7 %all-to-all-done = f32[128,1,896]{2,1,0:T(1,128)S(1)} async-done(((f32[128,1,896]{2,1,0:T(1,128)}), f32[128,1,896]{2,1,0:T(1,128)S(1)}, u32[]{:S(2)}, u32[]{:S(2)}) %all-to-all-start) | async-done | bytes 458784 | tf_op jit(solution)/shard_map/all_to_all | solution.py:551
  28.1 3.2 %shard_map.137 = f32[960,128]{1,0:T(8,128)} custom-call(s32[6]{0:T(128)S(1)} %stack.45.place_ref, f32[896,128]{1,0:T(8,128)S(1)} %bitcast.46, bf16[2,192,256]{2,1,0:T(8,128)(2,1)S(1)} %copy-done.11, bf16[2,192,256]{2,1,0:T(8,128)(2,1)S(1)} %copy-done.10, bf16[2,192,192]{2,1,0:T(8,128)(2,1)S(1)} %copy-done.3), custom_call_target="tpu_custom_call" | custom-call | tf_op jit(solution)/shard_map/pallas_call | solution.py:266
  31.3 5.3 %all-to-all-start.1 = ((f32[64,1,1920]{2,1,0:T(1,128)}), f32[64,1,1920]{2,1,0:T(1,128)S(1)}, u32[]{:S(2)}, u32[]{:S(2)}) async-start(f32[64,1,1920]{2,1,0:T(1,128)} %bitcast.11), calls=%async_computation.1 | async-start | bytes 983040 | tf_op jit(solution)/shard_map/all_to_all | solution.py:551
  36.7 4.1 %collective-permute-start.3 = (f32[2,72,192]{2,1,0:T(8,128)S(1)}, f32[2,72,192]{2,1,0:T(8,128)S(1)}, u32[]{:S(2)}, u32[]{:S(2)}) collective-permute-start(f32[2,72,192]{2,1,0:T(8,128)S(1)} %get-tuple-element.22), channel_id=1, source_target_pairs={{2,0},{4,2},{14,12},{8,14},{3,1},{5,3},{15,13},{9,15},{18,16},{20,... | collective-permute-start | bytes 331784 | tf_op jit(solution)/shard_map/ppermute | solution.py:569
  40.8 1.6 collective-permute-start.2
  43.1 2.5 %collective-permute-done.3 = f32[2,72,192]{2,1,0:T(8,128)S(1)} collective-permute-done((f32[2,72,192]{2,1,0:T(8,128)S(1)}, f32[2,72,192]{2,1,0:T(8,128)S(1)}, u32[]{:S(2)}, u32[]{:S(2)}) %collective-permute-start.3) | collective-permute-done | bytes 110624 | tf_op jit(solution)/shard_map/ppermute | solution.py:569
  45.7 2.9 %all-to-all-done.1 = f32[64,1,1920]{2,1,0:T(1,128)S(1)} async-done(((f32[64,1,1920]{2,1,0:T(1,128)}), f32[64,1,1920]{2,1,0:T(1,128)S(1)}, u32[]{:S(2)}, u32[]{:S(2)}) %all-to-all-start.1) | async-done | bytes 491552 | tf_op jit(solution)/shard_map/all_to_all | solution.py:551
  48.6 3.7 %shard_map.138 = f32[960,128]{1,0:T(8,128)} custom-call(s32[6]{0:T(128)S(1)} %stack.45.place_ref, f32[960,128]{1,0:T(8,128)S(1)} %bitcast.45, bf16[2,192,192]{2,1,0:T(8,128)(2,1)S(1)} %copy-done.3, bf16[2,256,256]{2,1,0:T(8,128)(2,1)S(1)} %copy-done.9), custom_call_target="tpu_custom_call" | custom-call | tf_op jit(solution)/shard_map/pallas_call | solution.py:299
  52.3 8.3 %all-to-all-start.2 = ((f32[64,1,1920]{2,1,0:T(1,128)}), f32[64,1,1920]{2,1,0:T(1,128)S(1)}, u32[]{:S(2)}, u32[]{:S(2)}) async-start(f32[64,1,1920]{2,1,0:T(1,128)} %bitcast.19), calls=%async_computation.2 | async-start | bytes 983040 | tf_op jit(solution)/shard_map/all_to_all | solution.py:551
  61.9 9.9 %all-to-all-done.2 = f32[64,1,1920]{2,1,0:T(1,128)S(1)} async-done(((f32[64,1,1920]{2,1,0:T(1,128)}), f32[64,1,1920]{2,1,0:T(1,128)S(1)}, u32[]{:S(2)}, u32[]{:S(2)}) %all-to-all-start.2) | async-done | bytes 491552 | tf_op jit(solution)/shard_map/all_to_all | solution.py:551
  71.8 2.6 %collective-permute-start.4 = (f32[960,128]{1,0:T(8,128)S(1)}, f32[960,128]{1,0:T(8,128)S(1)}, u32[]{:S(2)}, u32[]{:S(2)}) collective-permute-start(f32[960,128]{1,0:T(8,128)S(1)} %bitcast.43), channel_id=1, source_target_pairs={{0,8},{8,0},{1,9},{9,1},{2,10},{10,2},{3,11},{11,3},{4,12},{12,4},... | collective-permute-start | bytes 1474568 | tf_op jit(solution)/shard_map/ppermute | solution.py:592
  74.5 1.4 collective-permute-done.4.other_ref
  75.9 3.3 %shard_map.139 = f32[1792,128]{1,0:T(8,128)S(1)} custom-call(s32[6]{0:T(128)S(1)} %stack.45.place_ref, f32[960,128]{1,0:T(8,128)S(1)} %bitcast.44, f32[960,128]{1,0:T(8,128)S(1)} %collective-permute-done.4.other_ref, f32[8,72,192]{2,1,0:T(8,128)S(1)} %bitcast.42, bf16[2,192,192]{2,1,0:T(8,128)(2,1)S(1)} %copy-done.3, bf16[2,384,192]{2,1,0:T(8,128)(2,1)S(1)} %copy-done.8, ...), custom_call_target="tpu_custom_call" | custom-call | tf_op jit(solution)/shard_map/pallas_call | solution.py:349
  79.2 20.5 %all_to_all.35 = f32[64,1,3584]{2,1,0:T(1,128)S(1)} all-to-all(f32[64,1,3584]{2,1,0:T(1,128)S(1)} %bitcast.40), channel_id=1, replica_groups=mesh['rows_0'=4,'rows_1'=2,'rows_2'=2,'cols_0'=4,'cols_1'=2] {'rows_0','..., dimensions={0} | all-to-all | bytes 1835008 | tf_op jit(solution)/shard_map/all_to_all | solution.py:551
  99.7 3.6 %shard_map.140 = (f32[384,1152]{1,0:T(8,128)}, f32[3456,128]{1,0:T(8,128)S(1)}) custom-call(f32[1792,128]{1,0:T(8,128)S(1)} %bitcast.41, bf16[2,384,192]{2,1,0:T(8,128)(2,1)S(1)} %copy-done.6, bf16[2,384,384]{2,1,0:T(8,128)(2,1)S(1)} %copy-done), custom_call_target="tpu_custom_call" | custom-call | tf_op jit(solution)/shard_map/pallas_call | solution.py:397
  103.3 32.0 %all_to_all.36 = f32[128,1,3456]{2,1,0:T(1,128)S(1)} all-to-all(f32[128,1,3456]{2,1,0:T(1,128)S(1)} %bitcast.48), channel_id=1, replica_groups=mesh['rows_0'=4,'rows_1'=2,'rows_2'=2,'cols_0'=4,'cols_1'=2] {'rows_0','..., dimensions={0} | all-to-all | bytes 3538944 | tf_op jit(solution)/shard_map/all_to_all | solution.py:551
  135.3 9.2 %shard_map.141 = f32[3456,128]{1,0:T(8,128)S(1)} custom-call(s32[6]{0:T(128)S(1)} %stack.45.place_ref, f32[3456,128]{1,0:T(8,128)S(1)} %bitcast.38, bf16[2,384,384]{2,1,0:T(8,128)(2,1)S(1)} %copy-done.5, bf16[2,384,384]{2,1,0:T(8,128)(2,1)S(1)} %copy-done.4, bf16[2,384,384]{2,1,0:T(8,128)(2,1)S(1)} %copy-done), custom_call_target="tpu_custom_call" | custom-call | tf_op jit(solution)/shard_map/pallas_call | solution.py:465
  144.5 31.1 %all_to_all.37 = f32[128,1,3456]{2,1,0:T(1,128)S(1)} all-to-all(f32[128,1,3456]{2,1,0:T(1,128)S(1)} %bitcast.39), channel_id=1, replica_groups=mesh['rows_0'=4,'rows_1'=2,'rows_2'=2,'cols_0'=4,'cols_1'=2] {'rows_0','..., dimensions={0} | all-to-all | bytes 3538944 | tf_op jit(solution)/shard_map/all_to_all | solution.py:551
  175.6 2.9 %shard_map.142 = (f32[1152,384]{1,0:T(8,128)S(1)}, f32[128,128]{1,0:T(8,128)S(1)}) custom-call(s32[6]{0:T(128)S(1)} %stack.45.place_ref, f32[3456,128]{1,0:T(8,128)S(1)} %bitcast.37, f32[384,1152]{1,0:T(8,128)S(1)} %copy-done.2, f32[1152,384]{1,0:T(8,128)S(1)} %bitcast.47, bf16[2,384,384]{2,1,0:T(8,128)(2,1)S(1)} %copy-done), custom_call_target="tpu_custom_call" | custom-call | tf_op jit(solution)/shard_map/pallas_call | solution.py:511
  178.5 14.2 %all_to_all.38 = f32[128,1,128]{2,1,0:T(1,128)S(1)} all-to-all(f32[128,1,128]{2,1,0:T(1,128)S(1)} %bitcast.50), channel_id=1, replica_groups=mesh['rows_0'=4,'rows_1'=2,'rows_2'=2,'cols_0'=4,'cols_1'=2] {'rows_0','..., dimensions={0} | all-to-all | bytes 131072 | tf_op jit(solution)/shard_map/all_to_all | solution.py:551
  192.7 1.3 shard_map.143
  (39 shorter events, 2.3 us)
Async XLA Ops:
  0.0 28.1 %copy-start.3 = (bf16[2,192,192]{2,1,0:T(8,128)(2,1)S(1)}, bf16[2,192,192]{2,1,0:T(8,128)(2,1)}, u32[]{:S(2)}) copy-start(bf16[2,192,192]{2,1,0:T(8,128)(2,1)} %constant.107.clone.matrix_ref) | copy-start | bytes 442372
  0.0 28.1 %copy-start.10 = (bf16[2,192,256]{2,1,0:T(8,128)(2,1)S(1)}, bf16[2,192,256]{2,1,0:T(8,128)(2,1)}, u32[]{:S(2)}) copy-start(bf16[2,192,256]{2,1,0:T(8,128)(2,1)} %constant.106.clone.ex_ref) | copy-start | bytes 589828
  0.0 28.1 %copy-start.11 = (bf16[2,192,256]{2,1,0:T(8,128)(2,1)S(1)}, bf16[2,192,256]{2,1,0:T(8,128)(2,1)}, u32[]{:S(2)}) copy-start(bf16[2,192,256]{2,1,0:T(8,128)(2,1)} %constant.105.clone.ey_ref) | copy-start | bytes 589828
  0.0 15.3 %copy-start.12 = (f32[12,24,192]{2,1,0:T(8,128)S(1)}, f32[12,24,192]{2,1,0:T(8,128)}, u32[]{:S(2)}) copy-start(f32[12,24,192]{2,1,0:T(8,128)} %param.15) | copy-start | bytes 663556
  0.0 15.3 %collective-permute-start = (f32[12,24,192]{2,1,0:T(8,128)}, f32[12,24,192]{2,1,0:T(8,128)S(1)}, u32[]{:S(2)}, u32[]{:S(2)}) collective-permute-start(f32[12,24,192]{2,1,0:T(8,128)} %param.15), channel_id=1, source_target_pairs={{0,1},{1,0},{2,3},{3,2},{4,5},{5,4},{6,7},{7,6},{8,9},{9,8},{10,11... | collective-permute-start | bytes 663560 | tf_op jit(solution)/shard_map/ppermute | solution.py:555
  4.5 23.6 %all-to-all-start = ((f32[128,1,896]{2,1,0:T(1,128)}), f32[128,1,896]{2,1,0:T(1,128)S(1)}, u32[]{:S(2)}, u32[]{:S(2)}) async-start(f32[128,1,896]{2,1,0:T(1,128)} %bitcast.7), calls=%async_computation | async-start | bytes 917504 | tf_op jit(solution)/shard_map/all_to_all | solution.py:551
  31.3 17.3 %copy-start.9 = (bf16[2,256,256]{2,1,0:T(8,128)(2,1)S(1)}, bf16[2,256,256]{2,1,0:T(8,128)(2,1)}, u32[]{:S(2)}) copy-start(bf16[2,256,256]{2,1,0:T(8,128)(2,1)} %constant.108.clone.wide_ref) | copy-start | bytes 786436
  31.3 17.3 %all-to-all-start.1 = ((f32[64,1,1920]{2,1,0:T(1,128)}), f32[64,1,1920]{2,1,0:T(1,128)S(1)}, u32[]{:S(2)}, u32[]{:S(2)}) async-start(f32[64,1,1920]{2,1,0:T(1,128)} %bitcast.11), calls=%async_computation.1 | async-start | bytes 983040 | tf_op jit(solution)/shard_map/all_to_all | solution.py:551
  36.7 8.9 %collective-permute-start.3 = (f32[2,72,192]{2,1,0:T(8,128)S(1)}, f32[2,72,192]{2,1,0:T(8,128)S(1)}, u32[]{:S(2)}, u32[]{:S(2)}) collective-permute-start(f32[2,72,192]{2,1,0:T(8,128)S(1)} %get-tuple-element.22), channel_id=1, source_target_pairs={{2,0},{4,2},{14,12},{8,14},{3,1},{5,3},{15,13},{9,15},{18,16},{20,... | collective-permute-start | bytes 331784 | tf_op jit(solution)/shard_map/ppermute | solution.py:569
  40.8 4.8 %collective-permute-start.2 = (f32[2,72,192]{2,1,0:T(8,128)S(1)}, f32[2,72,192]{2,1,0:T(8,128)S(1)}, u32[]{:S(2)}, u32[]{:S(2)}) collective-permute-start(f32[2,72,192]{2,1,0:T(8,128)S(1)} %get-tuple-element.23), channel_id=1, source_target_pairs={{4,0},{6,2},{8,12},{10,14},{5,1},{7,3},{9,13},{11,15},{20,16},{22,... | collective-permute-start | bytes 331784 | tf_op jit(solution)/shard_map/ppermute | solution.py:569
  42.4 3.2 %collective-permute-start.1 = (f32[2,72,192]{2,1,0:T(8,128)S(1)}, f32[2,72,192]{2,1,0:T(8,128)S(1)}, u32[]{:S(2)}, u32[]{:S(2)}) collective-permute-start(f32[2,72,192]{2,1,0:T(8,128)S(1)} %get-tuple-element.24), channel_id=1, source_target_pairs={{6,0},{0,2},{10,12},{12,14},{7,1},{1,3},{11,13},{13,15},{22,16},{1... | collective-permute-start | bytes 331784 | tf_op jit(solution)/shard_map/ppermute | solution.py:569
  48.6 27.3 %copy-start.7 = (bf16[2,2,192,256]{3,2,1,0:T(8,128)(2,1)S(1)}, bf16[2,2,192,256]{3,2,1,0:T(8,128)(2,1)}, u32[]{:S(2)}) copy-start(bf16[2,2,192,256]{3,2,1,0:T(8,128)(2,1)} %constant.110.clone.ly_ref) | copy-start | bytes 1179652
  48.6 27.3 %copy-start.8 = (bf16[2,384,192]{2,1,0:T(8,128)(2,1)S(1)}, bf16[2,384,192]{2,1,0:T(8,128)(2,1)}, u32[]{:S(2)}) copy-start(bf16[2,384,192]{2,1,0:T(8,128)(2,1)} %constant.109.clone.lz_ref) | copy-start | bytes 884740
  52.3 19.5 %all-to-all-start.2 = ((f32[64,1,1920]{2,1,0:T(1,128)}), f32[64,1,1920]{2,1,0:T(1,128)S(1)}, u32[]{:S(2)}, u32[]{:S(2)}) async-start(f32[64,1,1920]{2,1,0:T(1,128)} %bitcast.19), calls=%async_computation.2 | async-start | bytes 983040 | tf_op jit(solution)/shard_map/all_to_all | solution.py:551
  60.6 13.8 %collective-permute-start.5 = (f32[4,2,72,192]{3,2,1,0:T(8,128)S(1)}, f32[4,2,72,192]{3,2,1,0:T(8,128)S(1)}, u32[]{:S(2)}, u32[]{:S(2)}) collective-permute-start(f32[4,2,72,192]{3,2,1,0:T(8,128)S(1)} %pad_maximum_fusion), channel_id=1, source_target_pairs={{0,8},{2,10},{12,4},{14,6},{1,9},{3,11},{13,5},{15,7},{16,24},{18,... | collective-permute-start | bytes 1327112 | tf_op jit(solution)/shard_map/ppermute | solution.py:576
  71.8 4.1 %collective-permute-start.4 = (f32[960,128]{1,0:T(8,128)S(1)}, f32[960,128]{1,0:T(8,128)S(1)}, u32[]{:S(2)}, u32[]{:S(2)}) collective-permute-start(f32[960,128]{1,0:T(8,128)S(1)} %bitcast.43), channel_id=1, source_target_pairs={{0,8},{8,0},{1,9},{9,1},{2,10},{10,2},{3,11},{11,3},{4,12},{12,4},... | collective-permute-start | bytes 1474568 | tf_op jit(solution)/shard_map/ppermute | solution.py:592
  79.2 20.5 %copy-start = (bf16[2,384,384]{2,1,0:T(8,128)(2,1)S(1)}, bf16[2,384,384]{2,1,0:T(8,128)(2,1)}, u32[]{:S(2)}) copy-start(bf16[2,384,384]{2,1,0:T(8,128)(2,1)} %constant.112.clone.matrix_hbm.matrix_ref) | copy-start | bytes 1769476
  79.2 20.5 %copy-start.6 = (bf16[2,384,192]{2,1,0:T(8,128)(2,1)S(1)}, bf16[2,384,192]{2,1,0:T(8,128)(2,1)}, u32[]{:S(2)}) copy-start(bf16[2,384,192]{2,1,0:T(8,128)(2,1)} %constant.111.clone.lift_ref) | copy-start | bytes 884740
  103.3 32.0 %copy-start.4 = (bf16[2,384,384]{2,1,0:T(8,128)(2,1)S(1)}, bf16[2,384,384]{2,1,0:T(8,128)(2,1)}, u32[]{:S(2)}) copy-start(bf16[2,384,384]{2,1,0:T(8,128)(2,1)} %constant.114.clone.back_hbm) | copy-start | bytes 1769476
  103.3 32.0 %copy-start.5 = (bf16[2,384,384]{2,1,0:T(8,128)(2,1)S(1)}, bf16[2,384,384]{2,1,0:T(8,128)(2,1)}, u32[]{:S(2)}) copy-start(bf16[2,384,384]{2,1,0:T(8,128)(2,1)} %constant.113.clone.out_hbm) | copy-start | bytes 1769476
  144.5 31.2 %copy-start.1 = (f32[48,24,384]{2,1,0:T(8,128)S(1)}, f32[48,24,384]{2,1,0:T(8,128)}, u32[]{:S(2)}) copy-start(f32[48,24,384]{2,1,0:T(8,128)} %param.16) | copy-start | bytes 5308420
  144.5 31.1 %copy-start.2 = (f32[384,1152]{1,0:T(8,128)S(1)}, f32[384,1152]{1,0:T(8,128)}, u32[]{:S(2)}) copy-start(f32[384,1152]{1,0:T(8,128)} %get-tuple-element.18.evolved_ref) | copy-start | bytes 5308420

commit v8 on v7

--- a/solution.py
+++ b/solution.py
@@ -585,12 +585,14 @@
     place = jnp.stack([core, across, near, chip, device, lax.axis_index(ROWS)])
 
     got = exchange(coarse_pencil(wave_coarse.reshape(288, NC)), ALL, 128).reshape(896, 128)
-    got, planes = lax.optimization_barrier((got, swap_planes(potential_coarse, near)))
-    got = exchange(coarse_z(place, got), CHIPS, 64).reshape(960, 128)
-    got, planes = lax.optimization_barrier((got, spread_planes(planes, across)))
+    planes = spread_planes(swap_planes(potential_coarse, near), across)
+    got, planes = lax.optimization_barrier((got, planes))
+    turned, planes = lax.optimization_barrier((coarse_z(place, got), planes))
+    got = exchange(turned, CHIPS, 64).reshape(960, 128)
+    got, planes = lax.optimization_barrier((got, share_planes(planes, core, across)))
     got = exchange(coarse_y(place, got), CHIPS, 64).reshape(960, 128)
     other = lax.ppermute(got, CORE, [(0, 1), (1, 0)])
-    turned = coarse_x(place, got, other, share_planes(planes, core, across))
+    turned = coarse_x(place, got, other, planes)
     got = exchange(turned, CHIPS, 64).reshape(1792, 128)
 
     evolved, spectrum = fine_in(got)

time: 195 us -> 197 us (1.010)
  blocking collectives: 97.8 us -> 114 us
  waiting for transfers between devices: 29.5 us -> 18 us
  starting transfers between devices: 36.6 us -> 34.3 us
    all_to_all x4 -> x5, blocking collectives: 97.8 us -> 114 us  [exchange(): return lax.all_to_all(flat, axes, split_axis=0, concat_axis=0, tiled=False)]
    all_to_all x3 -> x2, waiting for transfers between devices: 25.5 us -> 14.6 us  [exchange(): return lax.all_to_all(flat, axes, split_axis=0, concat_axis=0, tiled=False)]
    all_to_all x3 -> x2, starting transfers between devices: 24.2 us -> 19.9 us  [exchange(): return lax.all_to_all(flat, axes, split_axis=0, concat_axis=0, tiled=False)]
    ppermute x3, starting transfers between devices: 6.39 us -> 8.93 us  [spread_planes(): chunk = lax.ppermute(chunk, (CORE, 'cols_0'), moves)]
  transfers between devices with their start and end apart: 9 -> 8, of which waited for: 5 -> 5; matrix products, arithmetic and copies ran while one was open for 0% -> 0% of each run, Pallas kernels for 1% -> 1%
where the time goes in v8:
time: 197 us; the launch traced here: 196 us
  blocking collectives  114 us (58%)
  starting transfers between devices  34.3 us (17%)
  Pallas kernels  28.8 us (15%)
  waiting for transfers between devices  18 us (9%)
    all_to_all x5, blocking collectives, exchange(): return lax.all_to_all(flat, axes, split_axis=0, concat_axis=0, tiled=False)  114 us
    all_to_all x2, starting transfers between devices, exchange(): return lax.all_to_all(flat, axes, split_axis=0, concat_axis=0, tiled=False)  19.9 us
    all_to_all x2, waiting for transfers between devices, exchange(): return lax.all_to_all(flat, axes, split_axis=0, concat_axis=0, tiled=False)  14.6 us
    pallas_call x1, Pallas kernels, fine_slab(): pl.pallas_call(fine_slab_kernel, out_shape=jax.ShapeDtypeStruct((3456, 12...  9.19 us
    ppermute x3, starting transfers between devices, spread_planes(): chunk = lax.ppermute(chunk, (CORE, 'cols_0'), moves)  8.93 us
  transfers between devices with their start and end apart: 8, of which 5 were waited for; matrix products, arithmetic and copies ran while one was open for 0% of the time, Pallas kernels for 1%

profile of v8, /device:TPU:1, one launch (start us, length us, event | category | flops | bytes accessed | tf_op | source)
XLA Modules:
  0.0 196.1 jit_solution(16841782967520158806)
XLA Ops:
  0.0 2.0 %collective-permute-start = (f32[12,24,192]{2,1,0:T(8,128)}, f32[12,24,192]{2,1,0:T(8,128)S(1)}, u32[]{:S(2)}, u32[]{:S(2)}) collective-permute-start(f32[12,24,192]{2,1,0:T(8,128)} %param.15), channel_id=1, source_target_pairs={{0,1},{1,0},{2,3},{3,2},{4,5},{5,4},{6,7},{7,6},{8,9},{9,8},{10,11... | collective-permute-start | bytes 663560 | tf_op jit(solution)/shard_map/ppermute | solution.py:555
  2.0 2.4 %shard_map.136 = f32[896,128]{1,0:T(8,128)} custom-call(f32[288,192]{1,0:T(8,128)} %bitcast.52, bf16[2,192,192]{2,1,0:T(8,128)(2,1)} %constant.104.clone.matrix_hbm), custom_call_target="tpu_custom_call" | custom-call | tf_op jit(solution)/shard_map/pallas_call | solution.py:217
  4.4 10.7 %all-to-all-start = ((f32[128,1,896]{2,1,0:T(1,128)}), f32[128,1,896]{2,1,0:T(1,128)S(1)}, u32[]{:S(2)}, u32[]{:S(2)}) async-start(f32[128,1,896]{2,1,0:T(1,128)} %bitcast.7), calls=%async_computation | async-start | bytes 917504 | tf_op jit(solution)/shard_map/all_to_all | solution.py:551
  16.0 7.0 %collective-permute-start.2 = (f32[2,72,192]{2,1,0:T(8,128)S(1)}, f32[2,72,192]{2,1,0:T(8,128)S(1)}, u32[]{:S(2)}, u32[]{:S(2)}) collective-permute-start(f32[2,72,192]{2,1,0:T(8,128)S(1)} %get-tuple-element.27), channel_id=1, source_target_pairs={{4,0},{6,2},{8,12},{10,14},{5,1},{7,3},{9,13},{11,15},{20,16},{22,... | collective-permute-start | bytes 331784 | tf_op jit(solution)/shard_map/ppermute | solution.py:569
  23.0 1.3 collective-permute-start.3
  25.0 1.3 collective-permute-done.3
  26.4 1.6 all-to-all-done
  28.0 3.2 %shard_map.137 = f32[960,128]{1,0:T(8,128)} custom-call(s32[6]{0:T(128)S(1)} %stack.45.place_ref, f32[896,128]{1,0:T(8,128)S(1)} %bitcast.47, bf16[2,192,256]{2,1,0:T(8,128)(2,1)S(1)} %copy-done.11, bf16[2,192,256]{2,1,0:T(8,128)(2,1)S(1)} %copy-done.10, bf16[2,192,192]{2,1,0:T(8,128)(2,1)S(1)} %copy-done.3), custom_call_target="tpu_custom_call" | custom-call | tf_op jit(solution)/shard_map/pallas_call | solution.py:266
  31.2 1.4 collective-permute-start.4
  32.6 9.2 %all-to-all-start.1 = ((f32[64,1,1920]{2,1,0:T(1,128)}), f32[64,1,1920]{2,1,0:T(1,128)S(1)}, u32[]{:S(2)}, u32[]{:S(2)}) async-start(f32[64,1,1920]{2,1,0:T(1,128)} %bitcast.17), calls=%async_computation.1 | async-start | bytes 983040 | tf_op jit(solution)/shard_map/all_to_all | solution.py:551
  42.0 12.9 %all-to-all-done.1 = f32[64,1,1920]{2,1,0:T(1,128)S(1)} async-done(((f32[64,1,1920]{2,1,0:T(1,128)}), f32[64,1,1920]{2,1,0:T(1,128)S(1)}, u32[]{:S(2)}, u32[]{:S(2)}) %all-to-all-start.1) | async-done | bytes 491552 | tf_op jit(solution)/shard_map/all_to_all | solution.py:551
  54.9 2.9 %shard_map.138 = f32[960,128]{1,0:T(8,128)S(1)} custom-call(s32[6]{0:T(128)S(1)} %stack.45.place_ref, f32[960,128]{1,0:T(8,128)S(1)} %bitcast.45, bf16[2,192,192]{2,1,0:T(8,128)(2,1)S(1)} %copy-done.3, bf16[2,256,256]{2,1,0:T(8,128)(2,1)S(1)} %copy-done.9), custom_call_target="tpu_custom_call" | custom-call | tf_op jit(solution)/shard_map/pallas_call | solution.py:299
  57.9 16.3 %all_to_all.35 = f32[64,1,1920]{2,1,0:T(1,128)S(1)} all-to-all(f32[64,1,1920]{2,1,0:T(1,128)S(1)} %bitcast.46), channel_id=1, replica_groups=mesh['rows_0'=4,'rows_1'=2,'rows_2'=2,'cols_0'=4,'cols_1'=2] {'rows_0','..., dimensions={0} | all-to-all | bytes 983040 | tf_op jit(solution)/shard_map/all_to_all | solution.py:551
  74.2 2.1 %collective-permute-start.5 = (f32[960,128]{1,0:T(8,128)S(1)}, f32[960,128]{1,0:T(8,128)S(1)}, u32[]{:S(2)}, u32[]{:S(2)}) collective-permute-start(f32[960,128]{1,0:T(8,128)S(1)} %bitcast.43), channel_id=1, source_target_pairs={{0,8},{8,0},{1,9},{9,1},{2,10},{10,2},{3,11},{11,3},{4,12},{12,4},... | collective-permute-start | bytes 1474568 | tf_op jit(solution)/shard_map/ppermute | solution.py:594
  76.3 1.5 collective-permute-done.5.other_ref
  77.8 3.3 %shard_map.139 = f32[1792,128]{1,0:T(8,128)S(1)} custom-call(s32[6]{0:T(128)S(1)} %stack.45.place_ref, f32[960,128]{1,0:T(8,128)S(1)} %bitcast.44, f32[960,128]{1,0:T(8,128)S(1)} %collective-permute-done.5.other_ref, f32[8,72,192]{2,1,0:T(8,128)S(1)} %bitcast.42, bf16[2,192,192]{2,1,0:T(8,128)(2,1)S(1)} %copy-done.3, bf16[2,384,192]{2,1,0:T(8,128)(2,1)S(1)} %copy-done.8, ...), custom_call_target="tpu_custom_call" | custom-call | tf_op jit(solution)/shard_map/pallas_call | solution.py:349
  81.1 20.5 %all_to_all.36 = f32[64,1,3584]{2,1,0:T(1,128)S(1)} all-to-all(f32[64,1,3584]{2,1,0:T(1,128)S(1)} %bitcast.40), channel_id=1, replica_groups=mesh['rows_0'=4,'rows_1'=2,'rows_2'=2,'cols_0'=4,'cols_1'=2] {'rows_0','..., dimensions={0} | all-to-all | bytes 1835008 | tf_op jit(solution)/shard_map/all_to_all | solution.py:551
  101.6 3.6 %shard_map.140 = (f32[384,1152]{1,0:T(8,128)}, f32[3456,128]{1,0:T(8,128)S(1)}) custom-call(f32[1792,128]{1,0:T(8,128)S(1)} %bitcast.41, bf16[2,384,192]{2,1,0:T(8,128)(2,1)S(1)} %copy-done.6, bf16[2,384,384]{2,1,0:T(8,128)(2,1)S(1)} %copy-done), custom_call_target="tpu_custom_call" | custom-call | tf_op jit(solution)/shard_map/pallas_call | solution.py:397
  105.2 32.0 %all_to_all.37 = f32[128,1,3456]{2,1,0:T(1,128)S(1)} all-to-all(f32[128,1,3456]{2,1,0:T(1,128)S(1)} %bitcast.49), channel_id=1, replica_groups=mesh['rows_0'=4,'rows_1'=2,'rows_2'=2,'cols_0'=4,'cols_1'=2] {'rows_0','..., dimensions={0} | all-to-all | bytes 3538944 | tf_op jit(solution)/shard_map/all_to_all | solution.py:551
  137.2 9.2 %shard_map.141 = f32[3456,128]{1,0:T(8,128)S(1)} custom-call(s32[6]{0:T(128)S(1)} %stack.45.place_ref, f32[3456,128]{1,0:T(8,128)S(1)} %bitcast.38, bf16[2,384,384]{2,1,0:T(8,128)(2,1)S(1)} %copy-done.5, bf16[2,384,384]{2,1,0:T(8,128)(2,1)S(1)} %copy-done.4, bf16[2,384,384]{2,1,0:T(8,128)(2,1)S(1)} %copy-done), custom_call_target="tpu_custom_call" | custom-call | tf_op jit(solution)/shard_map/pallas_call | solution.py:465
  146.4 31.1 %all_to_all.38 = f32[128,1,3456]{2,1,0:T(1,128)S(1)} all-to-all(f32[128,1,3456]{2,1,0:T(1,128)S(1)} %bitcast.39), channel_id=1, replica_groups=mesh['rows_0'=4,'rows_1'=2,'rows_2'=2,'cols_0'=4,'cols_1'=2] {'rows_0','..., dimensions={0} | all-to-all | bytes 3538944 | tf_op jit(solution)/shard_map/all_to_all | solution.py:551
  177.6 2.9 %shard_map.142 = (f32[1152,384]{1,0:T(8,128)S(1)}, f32[128,128]{1,0:T(8,128)S(1)}) custom-call(s32[6]{0:T(128)S(1)} %stack.45.place_ref, f32[3456,128]{1,0:T(8,128)S(1)} %bitcast.37, f32[384,1152]{1,0:T(8,128)S(1)} %copy-done.2, f32[1152,384]{1,0:T(8,128)S(1)} %bitcast.48, bf16[2,384,384]{2,1,0:T(8,128)(2,1)S(1)} %copy-done), custom_call_target="tpu_custom_call" | custom-call | tf_op jit(solution)/shard_map/pallas_call | solution.py:511
  180.4 14.2 %all_to_all.39 = f32[128,1,128]{2,1,0:T(1,128)S(1)} all-to-all(f32[128,1,128]{2,1,0:T(1,128)S(1)} %bitcast.51), channel_id=1, replica_groups=mesh['rows_0'=4,'rows_1'=2,'rows_2'=2,'cols_0'=4,'cols_1'=2] {'rows_0','..., dimensions={0} | all-to-all | bytes 131072 | tf_op jit(solution)/shard_map/all_to_all | solution.py:551
  194.6 1.3 shard_map.143
  (37 shorter events, 1.7 us)
Async XLA Ops:
  0.0 15.2 %copy-start.12 = (f32[12,24,192]{2,1,0:T(8,128)S(1)}, f32[12,24,192]{2,1,0:T(8,128)}, u32[]{:S(2)}) copy-start(f32[12,24,192]{2,1,0:T(8,128)} %param.15) | copy-start | bytes 663556
  0.0 15.2 %collective-permute-start = (f32[12,24,192]{2,1,0:T(8,128)}, f32[12,24,192]{2,1,0:T(8,128)S(1)}, u32[]{:S(2)}, u32[]{:S(2)}) collective-permute-start(f32[12,24,192]{2,1,0:T(8,128)} %param.15), channel_id=1, source_target_pairs={{0,1},{1,0},{2,3},{3,2},{4,5},{5,4},{6,7},{7,6},{8,9},{9,8},{10,11... | collective-permute-start | bytes 663560 | tf_op jit(solution)/shard_map/ppermute | solution.py:555
  4.4 23.6 %copy-start.3 = (bf16[2,192,192]{2,1,0:T(8,128)(2,1)S(1)}, bf16[2,192,192]{2,1,0:T(8,128)(2,1)}, u32[]{:S(2)}) copy-start(bf16[2,192,192]{2,1,0:T(8,128)(2,1)} %constant.107.clone.matrix_ref) | copy-start | bytes 442372
  4.4 23.6 %copy-start.10 = (bf16[2,192,256]{2,1,0:T(8,128)(2,1)S(1)}, bf16[2,192,256]{2,1,0:T(8,128)(2,1)}, u32[]{:S(2)}) copy-start(bf16[2,192,256]{2,1,0:T(8,128)(2,1)} %constant.106.clone.ex_ref) | copy-start | bytes 589828
  4.4 23.6 %copy-start.11 = (bf16[2,192,256]{2,1,0:T(8,128)(2,1)S(1)}, bf16[2,192,256]{2,1,0:T(8,128)(2,1)}, u32[]{:S(2)}) copy-start(bf16[2,192,256]{2,1,0:T(8,128)(2,1)} %constant.105.clone.ey_ref) | copy-start | bytes 589828
  4.4 23.6 %all-to-all-start = ((f32[128,1,896]{2,1,0:T(1,128)}), f32[128,1,896]{2,1,0:T(1,128)S(1)}, u32[]{:S(2)}, u32[]{:S(2)}) async-start(f32[128,1,896]{2,1,0:T(1,128)} %bitcast.7), calls=%async_computation | async-start | bytes 917504 | tf_op jit(solution)/shard_map/all_to_all | solution.py:551
  15.3 9.1 %collective-permute-start.1 = (f32[2,72,192]{2,1,0:T(8,128)S(1)}, f32[2,72,192]{2,1,0:T(8,128)S(1)}, u32[]{:S(2)}, u32[]{:S(2)}) collective-permute-start(f32[2,72,192]{2,1,0:T(8,128)S(1)} %get-tuple-element.26), channel_id=1, source_target_pairs={{6,0},{0,2},{10,12},{12,14},{7,1},{1,3},{11,13},{13,15},{22,16},{1... | collective-permute-start | bytes 331784 | tf_op jit(solution)/shard_map/ppermute | solution.py:569
  16.0 9.0 %collective-permute-start.2 = (f32[2,72,192]{2,1,0:T(8,128)S(1)}, f32[2,72,192]{2,1,0:T(8,128)S(1)}, u32[]{:S(2)}, u32[]{:S(2)}) collective-permute-start(f32[2,72,192]{2,1,0:T(8,128)S(1)} %get-tuple-element.27), channel_id=1, source_target_pairs={{4,0},{6,2},{8,12},{10,14},{5,1},{7,3},{9,13},{11,15},{20,16},{22,... | collective-permute-start | bytes 331784 | tf_op jit(solution)/shard_map/ppermute | solution.py:569
  23.0 3.4 %collective-permute-start.3 = (f32[2,72,192]{2,1,0:T(8,128)S(1)}, f32[2,72,192]{2,1,0:T(8,128)S(1)}, u32[]{:S(2)}, u32[]{:S(2)}) collective-permute-start(f32[2,72,192]{2,1,0:T(8,128)S(1)} %get-tuple-element.28), channel_id=1, source_target_pairs={{2,0},{4,2},{14,12},{8,14},{3,1},{5,3},{15,13},{9,15},{18,16},{20,... | collective-permute-start | bytes 331784 | tf_op jit(solution)/shard_map/ppermute | solution.py:569
  31.2 23.7 %copy-start.9 = (bf16[2,256,256]{2,1,0:T(8,128)(2,1)S(1)}, bf16[2,256,256]{2,1,0:T(8,128)(2,1)}, u32[]{:S(2)}) copy-start(bf16[2,256,256]{2,1,0:T(8,128)(2,1)} %constant.108.clone.wide_ref) | copy-start | bytes 786436
  31.2 10.7 %collective-permute-start.4 = (f32[4,2,72,192]{3,2,1,0:T(8,128)S(1)}, f32[4,2,72,192]{3,2,1,0:T(8,128)S(1)}, u32[]{:S(2)}, u32[]{:S(2)}) collective-permute-start(f32[4,2,72,192]{3,2,1,0:T(8,128)S(1)} %pad_maximum_fusion), channel_id=1, source_target_pairs={{0,8},{2,10},{12,4},{14,6},{1,9},{3,11},{13,5},{15,7},{16,24},{18,... | collective-permute-start | bytes 1327112 | tf_op jit(solution)/shard_map/ppermute | solution.py:576
  32.6 22.3 %all-to-all-start.1 = ((f32[64,1,1920]{2,1,0:T(1,128)}), f32[64,1,1920]{2,1,0:T(1,128)S(1)}, u32[]{:S(2)}, u32[]{:S(2)}) async-start(f32[64,1,1920]{2,1,0:T(1,128)} %bitcast.17), calls=%async_computation.1 | async-start | bytes 983040 | tf_op jit(solution)/shard_map/all_to_all | solution.py:551
  41.9 35.9 %copy-start.7 = (bf16[2,2,192,256]{3,2,1,0:T(8,128)(2,1)S(1)}, bf16[2,2,192,256]{3,2,1,0:T(8,128)(2,1)}, u32[]{:S(2)}) copy-start(bf16[2,2,192,256]{3,2,1,0:T(8,128)(2,1)} %constant.110.clone.ly_ref) | copy-start | bytes 1179652
  41.9 35.9 %copy-start.8 = (bf16[2,384,192]{2,1,0:T(8,128)(2,1)S(1)}, bf16[2,384,192]{2,1,0:T(8,128)(2,1)}, u32[]{:S(2)}) copy-start(bf16[2,384,192]{2,1,0:T(8,128)(2,1)} %constant.109.clone.lz_ref) | copy-start | bytes 884740
  74.2 3.6 %collective-permute-start.5 = (f32[960,128]{1,0:T(8,128)S(1)}, f32[960,128]{1,0:T(8,128)S(1)}, u32[]{:S(2)}, u32[]{:S(2)}) collective-permute-start(f32[960,128]{1,0:T(8,128)S(1)} %bitcast.43), channel_id=1, source_target_pairs={{0,8},{8,0},{1,9},{9,1},{2,10},{10,2},{3,11},{11,3},{4,12},{12,4},... | collective-permute-start | bytes 1474568 | tf_op jit(solution)/shard_map/ppermute | solution.py:594
  81.1 20.5 %copy-start = (bf16[2,384,384]{2,1,0:T(8,128)(2,1)S(1)}, bf16[2,384,384]{2,1,0:T(8,128)(2,1)}, u32[]{:S(2)}) copy-start(bf16[2,384,384]{2,1,0:T(8,128)(2,1)} %constant.112.clone.matrix_hbm.matrix_ref) | copy-start | bytes 1769476
  81.1 20.5 %copy-start.6 = (bf16[2,384,192]{2,1,0:T(8,128)(2,1)S(1)}, bf16[2,384,192]{2,1,0:T(8,128)(2,1)}, u32[]{:S(2)}) copy-start(bf16[2,384,192]{2,1,0:T(8,128)(2,1)} %constant.111.clone.lift_ref) | copy-start | bytes 884740
  105.2 32.0 %copy-start.4 = (bf16[2,384,384]{2,1,0:T(8,128)(2,1)S(1)}, bf16[2,384,384]{2,1,0:T(8,128)(2,1)}, u32[]{:S(2)}) copy-start(bf16[2,384,384]{2,1,0:T(8,128)(2,1)} %constant.114.clone.back_hbm) | copy-start | bytes 1769476
  105.2 32.0 %copy-start.5 = (bf16[2,384,384]{2,1,0:T(8,128)(2,1)S(1)}, bf16[2,384,384]{2,1,0:T(8,128)(2,1)}, u32[]{:S(2)}) copy-start(bf16[2,384,384]{2,1,0:T(8,128)(2,1)} %constant.113.clone.out_hbm) | copy-start | bytes 1769476
  146.4 31.1 %copy-start.1 = (f32[48,24,384]{2,1,0:T(8,128)S(1)}, f32[48,24,384]{2,1,0:T(8,128)}, u32[]{:S(2)}) copy-start(f32[48,24,384]{2,1,0:T(8,128)} %param.16) | copy-start | bytes 5308420
  146.4 31.1 %copy-start.2 = (f32[384,1152]{1,0:T(8,128)S(1)}, f32[384,1152]{1,0:T(8,128)}, u32[]{:S(2)}) copy-start(f32[384,1152]{1,0:T(8,128)} %get-tuple-element.22.evolved_ref) | copy-start | bytes 5308420

commit v9 on v7

--- a/solution.py
+++ b/solution.py
@@ -587,7 +587,7 @@
     got = exchange(coarse_pencil(wave_coarse.reshape(288, NC)), ALL, 128).reshape(896, 128)
     got, planes = lax.optimization_barrier((got, swap_planes(potential_coarse, near)))
     got = exchange(coarse_z(place, got), CHIPS, 64).reshape(960, 128)
-    got, planes = lax.optimization_barrier((got, spread_planes(planes, across)))
+    planes = spread_planes(planes, across)
     got = exchange(coarse_y(place, got), CHIPS, 64).reshape(960, 128)
     other = lax.ppermute(got, CORE, [(0, 1), (1, 0)])
     turned = coarse_x(place, got, other, share_planes(planes, core, across))

time: 195 us -> 198 us (1.015)
  blocking collectives: 97.8 us -> 101 us
    ppermute x1, starting transfers between devices: 2.58 us -> 6.87 us  [per_device(): other = lax.ppermute(got, CORE, [(0, 1), (1, 0)])]
    all_to_all x3, starting transfers between devices: 24.2 us -> 20.6 us  [exchange(): return lax.all_to_all(flat, axes, split_axis=0, concat_axis=0, tiled=False)]
    all_to_all x4, blocking collectives: 97.8 us -> 101 us  [exchange(): return lax.all_to_all(flat, axes, split_axis=0, concat_axis=0, tiled=False)]
  transfers between devices with their start and end apart: 9 -> 9, of which waited for: 5 -> 4; matrix products, arithmetic and copies ran while one was open for 0% -> 1% of each run, Pallas kernels for 1% -> 1%
where the time goes in v9:
time: 198 us; the launch traced here: 197 us
  blocking collectives  101 us (51%)
  starting transfers between devices  37.4 us (19%)
  Pallas kernels  29.5 us (15%)
  waiting for transfers between devices  28 us (14%)
    all_to_all x4, blocking collectives, exchange(): return lax.all_to_all(flat, axes, split_axis=0, concat_axis=0, tiled=False)  101 us
    all_to_all x3, waiting for transfers between devices, exchange(): return lax.all_to_all(flat, axes, split_axis=0, concat_axis=0, tiled=False)  24.6 us
    all_to_all x3, starting transfers between devices, exchange(): return lax.all_to_all(flat, axes, split_axis=0, concat_axis=0, tiled=False)  20.6 us
    pallas_call x1, Pallas kernels, fine_slab(): pl.pallas_call(fine_slab_kernel, out_shape=jax.ShapeDtypeStruct((3456, 12...  9.16 us
    ppermute x1, starting transfers between devices, per_device(): other = lax.ppermute(got, CORE, [(0, 1), (1, 0)])  6.87 us
    ppermute x3, starting transfers between devices, spread_planes(): chunk = lax.ppermute(chunk, (CORE, 'cols_0'), moves)  6.52 us
  transfers between devices with their start and end apart: 9, of which 4 were waited for; matrix products, arithmetic and copies ran while one was open for 1% of the time, Pallas kernels for 1%

profile of v9, /device:TPU:1, one launch (start us, length us, event | category | flops | bytes accessed | tf_op | source)
XLA Modules:
  0.0 197.5 jit_solution(943800777404246598)
XLA Ops:
  0.0 2.1 %collective-permute-start = (f32[12,24,192]{2,1,0:T(8,128)}, f32[12,24,192]{2,1,0:T(8,128)S(1)}, u32[]{:S(2)}, u32[]{:S(2)}) collective-permute-start(f32[12,24,192]{2,1,0:T(8,128)} %param.15), channel_id=1, source_target_pairs={{0,1},{1,0},{2,3},{3,2},{4,5},{5,4},{6,7},{7,6},{8,9},{9,8},{10,11... | collective-permute-start | bytes 663560 | tf_op jit(solution)/shard_map/ppermute | solution.py:555
  2.1 2.4 %shard_map.136 = f32[896,128]{1,0:T(8,128)} custom-call(f32[288,192]{1,0:T(8,128)} %bitcast.57, bf16[2,192,192]{2,1,0:T(8,128)(2,1)} %constant.104.clone.matrix_hbm), custom_call_target="tpu_custom_call" | custom-call | tf_op jit(solution)/shard_map/pallas_call | solution.py:217
  4.5 10.7 %all-to-all-start = ((f32[128,1,896]{2,1,0:T(1,128)}), f32[128,1,896]{2,1,0:T(1,128)S(1)}, u32[]{:S(2)}, u32[]{:S(2)}) async-start(f32[128,1,896]{2,1,0:T(1,128)} %bitcast.7), calls=%async_computation | async-start | bytes 917504 | tf_op jit(solution)/shard_map/all_to_all | solution.py:551
  15.4 12.7 %all-to-all-done = f32[128,1,896]{2,1,0:T(1,128)S(1)} async-done(((f32[128,1,896]{2,1,0:T(1,128)}), f32[128,1,896]{2,1,0:T(1,128)S(1)}, u32[]{:S(2)}, u32[]{:S(2)}) %all-to-all-start) | async-done | bytes 458784 | tf_op jit(solution)/shard_map/all_to_all | solution.py:551
  28.1 3.2 %shard_map.137 = f32[960,128]{1,0:T(8,128)} custom-call(s32[6]{0:T(128)S(1)} %stack.45.place_ref, f32[896,128]{1,0:T(8,128)S(1)} %bitcast.46, bf16[2,192,256]{2,1,0:T(8,128)(2,1)S(1)} %copy-done.11, bf16[2,192,256]{2,1,0:T(8,128)(2,1)S(1)} %copy-done.10, bf16[2,192,192]{2,1,0:T(8,128)(2,1)S(1)} %copy-done.3), custom_call_target="tpu_custom_call" | custom-call | tf_op jit(solution)/shard_map/pallas_call | solution.py:266
  31.3 5.2 %all-to-all-start.1 = ((f32[64,1,1920]{2,1,0:T(1,128)}), f32[64,1,1920]{2,1,0:T(1,128)S(1)}, u32[]{:S(2)}, u32[]{:S(2)}) async-start(f32[64,1,1920]{2,1,0:T(1,128)} %bitcast.11), calls=%async_computation.1 | async-start | bytes 983040 | tf_op jit(solution)/shard_map/all_to_all | solution.py:551
  36.5 11.9 %all-to-all-done.1 = f32[64,1,1920]{2,1,0:T(1,128)S(1)} async-done(((f32[64,1,1920]{2,1,0:T(1,128)}), f32[64,1,1920]{2,1,0:T(1,128)S(1)}, u32[]{:S(2)}, u32[]{:S(2)}) %all-to-all-start.1) | async-done | bytes 491552 | tf_op jit(solution)/shard_map/all_to_all | solution.py:551
  48.4 3.7 %shard_map.138 = f32[960,128]{1,0:T(8,128)} custom-call(s32[6]{0:T(128)S(1)} %stack.45.place_ref, f32[960,128]{1,0:T(8,128)S(1)} %bitcast.45, bf16[2,192,192]{2,1,0:T(8,128)(2,1)S(1)} %copy-done.3, bf16[2,256,256]{2,1,0:T(8,128)(2,1)S(1)} %copy-done.9), custom_call_target="tpu_custom_call" | custom-call | tf_op jit(solution)/shard_map/pallas_call | solution.py:299
  52.1 4.8 %all-to-all-start.2 = ((f32[64,1,1920]{2,1,0:T(1,128)}), f32[64,1,1920]{2,1,0:T(1,128)S(1)}, u32[]{:S(2)}, u32[]{:S(2)}) async-start(f32[64,1,1920]{2,1,0:T(1,128)} %bitcast.13), calls=%async_computation.2 | async-start | bytes 983040 | tf_op jit(solution)/shard_map/all_to_all | solution.py:551
  57.0 4.3 %collective-permute-start.4 = (f32[2,72,192]{2,1,0:T(8,128)S(1)}, f32[2,72,192]{2,1,0:T(8,128)S(1)}, u32[]{:S(2)}, u32[]{:S(2)}) collective-permute-start(f32[2,72,192]{2,1,0:T(8,128)S(1)} %get-tuple-element.18), channel_id=1, source_target_pairs={{2,0},{4,2},{14,12},{8,14},{3,1},{5,3},{15,13},{9,15},{18,16},{20,... | collective-permute-start | bytes 331784 | tf_op jit(solution)/shard_map/ppermute | solution.py:569
  61.3 1.6 collective-permute-start.3
  63.5 2.6 %collective-permute-done.4 = f32[2,72,192]{2,1,0:T(8,128)S(1)} collective-permute-done((f32[2,72,192]{2,1,0:T(8,128)S(1)}, f32[2,72,192]{2,1,0:T(8,128)S(1)}, u32[]{:S(2)}, u32[]{:S(2)}) %collective-permute-start.4) | collective-permute-done | bytes 110624 | tf_op jit(solution)/shard_map/ppermute | solution.py:569
  66.2 1.3 collective-permute-start.5
  67.5 6.9 %collective-permute-start.1 = (f32[960,128]{1,0:T(8,128)S(1)}, f32[960,128]{1,0:T(8,128)S(1)}, u32[]{:S(2)}, u32[]{:S(2)}) collective-permute-start(f32[960,128]{1,0:T(8,128)S(1)} %bitcast.43), channel_id=1, source_target_pairs={{0,8},{8,0},{1,9},{9,1},{2,10},{10,2},{3,11},{11,3},{4,12},{12,4},... | collective-permute-start | bytes 1474568 | tf_op jit(solution)/shard_map/ppermute | solution.py:592
  75.1 1.1 broadcast_select_fusion
  76.3 3.3 %shard_map.139 = f32[1792,128]{1,0:T(8,128)S(1)} custom-call(s32[6]{0:T(128)S(1)} %stack.45.place_ref, f32[960,128]{1,0:T(8,128)S(1)} %bitcast.44, f32[960,128]{1,0:T(8,128)S(1)} %collective-permute-done.1.other_ref, f32[8,72,192]{2,1,0:T(8,128)S(1)} %bitcast.42, bf16[2,192,192]{2,1,0:T(8,128)(2,1)S(1)} %copy-done.3, bf16[2,384,192]{2,1,0:T(8,128)(2,1)S(1)} %copy-done.8, ...), custom_call_target="tpu_custom_call" | custom-call | tf_op jit(solution)/shard_map/pallas_call | solution.py:349
  79.6 23.7 %all_to_all.35 = f32[64,1,3584]{2,1,0:T(1,128)S(1)} all-to-all(f32[64,1,3584]{2,1,0:T(1,128)S(1)} %bitcast.40), channel_id=1, replica_groups=mesh['rows_0'=4,'rows_1'=2,'rows_2'=2,'cols_0'=4,'cols_1'=2] {'rows_0','..., dimensions={0} | all-to-all | bytes 1835008 | tf_op jit(solution)/shard_map/all_to_all | solution.py:551
  103.3 3.6 %shard_map.140 = (f32[384,1152]{1,0:T(8,128)}, f32[3456,128]{1,0:T(8,128)S(1)}) custom-call(f32[1792,128]{1,0:T(8,128)S(1)} %bitcast.41, bf16[2,384,192]{2,1,0:T(8,128)(2,1)S(1)} %copy-done.6, bf16[2,384,384]{2,1,0:T(8,128)(2,1)S(1)} %copy-done), custom_call_target="tpu_custom_call" | custom-call | tf_op jit(solution)/shard_map/pallas_call | solution.py:397
  106.9 31.7 %all_to_all.36 = f32[128,1,3456]{2,1,0:T(1,128)S(1)} all-to-all(f32[128,1,3456]{2,1,0:T(1,128)S(1)} %bitcast.48), channel_id=1, replica_groups=mesh['rows_0'=4,'rows_1'=2,'rows_2'=2,'cols_0'=4,'cols_1'=2] {'rows_0','..., dimensions={0} | all-to-all | bytes 3538944 | tf_op jit(solution)/shard_map/all_to_all | solution.py:551
  138.6 9.2 %shard_map.141 = f32[3456,128]{1,0:T(8,128)S(1)} custom-call(s32[6]{0:T(128)S(1)} %stack.45.place_ref, f32[3456,128]{1,0:T(8,128)S(1)} %bitcast.38, bf16[2,384,384]{2,1,0:T(8,128)(2,1)S(1)} %copy-done.5, bf16[2,384,384]{2,1,0:T(8,128)(2,1)S(1)} %copy-done.4, bf16[2,384,384]{2,1,0:T(8,128)(2,1)S(1)} %copy-done), custom_call_target="tpu_custom_call" | custom-call | tf_op jit(solution)/shard_map/pallas_call | solution.py:465
  147.8 31.1 %all_to_all.37 = f32[128,1,3456]{2,1,0:T(1,128)S(1)} all-to-all(f32[128,1,3456]{2,1,0:T(1,128)S(1)} %bitcast.39), channel_id=1, replica_groups=mesh['rows_0'=4,'rows_1'=2,'rows_2'=2,'cols_0'=4,'cols_1'=2] {'rows_0','..., dimensions={0} | all-to-all | bytes 3538944 | tf_op jit(solution)/shard_map/all_to_all | solution.py:551
  178.9 2.9 %shard_map.142 = (f32[1152,384]{1,0:T(8,128)S(1)}, f32[128,128]{1,0:T(8,128)S(1)}) custom-call(s32[6]{0:T(128)S(1)} %stack.45.place_ref, f32[3456,128]{1,0:T(8,128)S(1)} %bitcast.37, f32[384,1152]{1,0:T(8,128)S(1)} %copy-done.2, f32[1152,384]{1,0:T(8,128)S(1)} %bitcast.47, bf16[2,384,384]{2,1,0:T(8,128)(2,1)S(1)} %copy-done), custom_call_target="tpu_custom_call" | custom-call | tf_op jit(solution)/shard_map/pallas_call | solution.py:511
  181.8 14.2 %all_to_all.38 = f32[128,1,128]{2,1,0:T(1,128)S(1)} all-to-all(f32[128,1,128]{2,1,0:T(1,128)S(1)} %bitcast.50), channel_id=1, replica_groups=mesh['rows_0'=4,'rows_1'=2,'rows_2'=2,'cols_0'=4,'cols_1'=2] {'rows_0','..., dimensions={0} | all-to-all | bytes 131072 | tf_op jit(solution)/shard_map/all_to_all | solution.py:551
  196.0 1.3 shard_map.143
  (39 shorter events, 1.8 us)
Async XLA Ops:
  0.0 28.1 %copy-start.3 = (bf16[2,192,192]{2,1,0:T(8,128)(2,1)S(1)}, bf16[2,192,192]{2,1,0:T(8,128)(2,1)}, u32[]{:S(2)}) copy-start(bf16[2,192,192]{2,1,0:T(8,128)(2,1)} %constant.107.clone.matrix_ref) | copy-start | bytes 442372
  0.0 28.1 %copy-start.10 = (bf16[2,192,256]{2,1,0:T(8,128)(2,1)S(1)}, bf16[2,192,256]{2,1,0:T(8,128)(2,1)}, u32[]{:S(2)}) copy-start(bf16[2,192,256]{2,1,0:T(8,128)(2,1)} %constant.106.clone.ex_ref) | copy-start | bytes 589828
  0.0 28.1 %copy-start.11 = (bf16[2,192,256]{2,1,0:T(8,128)(2,1)S(1)}, bf16[2,192,256]{2,1,0:T(8,128)(2,1)}, u32[]{:S(2)}) copy-start(bf16[2,192,256]{2,1,0:T(8,128)(2,1)} %constant.105.clone.ey_ref) | copy-start | bytes 589828
  0.0 15.3 %copy-start.12 = (f32[12,24,192]{2,1,0:T(8,128)S(1)}, f32[12,24,192]{2,1,0:T(8,128)}, u32[]{:S(2)}) copy-start(f32[12,24,192]{2,1,0:T(8,128)} %param.15) | copy-start | bytes 663556
  0.0 15.3 %collective-permute-start = (f32[12,24,192]{2,1,0:T(8,128)}, f32[12,24,192]{2,1,0:T(8,128)S(1)}, u32[]{:S(2)}, u32[]{:S(2)}) collective-permute-start(f32[12,24,192]{2,1,0:T(8,128)} %param.15), channel_id=1, source_target_pairs={{0,1},{1,0},{2,3},{3,2},{4,5},{5,4},{6,7},{7,6},{8,9},{9,8},{10,11... | collective-permute-start | bytes 663560 | tf_op jit(solution)/shard_map/ppermute | solution.py:555
  4.5 23.6 %all-to-all-start = ((f32[128,1,896]{2,1,0:T(1,128)}), f32[128,1,896]{2,1,0:T(1,128)S(1)}, u32[]{:S(2)}, u32[]{:S(2)}) async-start(f32[128,1,896]{2,1,0:T(1,128)} %bitcast.7), calls=%async_computation | async-start | bytes 917504 | tf_op jit(solution)/shard_map/all_to_all | solution.py:551
  15.3 33.1 %copy-start.9 = (bf16[2,256,256]{2,1,0:T(8,128)(2,1)S(1)}, bf16[2,256,256]{2,1,0:T(8,128)(2,1)}, u32[]{:S(2)}) copy-start(bf16[2,256,256]{2,1,0:T(8,128)(2,1)} %constant.108.clone.wide_ref) | copy-start | bytes 786436
  31.3 17.1 %all-to-all-start.1 = ((f32[64,1,1920]{2,1,0:T(1,128)}), f32[64,1,1920]{2,1,0:T(1,128)S(1)}, u32[]{:S(2)}, u32[]{:S(2)}) async-start(f32[64,1,1920]{2,1,0:T(1,128)} %bitcast.11), calls=%async_computation.1 | async-start | bytes 983040 | tf_op jit(solution)/shard_map/all_to_all | solution.py:551
  52.1 15.4 %all-to-all-start.2 = ((f32[64,1,1920]{2,1,0:T(1,128)}), f32[64,1,1920]{2,1,0:T(1,128)S(1)}, u32[]{:S(2)}, u32[]{:S(2)}) async-start(f32[64,1,1920]{2,1,0:T(1,128)} %bitcast.13), calls=%async_computation.2 | async-start | bytes 983040 | tf_op jit(solution)/shard_map/all_to_all | solution.py:551
  57.0 19.3 %copy-start.7 = (bf16[2,2,192,256]{3,2,1,0:T(8,128)(2,1)S(1)}, bf16[2,2,192,256]{3,2,1,0:T(8,128)(2,1)}, u32[]{:S(2)}) copy-start(bf16[2,2,192,256]{3,2,1,0:T(8,128)(2,1)} %constant.110.clone.ly_ref) | copy-start | bytes 1179652
  57.0 19.3 %copy-start.8 = (bf16[2,384,192]{2,1,0:T(8,128)(2,1)S(1)}, bf16[2,384,192]{2,1,0:T(8,128)(2,1)}, u32[]{:S(2)}) copy-start(bf16[2,384,192]{2,1,0:T(8,128)(2,1)} %constant.109.clone.lz_ref) | copy-start | bytes 884740
  57.0 9.1 %collective-permute-start.4 = (f32[2,72,192]{2,1,0:T(8,128)S(1)}, f32[2,72,192]{2,1,0:T(8,128)S(1)}, u32[]{:S(2)}, u32[]{:S(2)}) collective-permute-start(f32[2,72,192]{2,1,0:T(8,128)S(1)} %get-tuple-element.18), channel_id=1, source_target_pairs={{2,0},{4,2},{14,12},{8,14},{3,1},{5,3},{15,13},{9,15},{18,16},{20,... | collective-permute-start | bytes 331784 | tf_op jit(solution)/shard_map/ppermute | solution.py:569
  61.3 4.9 %collective-permute-start.3 = (f32[2,72,192]{2,1,0:T(8,128)S(1)}, f32[2,72,192]{2,1,0:T(8,128)S(1)}, u32[]{:S(2)}, u32[]{:S(2)}) collective-permute-start(f32[2,72,192]{2,1,0:T(8,128)S(1)} %get-tuple-element.19), channel_id=1, source_target_pairs={{4,0},{6,2},{8,12},{10,14},{5,1},{7,3},{9,13},{11,15},{20,16},{22,... | collective-permute-start | bytes 331784 | tf_op jit(solution)/shard_map/ppermute | solution.py:569
  62.9 3.3 %collective-permute-start.2 = (f32[2,72,192]{2,1,0:T(8,128)S(1)}, f32[2,72,192]{2,1,0:T(8,128)S(1)}, u32[]{:S(2)}, u32[]{:S(2)}) collective-permute-start(f32[2,72,192]{2,1,0:T(8,128)S(1)} %get-tuple-element.20), channel_id=1, source_target_pairs={{6,0},{0,2},{10,12},{12,14},{7,1},{1,3},{11,13},{13,15},{22,16},{1... | collective-permute-start | bytes 331784 | tf_op jit(solution)/shard_map/ppermute | solution.py:569
  66.2 9.0 %collective-permute-start.5 = (f32[4,2,72,192]{3,2,1,0:T(8,128)S(1)}, f32[4,2,72,192]{3,2,1,0:T(8,128)}, u32[]{:S(2)}, u32[]{:S(2)}) collective-permute-start(f32[4,2,72,192]{3,2,1,0:T(8,128)S(1)} %pad_maximum_fusion), channel_id=1, source_target_pairs={{0,8},{2,10},{12,4},{14,6},{1,9},{3,11},{13,5},{15,7},{16,24},{18,... | collective-permute-start | bytes 1327112 | tf_op jit(solution)/shard_map/ppermute | solution.py:576
  67.5 8.8 %collective-permute-start.1 = (f32[960,128]{1,0:T(8,128)S(1)}, f32[960,128]{1,0:T(8,128)S(1)}, u32[]{:S(2)}, u32[]{:S(2)}) collective-permute-start(f32[960,128]{1,0:T(8,128)S(1)} %bitcast.43), channel_id=1, source_target_pairs={{0,8},{8,0},{1,9},{9,1},{2,10},{10,2},{3,11},{11,3},{4,12},{12,4},... | collective-permute-start | bytes 1474568 | tf_op jit(solution)/shard_map/ppermute | solution.py:592
  79.6 23.7 %copy-start = (bf16[2,384,384]{2,1,0:T(8,128)(2,1)S(1)}, bf16[2,384,384]{2,1,0:T(8,128)(2,1)}, u32[]{:S(2)}) copy-start(bf16[2,384,384]{2,1,0:T(8,128)(2,1)} %constant.112.clone.matrix_hbm.matrix_ref) | copy-start | bytes 1769476
  79.6 23.7 %copy-start.6 = (bf16[2,384,192]{2,1,0:T(8,128)(2,1)S(1)}, bf16[2,384,192]{2,1,0:T(8,128)(2,1)}, u32[]{:S(2)}) copy-start(bf16[2,384,192]{2,1,0:T(8,128)(2,1)} %constant.111.clone.lift_ref) | copy-start | bytes 884740
  106.9 31.7 %copy-start.4 = (bf16[2,384,384]{2,1,0:T(8,128)(2,1)S(1)}, bf16[2,384,384]{2,1,0:T(8,128)(2,1)}, u32[]{:S(2)}) copy-start(bf16[2,384,384]{2,1,0:T(8,128)(2,1)} %constant.114.clone.back_hbm) | copy-start | bytes 1769476
  106.9 31.7 %copy-start.5 = (bf16[2,384,384]{2,1,0:T(8,128)(2,1)S(1)}, bf16[2,384,384]{2,1,0:T(8,128)(2,1)}, u32[]{:S(2)}) copy-start(bf16[2,384,384]{2,1,0:T(8,128)(2,1)} %constant.113.clone.out_hbm) | copy-start | bytes 1769476
  147.8 31.2 %copy-start.1 = (f32[48,24,384]{2,1,0:T(8,128)S(1)}, f32[48,24,384]{2,1,0:T(8,128)}, u32[]{:S(2)}) copy-start(f32[48,24,384]{2,1,0:T(8,128)} %param.16) | copy-start | bytes 5308420
  147.8 31.1 %copy-start.2 = (f32[384,1152]{1,0:T(8,128)S(1)}, f32[384,1152]{1,0:T(8,128)}, u32[]{:S(2)}) copy-start(f32[384,1152]{1,0:T(8,128)} %get-tuple-element.14.evolved_ref) | copy-start | bytes 5308420
